TPU v7x, 256 devices: a whole 4x4x8 slice. The times are simulated.
256 devices in a mesh: dp: 8 (over x, core), cut: 32 (over y, z).
Axes of the slice: x: 4, y: 4, z: 8, core: 2. Of those that a mesh axis runs over, the one named last changes fastest.
Arguments:
- node_feat: bfloat16 [128, 262144], P(None, ('dp', 'cut')), parts along dimension 1, may hold values from -6 to 6
- edge_feat: bfloat16 [128, 1048576], P(None, ('dp', 'cut')), parts along dimension 1, may hold values from -6 to 6
- route: int32 [256, 32, 128], P(('dp', 'cut')), parts along dimension 0, may hold values from 0 to 1023, as said below
- block_tile: int32 [8192, 2], P(('dp', 'cut')), parts along dimension 0, may hold values from 0 to 39
- block_offset: int32 [8192, 2, 128], P(('dp', 'cut')), parts along dimension 0, may hold values from 0 to 127
- block_count: int32 [8192], P(('dp', 'cut')), parts along dimension 0, may hold values from 1 to 128, as said below
- w_edge1: bfloat16 [128, 384], replicated, may hold values from -0.3125 to 0.3125
- bias_edge1: float32 [128], replicated, may hold values from -3 to 3
- w_edge2: bfloat16 [128, 128], replicated, may hold values from -0.5 to 0.5
- gain_edge: float32 [128], replicated, may hold values from 0.1 to 1.9
- shift_edge: float32 [128], replicated, may hold values from -3 to 3
- w_node1: bfloat16 [128, 256], replicated, may hold values from -0.375 to 0.375
- bias_node1: float32 [128], replicated, may hold values from -3 to 3
- w_node2: bfloat16 [128, 128], replicated, may hold values from -0.5 to 0.5
- gain_node: float32 [128], replicated, may hold values from 0.1 to 1.9
- shift_node: float32 [128], replicated, may hold values from -3 to 3
- node_cot: bfloat16 [128, 262144], P(None, ('dp', 'cut')), parts along dimension 1, may hold values from -6 to 6
Outputs:
- node_out: bfloat16 [128, 262144], P(None, ('dp', 'cut')), parts along dimension 1
- node_grad: float32 [128, 262144], P(None, ('dp', 'cut')), parts along dimension 1
- edge_grad: bfloat16 [128, 1048576], P(None, ('dp', 'cut')), parts along dimension 1
- param_grad: float32 [923648], P('dp'), parts along dimension 0
There are 8 independent parts, one for each index of `dp`. A program takes and returns all parts, laid end to end along the dimension named above; an argument that names none is the same for every part. Nothing has to cross between parts.
Inputs may be any that keep to these rules, and one draw needn't show every extreme that they name: route[c, p, :] holds 128 distinct master rows of partition p. `block_count`: the first block of each partition is full.
All inputs are finite; a program needn't handle non-finite values.
Results may differ from a plain program's by a relative error of at most 0.024.
Values may be sent and summed in bfloat16 or wider, within the bound.
No kernel may reach another device: no remote copies, remote signals or barrier semaphores. Data moves between devices by JAX's collectives and lax.ppermute only.
A program may use at most 128 MiB of HBM per device.

v0:
```python
import math

import jax
import jax.numpy as jnp
from jax import lax
from jax.sharding import PartitionSpec as P


def silu_slope(values):
    sigmoid_val = jax.nn.sigmoid(values)
    return sigmoid_val * (1.0 + values * (1.0 - sigmoid_val))


def layer_norm(values):
    centred = values - jnp.mean(values, axis=0, keepdims=True)
    inverse = lax.rsqrt(jnp.mean(centred * centred, axis=0, keepdims=True) + 1e-05)
    return (centred * inverse, inverse)


def norm_back(upstream, normed, inverse, gain_vec):
    scaled = upstream * gain_vec[:, None]
    return inverse * (
        scaled
        - jnp.mean(scaled, axis=0, keepdims=True)
        - normed * jnp.mean(scaled * normed, axis=0, keepdims=True)
    )


def row_contract(left, right):
    return lax.dot_general(
        left, right, (((1,), (1,)), ((), ())), preferred_element_type=jnp.float32
    )


def lead_contract(weight, values):
    return lax.dot_general(
        weight, values, (((0,), (0,)), ((), ())), preferred_element_type=jnp.float32
    )


def per_device(
    node_feat,
    edge_feat,
    route,
    block_tile,
    block_offset,
    block_count,
    w_edge1,
    bias_edge1,
    w_edge2,
    gain_edge,
    shift_edge,
    w_node1,
    bias_node1,
    w_node2,
    gain_node,
    shift_node,
    node_cot,
):
    latent = node_feat.shape[0]
    masters = node_feat.shape[1]
    peer_count = lax.axis_size("cut")
    total_nodes = masters * peer_count
    total_edges = edge_feat.shape[1] * peer_count
    mirror_index = lax.all_to_all(route[0], "cut", split_axis=0, concat_axis=0, tiled=True).reshape(
        -1
    )

    def fetch_mirrors(master_part):
        outgoing = jnp.take(master_part, mirror_index, axis=1)
        result = lax.all_to_all(outgoing, "cut", split_axis=1, concat_axis=1, tiled=True)
        return result

    def reduce_mirrors(master_part, mirror_part):
        returned = lax.all_to_all(
            mirror_part.astype(jnp.bfloat16), "cut", split_axis=1, concat_axis=1, tiled=True
        ).astype(mirror_part.dtype)
        result = master_part.at[:, mirror_index].add(returned)
        return result

    columns = 128 * block_tile[:, :, None] + block_offset
    send_cols = columns[:, 0, :].reshape(-1)
    recv_cols = columns[:, 1, :].reshape(-1)
    live_mask = (
        (jnp.arange(block_offset.shape[2], dtype=jnp.int32)[None, :] < block_count[:, None])
        .reshape(-1)
        .astype(jnp.float32)
    )
    node_table = jnp.concatenate([node_feat, fetch_mirrors(node_feat)], axis=1)
    local_width = node_table.shape[1]
    stacked = jnp.concatenate(
        [
            edge_feat,
            jnp.take(node_table, send_cols, axis=1),
            jnp.take(node_table, recv_cols, axis=1),
        ],
        axis=0,
    )
    edge_pre = jnp.dot(w_edge1, stacked, preferred_element_type=jnp.float32) + bias_edge1[:, None]
    edge_hidden = jax.nn.silu(edge_pre).astype(jnp.bfloat16)
    edge_post = jnp.dot(w_edge2, edge_hidden, preferred_element_type=jnp.float32)
    edge_normed, edge_inv = layer_norm(edge_post)
    message = (gain_edge[:, None] * edge_normed + shift_edge[:, None]) * live_mask[None, :]
    local_sums = jnp.zeros((latent, local_width), jnp.float32).at[:, recv_cols].add(message)
    aggregate = reduce_mirrors(local_sums[:, :masters], local_sums[:, masters:])
    agg_low = aggregate.astype(jnp.bfloat16)
    node_input = jnp.concatenate([node_feat, agg_low], axis=0)
    node_pre = (
        jnp.dot(w_node1, node_input, preferred_element_type=jnp.float32) + bias_node1[:, None]
    )
    node_hidden = jax.nn.silu(node_pre).astype(jnp.bfloat16)
    node_post = jnp.dot(w_node2, node_hidden, preferred_element_type=jnp.float32)
    node_normed, node_inv = layer_norm(node_post)
    node_out = (
        node_feat.astype(jnp.float32) + gain_node[:, None] * node_normed + shift_node[:, None]
    ).astype(jnp.bfloat16)
    upstream = node_cot.astype(jnp.float32)
    grad_gain_node = jnp.sum(upstream * node_normed, axis=1)
    grad_shift_node = jnp.sum(upstream, axis=1)
    grad_node_post = norm_back(upstream, node_normed, node_inv, gain_node).astype(jnp.bfloat16)
    grad_w_node2 = row_contract(grad_node_post, node_hidden)
    grad_node_full = lead_contract(w_node2, grad_node_post) * silu_slope(node_pre)
    grad_node_pre = grad_node_full.astype(jnp.bfloat16)
    grad_w_node1 = row_contract(grad_node_pre, node_input)
    grad_bias_node1 = jnp.sum(grad_node_full, axis=1)
    node_direct = lead_contract(w_node1[:, :latent], grad_node_pre)
    grad_agg = lead_contract(w_node1[:, latent:], grad_node_pre).astype(jnp.bfloat16)
    node_vec = jnp.concatenate(
        [
            grad_w_node1.reshape(-1),
            grad_bias_node1,
            grad_w_node2.reshape(-1),
            grad_gain_node,
            grad_shift_node,
        ]
    )
    agg_table = jnp.concatenate([grad_agg, fetch_mirrors(grad_agg)], axis=1)
    grad_message = jnp.take(agg_table, recv_cols, axis=1).astype(jnp.float32) * live_mask[None, :]
    grad_gain_edge = jnp.sum(grad_message * edge_normed, axis=1)
    grad_shift_edge = jnp.sum(grad_message, axis=1)
    grad_edge_post = norm_back(grad_message, edge_normed, edge_inv, gain_edge).astype(jnp.bfloat16)
    grad_w_edge2 = row_contract(grad_edge_post, edge_hidden)
    grad_edge_full = lead_contract(w_edge2, grad_edge_post) * silu_slope(edge_pre)
    grad_edge_pre = grad_edge_full.astype(jnp.bfloat16)
    grad_w_edge1 = row_contract(grad_edge_pre, stacked)
    grad_bias_edge1 = jnp.sum(grad_edge_full, axis=1)
    edge_grad = lead_contract(w_edge1[:, :latent], grad_edge_pre).astype(jnp.bfloat16)
    grad_send = lead_contract(w_edge1[:, latent : 2 * latent], grad_edge_pre)
    grad_recv = lead_contract(w_edge1[:, 2 * latent :], grad_edge_pre)
    grad_table = (
        jnp.zeros((latent, local_width), jnp.float32)
        .at[:, send_cols]
        .add(grad_send)
        .at[:, recv_cols]
        .add(grad_recv)
    )
    node_grad = (
        upstream + node_direct + reduce_mirrors(grad_table[:, :masters], grad_table[:, masters:])
    )
    edge_vec = jnp.concatenate(
        [
            grad_w_edge1.reshape(-1),
            grad_bias_edge1,
            grad_w_edge2.reshape(-1),
            grad_gain_edge,
            grad_shift_edge,
        ]
    )
    summed = lax.psum(jnp.concatenate([edge_vec, node_vec]).astype(jnp.bfloat16), "cut").astype(
        jnp.float32
    )
    edge_summed = summed[: edge_vec.shape[0]]
    node_summed = summed[edge_vec.shape[0] :]
    param_grad = jnp.concatenate(
        [edge_summed / math.sqrt(total_edges), node_summed / math.sqrt(total_nodes)]
    )
    return (node_out, node_grad, edge_grad, param_grad)


def solution(mesh):
    in_specs = (
        P(None, ("dp", "cut")),
        P(None, ("dp", "cut")),
        P(("dp", "cut"), None, None),
        P(("dp", "cut"), None),
        P(("dp", "cut"), None, None),
        P(("dp", "cut")),
        P(),
        P(),
        P(),
        P(),
        P(),
        P(),
        P(),
        P(),
        P(),
        P(),
        P(None, ("dp", "cut")),
    )
    out_specs = (P(None, ("dp", "cut")), P(None, ("dp", "cut")), P(None, ("dp", "cut")), P("dp"))
    return jax.shard_map(
        per_device, mesh=mesh, in_specs=in_specs, out_specs=out_specs, check_vma=False
    )
```

profile of v0, /device:TPU:6, one launch (start us, length us, event | category | flops | bytes accessed | tf_op | source)
XLA Modules:
  0.0 507.0 jit_solution(10482661762203878273)
XLA Ops:
  7.2 11.5 %all-to-all-start = ((s32[32,1,128]{2,1,0:T(1,128)}), s32[32,1,128]{2,1,0:T(1,128)S(1)}, u32[]{:S(2)}, u32[]{:S(2)}) async-start(s32[32,1,128]{2,1,0:T(1,128)} %bitcast.144), calls=%async_computation | async-start | bytes 32768 | tf_op jit(solution)/shard_map/all_to_all | solution.py:65
  18.7 0.7 broadcast_multiply_fusion.6
  19.5 0.9 broadcast_add_fusion
  20.3 1.1 copy.38
  21.4 7.0 %all-to-all-done = s32[32,1,128]{2,1,0:T(1,128)S(1)} async-done(((s32[32,1,128]{2,1,0:T(1,128)}), s32[32,1,128]{2,1,0:T(1,128)S(1)}, u32[]{:S(2)}, u32[]{:S(2)}) %all-to-all-start) | async-done | bytes 16416 | tf_op jit(solution)/shard_map/all_to_all | solution.py:65
  28.4 12.1 %gather_fusion = bf16[4096,128]{1,0:T(8,128)(2,1)S(1)} fusion(bf16[128,1024]{0,1:T(8,128)(2,1)S(1)} %copy.38, s32[4096]{0:T(1024)S(1)} %fusion.48), kind=kCustom, calls=%fused_computation.clone | custom fusion | bytes 2113536 | tf_op jit(solution)/shard_map/jit(_take)/gather | solution.py:70
  40.6 2.9 broadcast_select_fusion.1
  43.5 3.9 all-to-all-start.1
  47.5 1.3 copy.36
  48.9 0.6 compare_select_fusion
  49.6 25.4 %all-to-all-done.1 = bf16[128,32,128]{0,2,1:T(8,128)(2,1)S(1)} async-done(((bf16[128,32,128]{0,2,1:T(8,128)(2,1)}), bf16[128,32,128]{0,2,1:T(8,128)(2,1)S(1)}, u32[]{:S(2)}, u32[]{:S(2)}) %all-to-all-start.1) | async-done | bytes 1048608 | tf_op jit(solution)/shard_map/all_to_all | solution.py:71
  75.1 12.1 %gather_fusion.1 = bf16[4096,128]{1,0:T(8,128)(2,1)S(1)} fusion(bf16[128,5120]{0,1:T(8,128)(2,1)S(1)} %pad_maximum_fusion.1, s32[4096]{0:T(1024)S(1)} %fusion.49), kind=kCustom, calls=%fused_computation.1.clone | custom fusion | bytes 2113536 | tf_op jit(solution)/shard_map/jit(_take)/gather | solution.py:94
  87.2 15.0 %gather_fusion.2 = bf16[4096,128]{1,0:T(8,128)(2,1)} fusion(bf16[128,5120]{0,1:T(8,128)(2,1)S(1)} %pad_maximum_fusion.1, s32[4096]{0:T(1024)S(1)} %fusion.50), kind=kCustom, calls=%fused_computation.3.clone | custom fusion | bytes 2113536 | tf_op jit(solution)/shard_map/jit(_take)/gather | solution.py:95
  102.3 3.1 select_bitcast_fusion
  105.4 2.3 multiply_convert_fusion
  107.7 0.4 fusion.60
  108.7 0.8 copy-done.1
  109.5 0.4 fusion.7
  110.0 1.8 copy.37
  111.8 23.3 %scatter_custom_fusion = f32[128,5120]{0,1:T(8,128)S(1)} fusion(s32[4096]{0:T(1024)S(1)} %bitcast.142, f32[4096,128]{1,0:T(8,128)} %copy.37, f32[]{:T(128)} %constant.26.clone.1), kind=kCustom, calls=%fused_computation.47 | custom fusion | flops 524288 | bytes 2621952 | tf_op jit(solution)/shard_map/scatter-add | solution.py:104
  135.1 1.1 slice.89
  136.2 5.1 %all-to-all-start.2 = ((bf16[128,32,128]{0,2,1:T(8,128)(2,1)}), bf16[128,32,128]{0,2,1:T(8,128)(2,1)}, u32[]{:S(2)}, u32[]{:S(2)}) async-start(bf16[128,32,128]{0,2,1:T(8,128)(2,1)} %bitcast.134), calls=%async_computation.2 | async-start | bytes 2097152 | tf_op jit(solution)/shard_map/all_to_all | solution.py:75
  141.4 27.5 %all-to-all-done.2 = bf16[128,32,128]{0,2,1:T(8,128)(2,1)} async-done(((bf16[128,32,128]{0,2,1:T(8,128)(2,1)}), bf16[128,32,128]{0,2,1:T(8,128)(2,1)}, u32[]{:S(2)}, u32[]{:S(2)}) %all-to-all-start.2) | async-done | bytes 1048608 | tf_op jit(solution)/shard_map/all_to_all | solution.py:75
  168.9 23.1 %scatter_custom_fusion.1 = f32[128,1024]{0,1:T(8,128)S(1)} fusion(f32[128,1024]{0,1:T(8,128)S(1)} %slice.66, s32[4096]{0:T(1024)S(1)} %bitcast.145, bf16[128,4096]{0,1:T(8,128)(2,1)} %bitcast.39), kind=kCustom, calls=%fused_computation.22 | custom fusion | flops 1048576 | bytes 1572864 | tf_op jit(solution)/shard_map/scatter-add | solution.py:78
  192.2 1.2 multiply_convert_fusion.1
  193.8 0.8 fusion.37
  194.6 1.0 fusion.35
  195.6 0.9 fusion.62
  196.7 12.1 %gather_fusion.3 = bf16[4096,128]{1,0:T(8,128)(2,1)S(1)} fusion(bf16[128,1024]{0,1:T(8,128)(2,1)S(1)} %fusion.25, s32[4096]{0:T(1024)S(1)} %fusion.48), kind=kCustom, calls=%fused_computation.2.clone | custom fusion | bytes 2113536 | tf_op jit(solution)/shard_map/jit(_take)/gather | solution.py:70
  208.8 2.9 broadcast_select_fusion
  211.7 5.0 all-to-all-start.3
  216.7 0.7 reduce.4
  217.8 0.8 fusion.29
  218.6 25.7 %all-to-all-done.3 = bf16[128,32,128]{0,2,1:T(8,128)(2,1)S(1)} async-done(((bf16[128,32,128]{0,2,1:T(8,128)(2,1)}), bf16[128,32,128]{0,2,1:T(8,128)(2,1)S(1)}, u32[]{:S(2)}, u32[]{:S(2)}) %all-to-all-start.3) | async-done | bytes 1048608 | tf_op jit(solution)/shard_map/all_to_all | solution.py:71
  244.4 15.0 %gather_fusion.4 = bf16[4096,128]{1,0:T(8,128)(2,1)} fusion(bf16[128,5120]{0,1:T(8,128)(2,1)S(1)} %pad_maximum_fusion.2, s32[4096]{0:T(1024)S(1)} %copy-done.18), kind=kCustom, calls=%fused_computation.4.clone | custom fusion | bytes 2113536 | tf_op jit(solution)/shard_map/jit(_take)/gather | solution.py:138
  259.4 1.6 copy.40
  261.3 2.5 fusion.12
  263.8 0.7 fusion.11
  264.6 0.5 copy-done.4
  265.0 0.4 fusion.28
  265.5 1.2 copy-done.41
  266.6 1.5 fusion.58
  268.2 0.3 copy-done.15
  268.5 1.4 fusion.26
  269.9 1.4 fusion.2
  271.3 1.8 fusion.42
  273.0 1.7 fusion.44
  274.8 23.3 %scatter_custom_fusion.2 = f32[128,5120]{0,1:T(8,128)S(1)} fusion(s32[4096]{0:T(1024)} %bitcast.147, f32[4096,128]{1,0:T(8,128)} %fusion.44, f32[]{:T(128)} %constant.26.clone.1), kind=kCustom, calls=%fused_computation.45 | custom fusion | flops 524288 | bytes 2621952 | tf_op jit(solution)/shard_map/scatter-add | solution.py:153
  298.1 23.8 %scatter_fusion = f32[128,5120]{0,1:T(8,128)S(1)} fusion(f32[128,5120]{0,1:T(8,128)S(1)} %scatter_custom_fusion.2, s32[4096]{0:T(1024)S(1)} %bitcast.143, f32[4096,128]{1,0:T(8,128)} %fusion.42), kind=kCustom, calls=%fused_computation.8 | custom fusion | flops 524288 | bytes 6307840 | tf_op jit(solution)/shard_map/scatter-add | solution.py:155
  322.0 1.1 slice.88
  323.1 1.0 reshape.207
  324.1 0.8 dynamic-update-slice.1
  324.9 0.5 dynamic-update-slice.2
  325.9 0.8 dynamic-update-slice.5
  326.7 0.8 dynamic-update-slice.6
  327.6 1.1 dynamic-update-slice.7
  329.1 0.7 copy-done.16
  329.8 2.3 copy.44
  332.8 5.0 all-to-all-start.4
  337.8 136.8 %all-reduce.2.cloned.1.call-done = bf16[115456]{0:T(1024)(128)(2,1)} async-done(((bf16[115456]{0:T(1024)(128)(2,1)}), bf16[115456]{0:T(1024)(128)(2,1)}) %all-reduce.2.cloned.1.call-update) | async-done | bytes 230928 | tf_op jit(solution)/shard_map/psum | solution.py:169
  474.6 1.0 convert_element_type.94
  475.7 0.8 pad_maximum_fusion.8
  476.5 22.7 %scatter_custom_fusion.4 = f32[128,1024]{0,1:T(8,128)S(1)} fusion(f32[128,1024]{0,1:T(8,128)S(1)} %copy.42, s32[4096]{0:T(1024)} %bitcast.146, bf16[128,4096]{0,1:T(8,128)(2,1)S(1)} %bitcast.132), kind=kCustom, calls=%fused_computation.20 | custom fusion | flops 1048576 | bytes 1572864 | tf_op jit(solution)/shard_map/scatter-add | solution.py:78
  499.2 1.0 copy.43
  (121 shorter events, 4.0 us)
Async XLA Ops:
  7.2 100.6 %copy-start = (bf16[128,128]{1,0:T(8,128)(2,1)S(1)}, bf16[128,128]{1,0:T(8,128)(2,1)}, u32[]{:S(2)}) copy-start(bf16[128,128]{1,0:T(8,128)(2,1)} %param.29) | copy-start | bytes 98308
  7.2 21.2 %all-to-all-start = ((s32[32,1,128]{2,1,0:T(1,128)}), s32[32,1,128]{2,1,0:T(1,128)S(1)}, u32[]{:S(2)}, u32[]{:S(2)}) async-start(s32[32,1,128]{2,1,0:T(1,128)} %bitcast.144), calls=%async_computation | async-start | bytes 32768 | tf_op jit(solution)/shard_map/all_to_all | solution.py:65
  40.6 6.8 %copy-start.38 = (s32[32]{0:T(128)S(1)}, s32[32]{0:T(128)}, u32[]{:S(2)}) copy-start(s32[32]{0:T(128)} %param.26) | copy-start | bytes 388
  40.6 6.9 %copy-start.8 = (bf16[128,4096]{1,0:T(8,128)(2,1)S(1)}, bf16[128,4096]{1,0:T(8,128)(2,1)}, u32[]{:S(2)}) copy-start(bf16[128,4096]{1,0:T(8,128)(2,1)} %param.22) | copy-start | bytes 3145732
  43.5 31.5 %all-to-all-start.1 = ((bf16[128,32,128]{0,2,1:T(8,128)(2,1)}), bf16[128,32,128]{0,2,1:T(8,128)(2,1)S(1)}, u32[]{:S(2)}, u32[]{:S(2)}) async-start(bf16[128,32,128]{0,2,1:T(8,128)(2,1)} %bitcast.6), calls=%async_computation.1 | async-start | bytes 2097152 | tf_op jit(solution)/shard_map/all_to_all | solution.py:71
  48.8 53.4 %copy-start.25 = (pred[4096]{0:T(1024)(128)(4,1)}, pred[4096]{0:T(1024)(128)(4,1)S(1)}, u32[]{:S(2)}) copy-start(pred[4096]{0:T(1024)(128)(4,1)S(1)} %compare_and_fusion) | copy-start | bytes 12292
  48.9 38.3 %copy-start.17 = (s32[4096]{0:T(1024)}, s32[4096]{0:T(1024)S(1)}, u32[]{:S(2)}) copy-start(s32[4096]{0:T(1024)S(1)} %fusion.50) | copy-start | bytes 49156
  49.6 62.2 %copy-start.21 = (s32[4096,1]{0,1:T(1,128)}, s32[4096,1]{0,1:T(1,128)S(1)}, u32[]{:S(2)}) copy-start(s32[4096,1]{0,1:T(1,128)S(1)} %get-tuple-element.26) | copy-start | bytes 49156
  102.3 3.1 copy-start.9
  102.3 3.1 copy-start.19
  102.3 3.1 copy-start.39
  105.3 2.4 copy-start.12
  105.4 2.4 copy-start.14
  107.7 1.0 copy-start.3
  107.7 1.8 copy-start.29
  107.7 1.8 copy-start.36
  108.2 1.3 copy-start.1
  136.2 32.7 %all-to-all-start.2 = ((bf16[128,32,128]{0,2,1:T(8,128)(2,1)}), bf16[128,32,128]{0,2,1:T(8,128)(2,1)}, u32[]{:S(2)}, u32[]{:S(2)}) async-start(bf16[128,32,128]{0,2,1:T(8,128)(2,1)} %bitcast.134), calls=%async_computation.2 | async-start | bytes 2097152 | tf_op jit(solution)/shard_map/all_to_all | solution.py:75
  141.3 50.8 %copy-start.40 = (f32[128]{0:T(128)S(1)}, f32[128]{0:T(128)}, u32[]{:S(2)}) copy-start(f32[128]{0:T(128)} %param.33) | copy-start | bytes 1540
  141.4 52.0 %copy-start.28 = (s32[4096,1]{0,1:T(1,128)}, s32[4096,1]{0,1:T(1,128)S(1)}, u32[]{:S(2)}) copy-start(s32[4096,1]{0,1:T(1,128)S(1)} %compare_select_fusion.1) | copy-start | bytes 49156
  192.1 1.3 copy-start.27
  192.1 1.6 copy-start.5
  192.1 1.6 copy-start.31
  192.2 2.4 copy-start.11
  192.2 2.4 copy-start.37
  194.6 1.9 copy-start.23
  196.4 21.0 %copy-start.6 = (bf16[128,1024]{0,1:T(8,128)(2,1)}, bf16[128,1024]{0,1:T(8,128)(2,1)S(1)}, u32[]{:S(2)}) copy-start(bf16[128,1024]{0,1:T(8,128)(2,1)S(1)} %get-tuple-element.39) | copy-start | bytes 786436
  211.7 32.6 %all-to-all-start.3 = ((bf16[128,32,128]{0,2,1:T(8,128)(2,1)}), bf16[128,32,128]{0,2,1:T(8,128)(2,1)S(1)}, u32[]{:S(2)}, u32[]{:S(2)}) async-start(bf16[128,32,128]{0,2,1:T(8,128)(2,1)} %bitcast.28), calls=%async_computation.3 | async-start | bytes 2097152 | tf_op jit(solution)/shard_map/all_to_all | solution.py:71
  216.7 257.9 %all-reduce.2.cloned.1.call-start = ((), (), s32[]{:S(2)}) async-start(), calls=%async_computation.5 | async-start | bytes 462848 | tf_op jit(solution)/shard_map/psum | solution.py:169
  217.4 27.0 %copy-start.18 = (s32[4096]{0:T(1024)S(1)}, s32[4096]{0:T(1024)}, u32[]{:S(2)}) copy-start(s32[4096]{0:T(1024)} %copy-done.17) | copy-start | bytes 49156
  259.4 1.9 copy-start.2
  261.3 2.5 copy-start.26
  261.3 2.5 copy-start.30
  263.8 1.2 copy-start.4
  265.0 1.6 copy-start.41
  266.6 1.5 copy-start.10
  266.6 1.5 copy-start.13
  266.6 1.9 copy-start.15
  268.5 1.4 copy-start.20
  274.8 23.3 %copy-start.22 = (s32[4096,1]{0,1:T(1,128)S(1)}, s32[4096,1]{0,1:T(1,128)}, u32[]{:S(2)}) copy-start(s32[4096,1]{0,1:T(1,128)} %copy-done.21) | copy-start | bytes 49156
  321.9 3.5 copy-start.35
  321.9 3.8 copy-start.34
  321.9 6.7 %copy-start.32 = (bf16[128]{0:T(256)(128)(2,1)S(1)}, bf16[128]{0:T(256)(128)(2,1)}, u32[]{:S(2)}) copy-start(bf16[128]{0:T(256)(128)(2,1)} %get-tuple-element.18) | copy-start | bytes 772
  321.9 7.0 %copy-start.33 = (bf16[128]{0:T(256)(128)(2,1)S(1)}, bf16[128]{0:T(256)(128)(2,1)}, u32[]{:S(2)}) copy-start(bf16[128]{0:T(256)(128)(2,1)} %reduce.4) | copy-start | bytes 772
  323.1 9.2 %copy-start.7 = (bf16[128,1024]{0,1:T(8,128)(2,1)S(1)}, bf16[128,1024]{0,1:T(8,128)(2,1)}, u32[]{:S(2)}) copy-start(bf16[128,1024]{0,1:T(8,128)(2,1)} %copy-done.6) | copy-start | bytes 786436
  323.1 9.2 %copy-start.24 = (bf16[128,256]{1,0:T(8,128)(2,1)S(1)}, bf16[128,256]{1,0:T(8,128)(2,1)}, u32[]{:S(2)}) copy-start(bf16[128,256]{1,0:T(8,128)(2,1)} %param.32) | copy-start | bytes 196612
  329.1 0.7 copy-start.16
  332.8 143.7 %all-to-all-start.4 = ((bf16[128,32,128]{0,2,1:T(8,128)(2,1)}), bf16[128,32,128]{0,2,1:T(8,128)(2,1)S(1)}, u32[]{:S(2)}, u32[]{:S(2)}) async-start(bf16[128,32,128]{0,2,1:T(8,128)(2,1)} %bitcast.32), calls=%async_computation.4 | async-start | bytes 2097152 | tf_op jit(solution)/shard_map/all_to_all | solution.py:75
Sparse Core Ops, SparseCore 0:
  329.9 144.6 all-reduce.1
where the time goes:
time: 508 us; the launch traced here: 507 us
  waiting for transfers between devices  222 us (44%)
  other arithmetic  136 us (27%)
  local copies, waits for them, and re-layouts  88.5 us (17%)
  starting transfers between devices  30.6 us (6%)
  matrix products  14.8 us (3%)
  between operations  14.8 us (3%)
    psum x1, waiting for transfers between devices, per_device(): lax.psum(jnp.concatenate([edge_vec, node_vec]).astype(jnp.bfloat16), 'cut')  137 us
    all_to_all x2, waiting for transfers between devices, fetch_mirrors(): lax.all_to_all(outgoing, 'cut', split_axis=1, concat_axis=1, tiled=True)  51.1 us
    scatter-add x2, other arithmetic, per_device(): grad_table = jnp.zeros((latent, local_width), jnp.float32).at[:, send_col...  47.1 us
    scatter-add x2, other arithmetic, reduce_mirrors(): result = master_part.at[:, mirror_index].add(returned)  45.9 us
    all_to_all x2, waiting for transfers between devices, reduce_mirrors(): lax.all_to_all(mirror_part.astype(jnp.bfloat16), 'cut', split_axis=1, con...  27.5 us
    gather x2, local copies, waits for them, and re-layouts, fetch_mirrors(): outgoing = jnp.take(master_part, mirror_index, axis=1)  24.3 us
    scatter-add x1, other arithmetic, per_device(): jnp.zeros((latent, local_width), jnp.float32).at[:, recv_cols].add(message)  23.3 us
    gather x2, local copies, waits for them, and re-layouts, per_device(): jnp.take(agg_table, recv_cols, axis=1).astype(jnp.float32)  16.7 us
  transfers between devices with their start and end apart: 6, of which 5 were waited for; matrix products, arithmetic and copies ran while one was open for 2% of the time, Pallas kernels for 0%

commit v1 on v0

v1 whole, which is shorter than its diff:
```python
import functools
import math

import jax
import jax.numpy as jnp
from jax import lax
from jax.experimental import pallas as pl
from jax.experimental.pallas import tpu as pltpu
from jax.sharding import PartitionSpec as P

F32 = jnp.float32
BF16 = jnp.bfloat16
TILE = 128
GROUP = 8
NODE_ROWS = 16
EDGE_ROWS = 24
INTERPRET = False


def dot_nn(left, right):
    return lax.dot_general(left, right, (((1,), (0,)), ((), ())), preferred_element_type=F32)


def dot_nt(left, right):
    return lax.dot_general(left, right, (((1,), (1,)), ((), ())), preferred_element_type=F32)


def dot_tn(left, right):
    return lax.dot_general(left, right, (((0,), (0,)), ((), ())), preferred_element_type=F32)


def one_hot(index_row, depth):
    rows = lax.broadcasted_iota(jnp.int32, (depth, index_row.shape[1]), 0)
    return jnp.where(rows == index_row, 1.0, 0.0).astype(BF16)


def sigmoid(values):
    return 1.0 / (1.0 + jnp.exp(-values))


def layer_norm(values):
    centred = values - jnp.mean(values, axis=0, keepdims=True)
    inverse = lax.rsqrt(jnp.mean(centred * centred, axis=0, keepdims=True) + 1e-05)
    return centred * inverse, inverse


def norm_back(upstream, normed, inverse, gain):
    scaled = upstream * gain
    return inverse * (
        scaled
        - jnp.mean(scaled, axis=0, keepdims=True)
        - normed * jnp.mean(scaled * normed, axis=0, keepdims=True)
    )


def gather_kernel(idx_ref, table_ref, out_ref):
    peers = out_ref.shape[0]
    depth = table_ref.shape[1]

    def body(q, carry):
        hot0 = one_hot(idx_ref[2 * q], depth)
        hot1 = one_hot(idx_ref[2 * q + 1], depth)
        picked = dot_nn(table_ref[...], jnp.concatenate([hot0, hot1], axis=1)).astype(BF16)
        out_ref[2 * q] = picked[:, :TILE]
        out_ref[2 * q + 1] = picked[:, TILE:]
        return carry

    lax.fori_loop(0, peers // 2, body, 0)


def fill_table(table, local_ref, mirror_ref):
    local_tiles = local_ref.shape[1] // TILE
    for t in range(local_tiles):
        table[t] = local_ref[:, t * TILE : (t + 1) * TILE]

    def body(p, carry):
        table[local_tiles + p] = mirror_ref[p, :TILE, :]
        return carry

    lax.fori_loop(0, mirror_ref.shape[0], body, 0)


def edge_fwd_kernel(
    tile_ref,
    count_ref,
    offset_ref,
    edge_ref,
    node_ref,
    mirror_ref,
    w1_ref,
    b1_ref,
    w2_ref,
    gain_ref,
    shift_ref,
    pair_ref,
    hidden_ref,
    slope_ref,
    normed_ref,
    inv_ref,
    local_ref,
    out_ref,
    table,
    total,
):
    step = pl.program_id(0)
    latent = edge_ref.shape[0]
    local_tiles = node_ref.shape[1] // TILE

    @pl.when(step == 0)
    def _():
        fill_table(table, node_ref, mirror_ref)
        total[...] = jnp.zeros_like(total)

    receiver_hot = []
    for j in range(GROUP):
        b = step * GROUP + j
        cols = slice(j * TILE, (j + 1) * TILE)
        hot_s = one_hot(offset_ref[j, 0:1, :], TILE)
        hot_r = one_hot(offset_ref[j, 1:2, :], TILE)
        receiver_hot.append(hot_r)
        pair_ref[:latent, cols] = dot_nn(table[tile_ref[b, 0]], hot_s).astype(BF16)
        pair_ref[latent:, cols] = dot_nn(table[tile_ref[b, 1]], hot_r).astype(BF16)
    pre = (
        dot_nn(w1_ref[:, :latent], edge_ref[...])
        + dot_nn(w1_ref[:, latent:], pair_ref[...])
        + b1_ref[...]
    )
    gate = sigmoid(pre)
    hidden = (pre * gate).astype(BF16)
    hidden_ref[...] = hidden
    slope_ref[...] = gate * (1.0 + pre * (1.0 - gate))
    normed, inverse = layer_norm(dot_nn(w2_ref[...], hidden))
    normed_ref[...] = normed
    inv_ref[...] = inverse
    message = gain_ref[...] * normed + shift_ref[...]
    lane = lax.broadcasted_iota(jnp.int32, (latent, TILE), 1)
    for j in range(GROUP):
        b = step * GROUP + j
        cols = slice(j * TILE, (j + 1) * TILE)
        kept = jnp.where(lane < count_ref[b], message[:, cols], 0.0).astype(BF16)
        tile = tile_ref[b, 1]
        total[tile] += dot_nt(kept, receiver_hot[j])

    @pl.when(step == pl.num_programs(0) - 1)
    def _():
        for t in range(local_tiles):
            local_ref[:, t * TILE : (t + 1) * TILE] = total[t]

        def body(p, carry):
            out_ref[p] = total[local_tiles + p].astype(BF16)
            return carry

        lax.fori_loop(0, out_ref.shape[0], body, 0)


def scatter_mirrors(total_ref, idx_ref, mirror_ref):
    depth = total_ref.shape[1]

    def body(q, carry):
        hot = jnp.concatenate(
            [one_hot(idx_ref[2 * q], depth), one_hot(idx_ref[2 * q + 1], depth)], axis=1
        )
        values = jnp.concatenate(
            [mirror_ref[2 * q, :TILE, :], mirror_ref[2 * q + 1, :TILE, :]], axis=1
        )
        total_ref[...] += dot_nt(values, hot)
        return carry

    lax.fori_loop(0, mirror_ref.shape[0] // 2, body, 0)


def row_sum(values):
    folded = values[:, :TILE]
    for start in range(TILE, values.shape[1], TILE):
        folded = folded + values[:, start : start + TILE]
    return jnp.sum(folded.T, axis=0, keepdims=True)


def node_kernel(
    idx_ref,
    local_ref,
    mirror_ref,
    node_ref,
    cot_ref,
    w1_ref,
    b1_ref,
    w2_ref,
    gain_ref,
    shift_ref,
    node_out_ref,
    base_ref,
    grad_agg_ref,
    out_ref,
    total,
    rows,
):
    latent = node_ref.shape[0]
    peers = out_ref.shape[0]
    depth = node_ref.shape[1]
    total[...] = local_ref[...]
    scatter_mirrors(total, idx_ref, mirror_ref)
    agg_low = total[...].astype(BF16)
    node_low = node_ref[...]
    pre = dot_nn(w1_ref[:, :latent], node_low) + dot_nn(w1_ref[:, latent:], agg_low) + b1_ref[...]
    gate = sigmoid(pre)
    hidden = (pre * gate).astype(BF16)
    normed, inverse = layer_norm(dot_nn(w2_ref[...], hidden))
    gain = gain_ref[...]
    node_out_ref[...] = (node_low.astype(F32) + gain * normed + shift_ref[...]).astype(BF16)
    upstream = cot_ref[...].astype(F32)
    grad_post = norm_back(upstream, normed, inverse, gain).astype(BF16)
    grad_full = dot_tn(w2_ref[...], grad_post) * (gate * (1.0 + pre * (1.0 - gate)))
    grad_pre = grad_full.astype(BF16)
    base_ref[...] = upstream + dot_tn(w1_ref[:, :latent], grad_pre)
    grad_agg_ref[...] = dot_tn(w1_ref[:, latent:], grad_pre).astype(BF16)
    rows[...] = jnp.zeros_like(rows)
    rows[0:latent, :] = dot_nt(grad_pre, node_low)
    rows[latent : 2 * latent, :] = dot_nt(grad_pre, agg_low)
    rows[2 * latent : 3 * latent, :] = dot_nt(grad_post, hidden)
    at = 3 * latent
    rows[at : at + 1, :] = row_sum(grad_full)
    rows[at + 1 : at + 2, :] = row_sum(upstream * normed)
    rows[at + 2 : at + 3, :] = row_sum(upstream)

    def body(q, carry):
        hot = jnp.concatenate(
            [one_hot(idx_ref[2 * q], depth), one_hot(idx_ref[2 * q + 1], depth)], axis=1
        )
        picked = dot_nn(grad_agg_ref[...], hot).astype(BF16)
        for k in range(2):
            p = 2 * q + k
            out_ref[p, :TILE, :] = picked[:, k * TILE : (k + 1) * TILE]
            start = pl.multiple_of(p * NODE_ROWS, NODE_ROWS)
            out_ref[p, TILE:, :] = rows[pl.ds(start, NODE_ROWS), :].astype(BF16)
        return carry

    lax.fori_loop(0, peers // 2, body, 0)


def edge_bwd_kernel(
    tile_ref,
    count_ref,
    offset_ref,
    edge_ref,
    pair_ref,
    hidden_ref,
    slope_ref,
    normed_ref,
    inv_ref,
    agg_ref,
    mirror_ref,
    base_ref,
    w1_ref,
    w2_ref,
    gain_ref,
    edge_grad_ref,
    local_ref,
    out_ref,
    table,
    total,
    grad_w1,
    grad_w2,
    sum_gain,
    sum_shift,
    sum_bias,
    rows,
):
    step = pl.program_id(0)
    latent = edge_ref.shape[0]
    local_tiles = agg_ref.shape[1] // TILE

    @pl.when(step == 0)
    def _():
        fill_table(table, agg_ref, mirror_ref)
        total[...] = jnp.zeros_like(total)
        grad_w1[...] = jnp.zeros_like(grad_w1)
        grad_w2[...] = jnp.zeros_like(grad_w2)
        sum_gain[...] = jnp.zeros_like(sum_gain)
        sum_shift[...] = jnp.zeros_like(sum_shift)
        sum_bias[...] = jnp.zeros_like(sum_bias)

    lane = lax.broadcasted_iota(jnp.int32, (latent, TILE), 1)
    hots = []
    picked = []
    for j in range(GROUP):
        b = step * GROUP + j
        hot_s = one_hot(offset_ref[j, 0:1, :], TILE)
        hot_r = one_hot(offset_ref[j, 1:2, :], TILE)
        hots.append((hot_s, hot_r))
        found = dot_nn(table[tile_ref[b, 1]], hot_r)
        picked.append(jnp.where(lane < count_ref[b], found, 0.0))
    upstream = jnp.concatenate(picked, axis=1)
    normed = normed_ref[...]
    weighted = upstream * normed
    grad_post = norm_back(upstream, normed, inv_ref[...], gain_ref[...]).astype(BF16)
    hidden = hidden_ref[...]
    grad_w2[...] += dot_nt(grad_post, hidden)
    grad_full = dot_tn(w2_ref[...], grad_post) * slope_ref[...]
    grad_pre = grad_full.astype(BF16)
    edge_grad_ref[...] = dot_tn(w1_ref[:, :latent], grad_pre).astype(BF16)
    grad_w1[:, :latent] += dot_nt(grad_pre, edge_ref[...])
    grad_w1[:, latent:] += dot_nt(grad_pre, pair_ref[...])
    for j in range(GROUP):
        b = step * GROUP + j
        cols = slice(j * TILE, (j + 1) * TILE)
        sum_gain[...] += weighted[:, cols]
        sum_shift[...] += upstream[:, cols]
        sum_bias[...] += grad_full[:, cols]
        hot_s, hot_r = hots[j]
        total[tile_ref[b, 0], :latent, :] += dot_nt(grad_pre[:, cols], hot_s)
        total[tile_ref[b, 1], latent:, :] += dot_nt(grad_pre[:, cols], hot_r)

    @pl.when(step == pl.num_programs(0) - 1)
    def _():
        for t in range(local_tiles):
            cols = slice(t * TILE, (t + 1) * TILE)
            back = dot_tn(w1_ref[:, latent : 2 * latent], total[t, :latent, :].astype(BF16))
            back += dot_tn(w1_ref[:, 2 * latent :], total[t, latent:, :].astype(BF16))
            local_ref[:, cols] = base_ref[:, cols] + back
        for c in range(3):
            rows[c * latent : (c + 1) * latent, :] = grad_w1[:, c * latent : (c + 1) * latent]
        rows[3 * latent : 4 * latent, :] = grad_w2[...]

        def body(p, carry):
            t = local_tiles + p
            back = dot_tn(w1_ref[:, latent : 2 * latent], total[t, :latent, :].astype(BF16))
            back += dot_tn(w1_ref[:, 2 * latent :], total[t, latent:, :].astype(BF16))
            out_ref[p, :TILE, :] = back.astype(BF16)
            start = pl.multiple_of(p * 16, 16)
            out_ref[p, TILE : TILE + 16, :] = rows[pl.ds(start, 16), :].astype(BF16)
            out_ref[p, TILE + 16 :, :] = jnp.zeros((EDGE_ROWS - 16, TILE), BF16)
            return carry

        lax.fori_loop(0, out_ref.shape[0], body, 0)
        tail = jnp.concatenate(
            [
                row_sum(sum_bias[...]),
                row_sum(sum_gain[...]),
                row_sum(sum_shift[...]),
                jnp.zeros((EDGE_ROWS - 19, TILE), F32),
            ],
            axis=0,
        )
        out_ref[0, TILE + 16 :, :] = tail.astype(BF16)


def final_kernel(idx_ref, local_ref, mirror_ref, out_ref):
    out_ref[...] = local_ref[...]
    scatter_mirrors(out_ref, idx_ref, mirror_ref)


def params_kernel(edge_scale, node_scale, all_ref, out_ref, edge_rows, node_rows):
    peers = all_ref.shape[0]
    for p in range(peers):
        edge_rows[p * 16 : (p + 1) * 16, :] = all_ref[p, :16, :].astype(F32) * edge_scale
        node_rows[p * NODE_ROWS : (p + 1) * NODE_ROWS, :] = (
            all_ref[p, EDGE_ROWS:, :].astype(F32) * node_scale
        )
    tail = all_ref[0, 16:EDGE_ROWS, :].astype(F32) * edge_scale
    n = TILE
    for c in range(3):
        out_ref[pl.ds(c, n, stride=3), :] = edge_rows[c * n : (c + 1) * n, :]
    out_ref[3 * n : 3 * n + 1, :] = tail[0:1]
    out_ref[3 * n + 1 : 4 * n + 1, :] = edge_rows[3 * n : 4 * n, :]
    out_ref[4 * n + 1 : 4 * n + 3, :] = tail[1:3]
    at = 4 * n + 3
    for c in range(2):
        out_ref[pl.ds(at + c, n, stride=2), :] = node_rows[c * n : (c + 1) * n, :]
    at += 2 * n
    out_ref[at : at + 1, :] = node_rows[3 * n : 3 * n + 1, :]
    out_ref[at + 1 : at + 1 + n, :] = node_rows[2 * n : 3 * n, :]
    out_ref[at + 1 + n : at + 3 + n, :] = node_rows[3 * n + 1 : 3 * n + 3, :]


VMEM = pl.BlockSpec(memory_space=pltpu.VMEM)
SMEM = pl.BlockSpec(memory_space=pltpu.SMEM)
PARAMS = pltpu.CompilerParams(vmem_limit_bytes=48 * 1024 * 1024)


def whole(kernel, out_shape, n_in, scratch, name):
    return pl.pallas_call(
        kernel,
        out_shape=out_shape,
        in_specs=[VMEM] * n_in,
        out_specs=jax.tree.map(lambda _: VMEM, out_shape),
        scratch_shapes=scratch,
        compiler_params=PARAMS,
        interpret=INTERPRET,
        name=name,
    )


def per_device(
    node_feat,
    edge_feat,
    route,
    block_tile,
    block_offset,
    block_count,
    w_edge1,
    bias_edge1,
    w_edge2,
    gain_edge,
    shift_edge,
    w_node1,
    bias_node1,
    w_node2,
    gain_node,
    shift_node,
    node_cot,
):
    latent, masters = node_feat.shape
    slots = edge_feat.shape[1]
    blocks = block_tile.shape[0]
    peers = lax.axis_size("cut")
    total_nodes = masters * peers
    total_edges = slots * peers
    tiles = masters // TILE + peers
    shape = jax.ShapeDtypeStruct

    def swap(values):
        return lax.all_to_all(values, "cut", split_axis=0, concat_axis=0, tiled=True)

    def column(vector):
        return vector[:, None]

    idx = swap(route[0][:, None, :])
    outgoing = whole(gather_kernel, shape((peers, latent, TILE), BF16), 2, [], "gather")(
        idx, node_feat
    )
    mirrors = swap(outgoing)

    steps = blocks // GROUP
    width = GROUP * TILE

    def full(dims):
        return pl.BlockSpec(dims, lambda i: (0,) * len(dims))

    def wide(height):
        return pl.BlockSpec((height, width), lambda i: (0, i))

    offsets = pl.BlockSpec((GROUP, 2, TILE), lambda i: (i, 0, 0))
    pair, hidden, slope, normed, inv, local_sum, returned = pl.pallas_call(
        edge_fwd_kernel,
        grid=(steps,),
        out_shape=(
            shape((2 * latent, slots), BF16),
            shape((latent, slots), BF16),
            shape((latent, slots), F32),
            shape((latent, slots), F32),
            shape((1, slots), F32),
            shape((latent, masters), F32),
            shape((peers, latent, TILE), BF16),
        ),
        in_specs=[
            SMEM,
            SMEM,
            offsets,
            wide(latent),
            full((latent, masters)),
            full((peers, latent, TILE)),
            full((latent, 3 * latent)),
            full((latent, 1)),
            full((latent, latent)),
            full((latent, 1)),
            full((latent, 1)),
        ],
        out_specs=(
            wide(2 * latent),
            wide(latent),
            wide(latent),
            wide(latent),
            wide(1),
            full((latent, masters)),
            full((peers, latent, TILE)),
        ),
        scratch_shapes=[
            pltpu.VMEM((tiles, latent, TILE), BF16),
            pltpu.VMEM((tiles, latent, TILE), F32),
        ],
        compiler_params=PARAMS,
        interpret=INTERPRET,
        name="edge_fwd",
    )(
        block_tile,
        block_count,
        block_offset,
        edge_feat,
        node_feat,
        mirrors,
        w_edge1,
        column(bias_edge1),
        w_edge2,
        column(gain_edge),
        column(shift_edge),
    )
    returned = swap(returned)

    node_out, base, grad_agg, outgoing = whole(
        node_kernel,
        (
            shape((latent, masters), BF16),
            shape((latent, masters), F32),
            shape((latent, masters), BF16),
            shape((peers, latent + NODE_ROWS, TILE), BF16),
        ),
        10,
        [pltpu.VMEM((latent, masters), F32), pltpu.VMEM((peers * NODE_ROWS, TILE), F32)],
        "node",
    )(
        idx,
        local_sum,
        returned,
        node_feat,
        node_cot,
        w_node1,
        column(bias_node1),
        w_node2,
        column(gain_node),
        column(shift_node),
    )
    mirrors = swap(outgoing)
    node_shard = jnp.sum(mirrors[:, latent:, :].astype(F32), axis=0).astype(BF16)

    edge_grad, local_grad, returned = pl.pallas_call(
        edge_bwd_kernel,
        grid=(steps,),
        out_shape=(
            shape((latent, slots), BF16),
            shape((latent, masters), F32),
            shape((peers, latent + EDGE_ROWS, TILE), BF16),
        ),
        in_specs=[
            SMEM,
            SMEM,
            offsets,
            wide(latent),
            wide(2 * latent),
            wide(latent),
            wide(latent),
            wide(latent),
            wide(1),
            full((latent, masters)),
            full((peers, latent + NODE_ROWS, TILE)),
            full((latent, masters)),
            full((latent, 3 * latent)),
            full((latent, latent)),
            full((latent, 1)),
        ],
        out_specs=(
            wide(latent),
            full((latent, masters)),
            full((peers, latent + EDGE_ROWS, TILE)),
        ),
        scratch_shapes=[
            pltpu.VMEM((tiles, latent, TILE), BF16),
            pltpu.VMEM((tiles, 2 * latent, TILE), F32),
            pltpu.VMEM((latent, 3 * latent), F32),
            pltpu.VMEM((latent, latent), F32),
            pltpu.VMEM((latent, TILE), F32),
            pltpu.VMEM((latent, TILE), F32),
            pltpu.VMEM((latent, TILE), F32),
            pltpu.VMEM((4 * latent, TILE), F32),
        ],
        compiler_params=PARAMS,
        interpret=INTERPRET,
        name="edge_bwd",
    )(
        block_tile,
        block_count,
        block_offset,
        edge_feat,
        pair,
        hidden,
        slope,
        normed,
        inv,
        grad_agg,
        mirrors,
        base,
        w_edge1,
        w_edge2,
        column(gain_edge),
    )
    returned = swap(returned)
    edge_shard = jnp.sum(returned[:, latent:, :].astype(F32), axis=0).astype(BF16)
    shard = jnp.concatenate([edge_shard, node_shard], axis=0)
    gathered = swap(jnp.broadcast_to(shard[None], (peers,) + shard.shape))
    node_grad = whole(final_kernel, shape((latent, masters), F32), 3, [], "final")(
        idx, local_grad, returned
    )
    param_rows = whole(
        functools.partial(
            params_kernel, 1.0 / math.sqrt(total_edges), 1.0 / math.sqrt(total_nodes)
        ),
        shape((902, TILE), F32),
        1,
        [pltpu.VMEM((peers * 16, TILE), F32), pltpu.VMEM((peers * NODE_ROWS, TILE), F32)],
        "params",
    )(gathered)
    return (node_out, node_grad, edge_grad, param_rows.reshape(-1))


def solution(mesh):
    nodes = P(None, ("dp", "cut"))
    rows = P(("dp", "cut"))
    in_specs = (nodes, nodes, rows, rows, rows, rows) + (P(),) * 10 + (nodes,)
    out_specs = (nodes, nodes, nodes, P("dp"))
    return jax.shard_map(
        per_device, mesh=mesh, in_specs=in_specs, out_specs=out_specs, check_vma=False
    )
```

time: 508 us -> 232 us (0.46)
  other arithmetic: 136 us -> 0.08 us
  waiting for transfers between devices: 222 us -> 89.1 us
  local copies, waits for them, and re-layouts: 88.5 us -> 20.1 us
  blocking collectives: 0 us -> 57.8 us
  Pallas kernels: 0 us -> 45.2 us
  matrix products: 14.8 us -> 0 us
  between operations: 14.8 us -> 0.81 us
  starting transfers between devices: 30.6 us -> 18 us
    psum x1 -> x0, waiting for transfers between devices: 137 us -> none  [per_device(): lax.psum(jnp.concatenate([edge_vec, node_vec]).astype(jnp.bfloat16), 'cut')]
    scatter-add x5 -> x0, other arithmetic: 116 us -> none  [the longest x2 47.1 us: per_device(): grad_table = jnp.zeros((latent, local_width), jnp.float32).at[:, send_col...]
    gather x6 -> x0, local copies, waits for them, and re-layouts: 68.1 us -> none  [the longest x2 24.3 us: fetch_mirrors(): outgoing = jnp.take(master_part, mirror_index, axis=1)]
    all_to_all x0 -> x2, blocking collectives: none -> 57.8 us  [swap(): lax.all_to_all(values, 'cut', split_axis=0, concat_axis=0, tiled=True)]
    pallas_call x0 -> x6, Pallas kernels: none -> 45.2 us  [the longest x1 15 us: per_device(): pl.pallas_call(edge_bwd_kernel, grid=(steps,), out_shape=(shape((latent,...]
    dot_general x15 -> x0, matrix products: 14.8 us -> none  [the longest x7 7.76 us: lead_contract(): lax.dot_general(weight, values, (((0,), (0,)), ((), ())), preferred_eleme...]
    all_to_all x5 -> x4, starting transfers between devices: 30.5 us -> 18 us  [swap(): lax.all_to_all(values, 'cut', split_axis=0, concat_axis=0, tiled=True)]
    select_n x5 -> x0, other arithmetic: 9.49 us -> none  [the longest x2 5.77 us: fetch_mirrors(): outgoing = jnp.take(master_part, mirror_index, axis=1)]
  transfers between devices with their start and end apart: 6 -> 4, of which waited for: 5 -> 4; matrix products, arithmetic and copies ran while one was open for 2% -> 2% of each run, Pallas kernels for 0% -> 3%
where the time goes in v1:
time: 232 us; the launch traced here: 231 us
  waiting for transfers between devices  89.1 us (38%)
  blocking collectives  57.8 us (25%)
  Pallas kernels  45.2 us (19%)
  local copies, waits for them, and re-layouts  20.1 us (9%)
  starting transfers between devices  18 us (8%)
    all_to_all x4, waiting for transfers between devices, swap(): lax.all_to_all(values, 'cut', split_axis=0, concat_axis=0, tiled=True)  89.1 us
    all_to_all x2, blocking collectives, swap(): lax.all_to_all(values, 'cut', split_axis=0, concat_axis=0, tiled=True)  57.8 us
    all_to_all x4, starting transfers between devices, swap(): lax.all_to_all(values, 'cut', split_axis=0, concat_axis=0, tiled=True)  18 us
    pallas_call x1, Pallas kernels, per_device(): pl.pallas_call(edge_bwd_kernel, grid=(steps,), out_shape=(shape((latent,...  15 us
    unnamed x61, local copies, waits for them, and re-layouts  14.8 us
    pallas_call x1, Pallas kernels, per_device(): whole(node_kernel, (shape((latent, masters), BF16), shape((latent, master...  10.7 us
    pallas_call x1, Pallas kernels, per_device(): pl.pallas_call(edge_fwd_kernel, grid=(steps,), out_shape=(shape((2 * late...  7.96 us
    pallas_call x1, Pallas kernels, per_device(): whole(final_kernel, shape((latent, masters), F32), 3, [], 'final')  5.82 us
  transfers between devices with their start and end apart: 4, of which 4 were waited for; matrix products, arithmetic and copies ran while one was open for 2% of the time, Pallas kernels for 3%

profile of v1, /device:TPU:6, one launch (start us, length us, event | category | flops | bytes accessed | tf_op | source)
XLA Modules:
  0.0 231.0 jit_solution(2353479894009828424)
XLA Ops:
  0.6 21.2 %all_to_all.30.idx_ref = s32[32,1,128]{2,1,0:T(1,128)S(1)} all-to-all(s32[32,1,128]{2,1,0:T(1,128)} %bitcast.9), channel_id=1, replica_groups=mesh['dp'=8,'cut'=32] {'cut'}, dimensions={0} | all-to-all | bytes 32768 | tf_op jit(solution)/shard_map/all_to_all | solution.py:422
  21.8 0.0 copy-start.1
  21.8 0.9 copy-done.1
  22.8 4.8 %gather.1 = bf16[32,128,128]{2,1,0:T(8,128)(2,1)} custom-call(s32[32,1,128]{2,1,0:T(1,128)S(1)} %all_to_all.30.idx_ref, bf16[128,1024]{1,0:T(8,128)(2,1)S(1)} %copy-done.1), custom_call_target="tpu_custom_call" | custom-call | tf_op jit(solution)/shard_map/gather/pallas_call | solution.py:428
  27.6 0.0 copy-start.26
  27.6 0.0 copy-start.27
  27.6 0.0 copy-start.28
  27.6 0.0 copy-start
  27.7 0.0 copy-start.2
  27.7 4.1 %all-to-all-start.1 = ((bf16[32,128,128]{2,1,0:T(8,128)(2,1)}), bf16[32,128,128]{2,1,0:T(8,128)(2,1)S(1)}, u32[]{:S(2)}, u32[]{:S(2)}) async-start(bf16[32,128,128]{2,1,0:T(8,128)(2,1)} %gather.1), calls=%async_computation.1 | async-start | bytes 2097152 | tf_op jit(solution)/shard_map/all_to_all | solution.py:422
  31.8 0.0 copy-done.26
  31.8 0.7 copy.21.tile_ref
  32.4 0.0 copy-done.27
  32.4 0.1 copy.23.gain_ref
  32.6 0.0 copy-done.28
  32.6 0.1 copy.22.b1_ref
  32.7 0.0 copy-done.29
  32.7 0.7 copy.24.shift_ref
  33.4 25.9 %all-to-all-done.1.mirror_ref = bf16[32,128,128]{2,1,0:T(8,128)(2,1)S(1)} async-done(((bf16[32,128,128]{2,1,0:T(8,128)(2,1)}), bf16[32,128,128]{2,1,0:T(8,128)(2,1)S(1)}, u32[]{:S(2)}, u32[]{:S(2)}) %all-to-all-start.1) | async-done | bytes 1048608 | tf_op jit(solution)/shard_map/all_to_all | solution.py:422
  59.3 0.0 copy-done
  59.3 0.0 copy-done.2
  59.3 0.9 copy-done.8
  60.2 0.8 copy-done.11
  61.1 0.7 copy-done.14
  61.8 0.8 copy-done.16
  62.5 0.8 copy-done.18
  63.3 0.7 copy-done.24
  64.0 8.0 %edge_fwd.1 = (bf16[256,4096]{1,0:T(8,128)(2,1)}, bf16[128,4096]{1,0:T(8,128)(2,1)S(1)}, f32[128,4096]{1,0:T(8,128)}, f32[128,4096]{1,0:T(8,128)}, f32[1,4096]{1...) custom-call(s32[32,2]{1,0:T(8,128)S(1)} %copy-done.14, s32[32]{0:T(128)S(1)} %copy-done.24, ...), custom_call_target="tpu_custom_call" | custom-call | tf_op jit(solution)/shard_map/edge_fwd/pallas_call | solution.py:443
  71.9 0.0 copy-start.6
  71.9 0.8 copy-done.6
  72.7 0.6 copy-done.22
  73.3 5.0 %all-to-all-start.2 = ((bf16[32,128,128]{2,1,0:T(8,128)(2,1)}), bf16[32,128,128]{2,1,0:T(8,128)(2,1)S(1)}, u32[]{:S(2)}, u32[]{:S(2)}) async-start(bf16[32,128,128]{2,1,0:T(8,128)(2,1)} %get-tuple-element.19), calls=%async_computation.2 | async-start | bytes 2097152 | tf_op jit(solution)/shard_map/all_to_all | solution.py:422
  78.3 0.8 copy.25.b1_ref
  79.1 1.4 copy.26.gain_ref
  80.5 1.4 copy.27.shift_ref
  81.9 24.1 %all-to-all-done.2.mirror_ref = bf16[32,128,128]{2,1,0:T(8,128)(2,1)S(1)} async-done(((bf16[32,128,128]{2,1,0:T(8,128)(2,1)}), bf16[32,128,128]{2,1,0:T(8,128)(2,1)S(1)}, u32[]{:S(2)}, u32[]{:S(2)}) %all-to-all-start.2) | async-done | bytes 1048608 | tf_op jit(solution)/shard_map/all_to_all | solution.py:422
  106.0 1.0 copy-done.7
  107.0 0.9 copy-done.10
  108.0 0.8 copy-done.12
  108.8 0.8 copy-done.13
  109.6 0.8 copy-done.20
  110.5 0.8 copy-done.21
  111.2 10.7 %node.1 = (bf16[128,1024]{1,0:T(8,128)(2,1)}, f32[128,1024]{1,0:T(8,128)S(1)}, bf16[128,1024]{1,0:T(8,128)(2,1)S(1)}, bf16[32,144,128]{2,1,0:T(8,128)(2,1)S(1)}) custom-call(s32[32,1,128]{2,1,0:T(1,128)S(1)} %all_to_all.30.idx_ref, f32[128,1024]{1,0:T(8,128)S(1)} %copy-done.7, bf16[32,128,128]{2,1,0:T(8,128)(2,1)S(1)} %all-to-all-done.2.mirror_ref, ...), custom_call_target="tpu_custom_call" | custom-call | tf_op jit(solution)/shard_map/node/pallas_call | solution.py:499
  122.0 0.0 copy-start.23
  122.0 0.0 copy-start.25
  122.0 36.6 %all_to_all.31.mirror_ref = bf16[32,144,128]{2,1,0:T(8,128)(2,1)S(1)} all-to-all(bf16[32,144,128]{2,1,0:T(8,128)(2,1)S(1)} %get-tuple-element.27), channel_id=1, replica_groups=mesh['dp'=8,'cut'=32] {'cut'}, dimensions={0} | all-to-all | bytes 2359296 | tf_op jit(solution)/shard_map/all_to_all | solution.py:422
  158.6 0.0 copy-done.9
  158.6 0.0 copy-done.15
  158.6 0.0 copy-done.17
  158.6 0.0 copy-done.19
  158.6 0.0 copy-done.23
  158.6 0.0 copy-done.25
  158.6 15.0 %edge_bwd.1 = (bf16[128,4096]{1,0:T(8,128)(2,1)}, f32[128,1024]{1,0:T(8,128)S(1)}, bf16[32,152,128]{2,1,0:T(8,128)(2,1)S(1)}) custom-call(s32[32,2]{1,0:T(8,128)S(1)} %copy-done.15, s32[32]{0:T(128)S(1)} %copy-done.25, s32[32,2,128]{2,1,0:T(2,128)S(1)} %copy-done.17, bf16[128,4096]{1,0:T(8,128)(2,1)S(1)} %copy-done, ...), custom_call_target="tpu_custom_call" | custom-call | tf_op jit(solution)/shard_map/edge_bwd/pallas_call | solution.py:525
  173.6 1.1 copy-done.3
  174.7 0.8 copy-done.4
  175.5 3.9 %all-to-all-start.4 = ((bf16[32,152,128]{2,1,0:T(8,128)(2,1)}), bf16[32,152,128]{2,1,0:T(8,128)(2,1)S(1)}, u32[]{:S(2)}, u32[]{:S(2)}) async-start(bf16[32,152,128]{2,1,0:T(8,128)(2,1)} %copy-done.3), calls=%async_computation.4 | async-start | bytes 2490368 | tf_op jit(solution)/shard_map/all_to_all | solution.py:422
  179.4 0.0 copy-start.5
  179.5 32.0 %all-to-all-done.4.mirror_ref = bf16[32,152,128]{2,1,0:T(8,128)(2,1)S(1)} async-done(((bf16[32,152,128]{2,1,0:T(8,128)(2,1)}), bf16[32,152,128]{2,1,0:T(8,128)(2,1)S(1)}, u32[]{:S(2)}, u32[]{:S(2)}) %all-to-all-start.4) | async-done | bytes 1245216 | tf_op jit(solution)/shard_map/all_to_all | solution.py:422
  211.6 0.8 broadcast_in_dim.31
  212.3 5.0 %all-to-all-start.5 = ((bf16[32,40,128]{2,1,0:T(8,128)(2,1)}), bf16[32,40,128]{2,1,0:T(8,128)(2,1)S(1)}, u32[]{:S(2)}, u32[]{:S(2)}) async-start(bf16[32,40,128]{2,1,0:T(8,128)(2,1)} %broadcast_in_dim.31), calls=%async_computation.5 | async-start | bytes 655360 | tf_op jit(solution)/shard_map/all_to_all | solution.py:422
  217.3 0.0 copy-done.5
  217.3 5.8 %final.1 = f32[128,1024]{1,0:T(8,128)} custom-call(s32[32,1,128]{2,1,0:T(1,128)S(1)} %all_to_all.30.idx_ref, f32[128,1024]{1,0:T(8,128)S(1)} %copy-done.5, bf16[32,152,128]{2,1,0:T(8,128)(2,1)S(1)} %all-to-all-done.4.mirror_ref), custom_call_target="tpu_custom_call" | custom-call | tf_op jit(solution)/shard_map/final/pallas_call | solution.py:589
  223.2 7.1 %all-to-all-done.5.all_ref = bf16[32,40,128]{2,1,0:T(8,128)(2,1)S(1)} async-done(((bf16[32,40,128]{2,1,0:T(8,128)(2,1)}), bf16[32,40,128]{2,1,0:T(8,128)(2,1)S(1)}, u32[]{:S(2)}, u32[]{:S(2)}) %all-to-all-start.5) | async-done | bytes 327712 | tf_op jit(solution)/shard_map/all_to_all | solution.py:422
  230.2 0.8 params.1
  (23 shorter events, 0.1 us)
Async XLA Ops:
  21.8 1.0 copy-start.1
  27.6 4.1 %copy-start.26 = (s32[32,2]{0,1:T(2,128)S(1)}, s32[32,2]{0,1:T(2,128)}, u32[]{:S(2)}) copy-start(s32[32,2]{0,1:T(2,128)} %param.20) | copy-start | bytes 772
  27.6 4.8 %copy-start.27 = (f32[128]{0:T(128)S(1)}, f32[128]{0:T(128)}, u32[]{:S(2)}) copy-start(f32[128]{0:T(128)} %param.26) | copy-start | bytes 1540
  27.6 4.9 %copy-start.28 = (f32[128]{0:T(128)S(1)}, f32[128]{0:T(128)}, u32[]{:S(2)}) copy-start(f32[128]{0:T(128)} %param.24) | copy-start | bytes 1540
  27.6 5.0 %copy-start.29 = (f32[128]{0:T(128)S(1)}, f32[128]{0:T(128)}, u32[]{:S(2)}) copy-start(f32[128]{0:T(128)} %param.27) | copy-start | bytes 1540
  27.6 31.7 %copy-start = (bf16[128,4096]{1,0:T(8,128)(2,1)S(1)}, bf16[128,4096]{1,0:T(8,128)(2,1)}, u32[]{:S(2)}) copy-start(bf16[128,4096]{1,0:T(8,128)(2,1)} %edge_ref.3) | copy-start | bytes 3145732
  27.7 31.7 %copy-start.2 = (bf16[128,1024]{1,0:T(8,128)(2,1)S(1)}, bf16[128,1024]{1,0:T(8,128)(2,1)}, u32[]{:S(2)}) copy-start(bf16[128,1024]{1,0:T(8,128)(2,1)} %node_ref.3) | copy-start | bytes 786436
  27.7 31.7 %all-to-all-start.1 = ((bf16[32,128,128]{2,1,0:T(8,128)(2,1)}), bf16[32,128,128]{2,1,0:T(8,128)(2,1)S(1)}, u32[]{:S(2)}, u32[]{:S(2)}) async-start(bf16[32,128,128]{2,1,0:T(8,128)(2,1)} %gather.1), calls=%async_computation.1 | async-start | bytes 2097152 | tf_op jit(solution)/shard_map/all_to_all | solution.py:422
  59.3 0.9 copy-start.8
  60.2 0.8 copy-start.11
  61.1 0.7 copy-start.14
  61.8 0.8 copy-start.16
  62.5 0.8 copy-start.18
  63.3 0.7 copy-start.24
  71.9 0.8 copy-start.6
  72.7 0.6 copy-start.22
  73.3 32.7 %all-to-all-start.2 = ((bf16[32,128,128]{2,1,0:T(8,128)(2,1)}), bf16[32,128,128]{2,1,0:T(8,128)(2,1)S(1)}, u32[]{:S(2)}, u32[]{:S(2)}) async-start(bf16[32,128,128]{2,1,0:T(8,128)(2,1)} %get-tuple-element.19), calls=%async_computation.2 | async-start | bytes 2097152 | tf_op jit(solution)/shard_map/all_to_all | solution.py:422
  106.0 1.0 copy-start.7
  107.0 0.9 copy-start.10
  108.0 0.8 copy-start.12
  108.8 0.8 copy-start.13
  109.6 0.8 copy-start.20
  110.5 0.8 copy-start.21
  122.0 36.6 %copy-start.9 = (bf16[128,384]{1,0:T(8,128)(2,1)S(1)}, bf16[128,384]{1,0:T(8,128)(2,1)}, u32[]{:S(2)}) copy-start(bf16[128,384]{1,0:T(8,128)(2,1)} %w1_ref.5) | copy-start | bytes 294916
  122.0 36.6 %copy-start.15 = (s32[32,2]{1,0:T(8,128)S(1)}, s32[32,2]{1,0:T(8,128)}, u32[]{:S(2)}) copy-start(s32[32,2]{1,0:T(8,128)} %copy.21.tile_ref) | copy-start | bytes 772
  122.0 36.6 %copy-start.17 = (s32[32,2,128]{2,1,0:T(2,128)S(1)}, s32[32,2,128]{2,1,0:T(2,128)}, u32[]{:S(2)}) copy-start(s32[32,2,128]{2,1,0:T(2,128)} %offset_ref.3) | copy-start | bytes 98308
  122.0 36.6 %copy-start.19 = (bf16[128,128]{1,0:T(8,128)(2,1)S(1)}, bf16[128,128]{1,0:T(8,128)(2,1)}, u32[]{:S(2)}) copy-start(bf16[128,128]{1,0:T(8,128)(2,1)} %w2_ref.5) | copy-start | bytes 98308
  122.0 36.6 %copy-start.23 = (f32[1,4096]{1,0:T(1,128)S(1)}, f32[1,4096]{1,0:T(1,128)}, u32[]{:S(2)}) copy-start(f32[1,4096]{1,0:T(1,128)} %copy-done.22) | copy-start | bytes 49156
  122.0 36.6 %copy-start.25 = (s32[32]{0:T(128)S(1)}, s32[32]{0:T(128)}, u32[]{:S(2)}) copy-start(s32[32]{0:T(128)} %count_ref.3) | copy-start | bytes 388
  173.6 1.1 copy-start.3
  174.7 0.8 copy-start.4
  175.5 36.0 %all-to-all-start.4 = ((bf16[32,152,128]{2,1,0:T(8,128)(2,1)}), bf16[32,152,128]{2,1,0:T(8,128)(2,1)S(1)}, u32[]{:S(2)}, u32[]{:S(2)}) async-start(bf16[32,152,128]{2,1,0:T(8,128)(2,1)} %copy-done.3), calls=%async_computation.4 | async-start | bytes 2490368 | tf_op jit(solution)/shard_map/all_to_all | solution.py:422
  179.4 37.9 %copy-start.5 = (f32[128,1024]{1,0:T(8,128)S(1)}, f32[128,1024]{1,0:T(8,128)}, u32[]{:S(2)}) copy-start(f32[128,1024]{1,0:T(8,128)} %copy-done.4) | copy-start | bytes 1572868
  212.3 17.9 %all-to-all-start.5 = ((bf16[32,40,128]{2,1,0:T(8,128)(2,1)}), bf16[32,40,128]{2,1,0:T(8,128)(2,1)S(1)}, u32[]{:S(2)}, u32[]{:S(2)}) async-start(bf16[32,40,128]{2,1,0:T(8,128)(2,1)} %broadcast_in_dim.31), calls=%async_computation.5 | async-start | bytes 655360 | tf_op jit(solution)/shard_map/all_to_all | solution.py:422

commit v2 on v1

--- a/solution.py
+++ b/solution.py
@@ -12,6 +12,7 @@
 BF16 = jnp.bfloat16
 TILE = 128
 GROUP = 8
+WIDE = 4
 NODE_ROWS = 16
 EDGE_ROWS = 24
 INTERPRET = False
@@ -36,6 +37,15 @@
 
 def sigmoid(values):
     return 1.0 / (1.0 + jnp.exp(-values))
+
+
+def one_hot_rows(index_columns, depth):
+    lanes = lax.broadcasted_iota(jnp.int32, (index_columns.shape[0], depth), 1)
+    return jnp.where(lanes == index_columns, 1.0, 0.0).astype(BF16)
+
+
+def column(row_ref):
+    return jnp.broadcast_to(row_ref[...], (8, row_ref.shape[1])).T[:, :1]
 
 
 def layer_norm(values):
@@ -53,19 +63,20 @@
     )
 
 
+def gather_peers(idx_ref, table, store):
+    depth = table.shape[1]
+    for q in range(0, idx_ref.shape[0], WIDE):
+        index_row = jnp.concatenate([idx_ref[q + k] for k in range(WIDE)], axis=1)
+        picked = dot_nn(table, one_hot(index_row, depth)).astype(BF16)
+        for k in range(WIDE):
+            store(q + k, picked[:, k * TILE : (k + 1) * TILE])
+
+
 def gather_kernel(idx_ref, table_ref, out_ref):
-    peers = out_ref.shape[0]
-    depth = table_ref.shape[1]
-
-    def body(q, carry):
-        hot0 = one_hot(idx_ref[2 * q], depth)
-        hot1 = one_hot(idx_ref[2 * q + 1], depth)
-        picked = dot_nn(table_ref[...], jnp.concatenate([hot0, hot1], axis=1)).astype(BF16)
-        out_ref[2 * q] = picked[:, :TILE]
-        out_ref[2 * q + 1] = picked[:, TILE:]
-        return carry
-
-    lax.fori_loop(0, peers // 2, body, 0)
+    def store(p, values):
+        out_ref[p] = values
+
+    gather_peers(idx_ref, table_ref[...], store)
 
 
 def fill_table(table, local_ref, mirror_ref):
@@ -111,19 +122,18 @@
         fill_table(table, node_ref, mirror_ref)
         total[...] = jnp.zeros_like(total)
 
-    receiver_hot = []
     for j in range(GROUP):
         b = step * GROUP + j
+        both = jnp.concatenate([offset_ref[j, 0:1, :], offset_ref[j, 1:2, :] + TILE], axis=1)
+        tiles = jnp.concatenate([table[tile_ref[0, b]], table[tile_ref[1, b]]], axis=1)
+        found = dot_nn(tiles, one_hot(both, 2 * TILE)).astype(BF16)
         cols = slice(j * TILE, (j + 1) * TILE)
-        hot_s = one_hot(offset_ref[j, 0:1, :], TILE)
-        hot_r = one_hot(offset_ref[j, 1:2, :], TILE)
-        receiver_hot.append(hot_r)
-        pair_ref[:latent, cols] = dot_nn(table[tile_ref[b, 0]], hot_s).astype(BF16)
-        pair_ref[latent:, cols] = dot_nn(table[tile_ref[b, 1]], hot_r).astype(BF16)
+        pair_ref[:latent, cols] = found[:, :TILE]
+        pair_ref[latent:, cols] = found[:, TILE:]
     pre = (
         dot_nn(w1_ref[:, :latent], edge_ref[...])
         + dot_nn(w1_ref[:, latent:], pair_ref[...])
-        + b1_ref[...]
+        + column(b1_ref)
     )
     gate = sigmoid(pre)
     hidden = (pre * gate).astype(BF16)
@@ -132,14 +142,15 @@
     normed, inverse = layer_norm(dot_nn(w2_ref[...], hidden))
     normed_ref[...] = normed
     inv_ref[...] = inverse
-    message = gain_ref[...] * normed + shift_ref[...]
+    message = column(gain_ref) * normed + column(shift_ref)
+    turned = offset_ref[:, 1, :].T
     lane = lax.broadcasted_iota(jnp.int32, (latent, TILE), 1)
     for j in range(GROUP):
         b = step * GROUP + j
         cols = slice(j * TILE, (j + 1) * TILE)
         kept = jnp.where(lane < count_ref[b], message[:, cols], 0.0).astype(BF16)
-        tile = tile_ref[b, 1]
-        total[tile] += dot_nt(kept, receiver_hot[j])
+        tile = tile_ref[1, b]
+        total[tile] += dot_nn(kept, one_hot_rows(turned[:, j : j + 1], TILE))
 
     @pl.when(step == pl.num_programs(0) - 1)
     def _():
@@ -153,20 +164,17 @@
         lax.fori_loop(0, out_ref.shape[0], body, 0)
 
 
-def scatter_mirrors(total_ref, idx_ref, mirror_ref):
-    depth = total_ref.shape[1]
-
-    def body(q, carry):
+def scatter_mirrors(total, idx_ref, mirror_ref):
+    depth = total.shape[1]
+    peers = idx_ref.shape[0]
+    turned = jnp.concatenate([idx_ref[p] for p in range(peers)], axis=0).T
+    for q in range(0, peers, WIDE):
         hot = jnp.concatenate(
-            [one_hot(idx_ref[2 * q], depth), one_hot(idx_ref[2 * q + 1], depth)], axis=1
+            [one_hot_rows(turned[:, p : p + 1], depth) for p in range(q, q + WIDE)], axis=0
         )
-        values = jnp.concatenate(
-            [mirror_ref[2 * q, :TILE, :], mirror_ref[2 * q + 1, :TILE, :]], axis=1
-        )
-        total_ref[...] += dot_nt(values, hot)
-        return carry
-
-    lax.fori_loop(0, mirror_ref.shape[0] // 2, body, 0)
+        values = jnp.concatenate([mirror_ref[p, :TILE, :] for p in range(q, q + WIDE)], axis=1)
+        total += dot_nn(values, hot)
+    return total
 
 
 def row_sum(values):
@@ -191,22 +199,17 @@
     base_ref,
     grad_agg_ref,
     out_ref,
-    total,
     rows,
 ):
     latent = node_ref.shape[0]
-    peers = out_ref.shape[0]
-    depth = node_ref.shape[1]
-    total[...] = local_ref[...]
-    scatter_mirrors(total, idx_ref, mirror_ref)
-    agg_low = total[...].astype(BF16)
+    agg_low = scatter_mirrors(local_ref[...], idx_ref, mirror_ref).astype(BF16)
     node_low = node_ref[...]
-    pre = dot_nn(w1_ref[:, :latent], node_low) + dot_nn(w1_ref[:, latent:], agg_low) + b1_ref[...]
+    pre = dot_nn(w1_ref[:, :latent], node_low) + dot_nn(w1_ref[:, latent:], agg_low) + column(b1_ref)
     gate = sigmoid(pre)
     hidden = (pre * gate).astype(BF16)
     normed, inverse = layer_norm(dot_nn(w2_ref[...], hidden))
-    gain = gain_ref[...]
-    node_out_ref[...] = (node_low.astype(F32) + gain * normed + shift_ref[...]).astype(BF16)
+    gain = column(gain_ref)
+    node_out_ref[...] = (node_low.astype(F32) + gain * normed + column(shift_ref)).astype(BF16)
     upstream = cot_ref[...].astype(F32)
     grad_post = norm_back(upstream, normed, inverse, gain).astype(BF16)
     grad_full = dot_tn(w2_ref[...], grad_post) * (gate * (1.0 + pre * (1.0 - gate)))
@@ -222,19 +225,11 @@
     rows[at + 1 : at + 2, :] = row_sum(upstream * normed)
     rows[at + 2 : at + 3, :] = row_sum(upstream)
 
-    def body(q, carry):
-        hot = jnp.concatenate(
-            [one_hot(idx_ref[2 * q], depth), one_hot(idx_ref[2 * q + 1], depth)], axis=1
-        )
-        picked = dot_nn(grad_agg_ref[...], hot).astype(BF16)
-        for k in range(2):
-            p = 2 * q + k
-            out_ref[p, :TILE, :] = picked[:, k * TILE : (k + 1) * TILE]
-            start = pl.multiple_of(p * NODE_ROWS, NODE_ROWS)
-            out_ref[p, TILE:, :] = rows[pl.ds(start, NODE_ROWS), :].astype(BF16)
-        return carry
-
-    lax.fori_loop(0, peers // 2, body, 0)
+    def store(p, values):
+        out_ref[p, :TILE, :] = values
+        out_ref[p, TILE:, :] = rows[p * NODE_ROWS : (p + 1) * NODE_ROWS, :].astype(BF16)
+
+    gather_peers(idx_ref, grad_agg_ref[...], store)
 
 
 def edge_bwd_kernel(
@@ -264,6 +259,9 @@
     sum_shift,
     sum_bias,
     rows,
+    w1_turned,
+    w1_pair,
+    w2_turned,
 ):
     step = pl.program_id(0)
     latent = edge_ref.shape[0]
@@ -278,60 +276,68 @@
         sum_gain[...] = jnp.zeros_like(sum_gain)
         sum_shift[...] = jnp.zeros_like(sum_shift)
         sum_bias[...] = jnp.zeros_like(sum_bias)
+        w2_turned[...] = w2_ref[...].T
+        w1_turned[...] = w1_ref[:, :latent].T
+        w1_pair[:, :latent] = w1_ref[:, latent : 2 * latent].T
+        w1_pair[:, latent:] = w1_ref[:, 2 * latent :].T
 
     lane = lax.broadcasted_iota(jnp.int32, (latent, TILE), 1)
-    hots = []
     picked = []
     for j in range(GROUP):
         b = step * GROUP + j
-        hot_s = one_hot(offset_ref[j, 0:1, :], TILE)
-        hot_r = one_hot(offset_ref[j, 1:2, :], TILE)
-        hots.append((hot_s, hot_r))
-        found = dot_nn(table[tile_ref[b, 1]], hot_r)
+        found = dot_nn(table[tile_ref[1, b]], one_hot(offset_ref[j, 1:2, :], TILE))
         picked.append(jnp.where(lane < count_ref[b], found, 0.0))
     upstream = jnp.concatenate(picked, axis=1)
     normed = normed_ref[...]
     weighted = upstream * normed
-    grad_post = norm_back(upstream, normed, inv_ref[...], gain_ref[...]).astype(BF16)
+    grad_post = norm_back(upstream, normed, inv_ref[...], column(gain_ref)).astype(BF16)
     hidden = hidden_ref[...]
-    grad_w2[...] += dot_nt(grad_post, hidden)
-    grad_full = dot_tn(w2_ref[...], grad_post) * slope_ref[...]
+    grad_full = dot_nn(w2_turned[...], grad_post) * slope_ref[...]
     grad_pre = grad_full.astype(BF16)
-    edge_grad_ref[...] = dot_tn(w1_ref[:, :latent], grad_pre).astype(BF16)
-    grad_w1[:, :latent] += dot_nt(grad_pre, edge_ref[...])
-    grad_w1[:, latent:] += dot_nt(grad_pre, pair_ref[...])
+    edge_grad_ref[...] = dot_nn(w1_turned[...], grad_pre).astype(BF16)
+    senders = offset_ref[:, 0, :].T
+    receivers = offset_ref[:, 1, :].T
+    gain_part, shift_part, bias_part = sum_gain[...], sum_shift[...], sum_bias[...]
     for j in range(GROUP):
         b = step * GROUP + j
         cols = slice(j * TILE, (j + 1) * TILE)
-        sum_gain[...] += weighted[:, cols]
-        sum_shift[...] += upstream[:, cols]
-        sum_bias[...] += grad_full[:, cols]
-        hot_s, hot_r = hots[j]
-        total[tile_ref[b, 0], :latent, :] += dot_nt(grad_pre[:, cols], hot_s)
-        total[tile_ref[b, 1], latent:, :] += dot_nt(grad_pre[:, cols], hot_r)
+        gain_part += weighted[:, cols]
+        shift_part += upstream[:, cols]
+        bias_part += grad_full[:, cols]
+        hot = jnp.concatenate(
+            [
+                one_hot_rows(senders[:, j : j + 1], TILE),
+                one_hot_rows(receivers[:, j : j + 1], TILE),
+            ],
+            axis=1,
+        )
+        spread = dot_nn(grad_pre[:, cols], hot)
+        total[tile_ref[0, b], :latent, :] += spread[:, :TILE]
+        total[tile_ref[1, b], latent:, :] += spread[:, TILE:]
+    sum_gain[...], sum_shift[...], sum_bias[...] = gain_part, shift_part, bias_part
+    grad_w2[...] += dot_nt(grad_post, hidden)
+    grad_w1[:, :latent] += dot_nt(grad_pre, edge_ref[...])
+    grad_w1[:, latent:] += dot_nt(grad_pre, pair_ref[...])
 
     @pl.when(step == pl.num_programs(0) - 1)
     def _():
-        for t in range(local_tiles):
-            cols = slice(t * TILE, (t + 1) * TILE)
-            back = dot_tn(w1_ref[:, latent : 2 * latent], total[t, :latent, :].astype(BF16))
-            back += dot_tn(w1_ref[:, 2 * latent :], total[t, latent:, :].astype(BF16))
-            local_ref[:, cols] = base_ref[:, cols] + back
         for c in range(3):
             rows[c * latent : (c + 1) * latent, :] = grad_w1[:, c * latent : (c + 1) * latent]
         rows[3 * latent : 4 * latent, :] = grad_w2[...]
-
-        def body(p, carry):
-            t = local_tiles + p
-            back = dot_tn(w1_ref[:, latent : 2 * latent], total[t, :latent, :].astype(BF16))
-            back += dot_tn(w1_ref[:, 2 * latent :], total[t, latent:, :].astype(BF16))
-            out_ref[p, :TILE, :] = back.astype(BF16)
-            start = pl.multiple_of(p * 16, 16)
-            out_ref[p, TILE : TILE + 16, :] = rows[pl.ds(start, 16), :].astype(BF16)
-            out_ref[p, TILE + 16 :, :] = jnp.zeros((EDGE_ROWS - 16, TILE), BF16)
-            return carry
-
-        lax.fori_loop(0, out_ref.shape[0], body, 0)
+        for t in range(0, table.shape[0], WIDE):
+            group = range(t, t + WIDE)
+            low = jnp.concatenate([total[k].astype(BF16) for k in group], axis=1)
+            back = dot_nn(w1_pair[...], low)
+            for k in group:
+                part = back[:, (k - t) * TILE : (k - t + 1) * TILE]
+                if k < local_tiles:
+                    cols = slice(k * TILE, (k + 1) * TILE)
+                    local_ref[:, cols] = base_ref[:, cols] + part
+                else:
+                    p = k - local_tiles
+                    out_ref[p, :TILE, :] = part.astype(BF16)
+                    out_ref[p, TILE : TILE + 16, :] = rows[p * 16 : p * 16 + 16, :].astype(BF16)
+                    out_ref[p, TILE + 16 :, :] = jnp.zeros((EDGE_ROWS - 16, TILE), BF16)
         tail = jnp.concatenate(
             [
                 row_sum(sum_bias[...]),
@@ -345,8 +351,7 @@
 
 
 def final_kernel(idx_ref, local_ref, mirror_ref, out_ref):
-    out_ref[...] = local_ref[...]
-    scatter_mirrors(out_ref, idx_ref, mirror_ref)
+    out_ref[...] = scatter_mirrors(local_ref[...], idx_ref, mirror_ref)
 
 
 def params_kernel(edge_scale, node_scale, all_ref, out_ref, edge_rows, node_rows):
@@ -374,7 +379,7 @@
 
 VMEM = pl.BlockSpec(memory_space=pltpu.VMEM)
 SMEM = pl.BlockSpec(memory_space=pltpu.SMEM)
-PARAMS = pltpu.CompilerParams(vmem_limit_bytes=48 * 1024 * 1024)
+PARAMS = pltpu.CompilerParams(vmem_limit_bytes=40 * 1024 * 1024)
 
 
 def whole(kernel, out_shape, n_in, scratch, name):
@@ -421,12 +426,21 @@
     def swap(values):
         return lax.all_to_all(values, "cut", split_axis=0, concat_axis=0, tiled=True)
 
-    def column(vector):
-        return vector[:, None]
+    def near(values):
+        return pltpu.with_memory_space_constraint(values, pltpu.VMEM)
+
+    def hbm(values):
+        return pltpu.with_memory_space_constraint(values, pltpu.HBM)
+
+    def sent(dims, dtype):
+        return pltpu.HBM(dims, dtype)
+
+    def row(vector):
+        return hbm(vector[None, :])
 
     idx = swap(route[0][:, None, :])
-    outgoing = whole(gather_kernel, shape((peers, latent, TILE), BF16), 2, [], "gather")(
-        idx, node_feat
+    outgoing = whole(gather_kernel, sent((peers, latent, TILE), BF16), 2, [], "gather")(
+        near(idx), hbm(node_feat)
     )
     mirrors = swap(outgoing)
 
@@ -444,13 +458,13 @@
         edge_fwd_kernel,
         grid=(steps,),
         out_shape=(
-            shape((2 * latent, slots), BF16),
-            shape((latent, slots), BF16),
-            shape((latent, slots), F32),
-            shape((latent, slots), F32),
-            shape((1, slots), F32),
-            shape((latent, masters), F32),
-            shape((peers, latent, TILE), BF16),
+            sent((2 * latent, slots), BF16),
+            sent((latent, slots), BF16),
+            sent((latent, slots), F32),
+            sent((latent, slots), F32),
+            sent((1, slots), F32),
+            sent((latent, masters), F32),
+            sent((peers, latent, TILE), BF16),
         ),
         in_specs=[
             SMEM,
@@ -460,10 +474,10 @@
             full((latent, masters)),
             full((peers, latent, TILE)),
             full((latent, 3 * latent)),
-            full((latent, 1)),
+            full((1, latent)),
             full((latent, latent)),
-            full((latent, 1)),
-            full((latent, 1)),
+            full((1, latent)),
+            full((1, latent)),
         ],
         out_specs=(
             wide(2 * latent),
@@ -482,42 +496,42 @@
         interpret=INTERPRET,
         name="edge_fwd",
     )(
-        block_tile,
-        block_count,
-        block_offset,
-        edge_feat,
-        node_feat,
-        mirrors,
-        w_edge1,
-        column(bias_edge1),
-        w_edge2,
-        column(gain_edge),
-        column(shift_edge),
+        hbm(block_tile.T),
+        hbm(block_count),
+        hbm(block_offset),
+        hbm(edge_feat),
+        hbm(node_feat),
+        near(mirrors),
+        hbm(w_edge1),
+        row(bias_edge1),
+        hbm(w_edge2),
+        row(gain_edge),
+        row(shift_edge),
     )
     returned = swap(returned)
 
     node_out, base, grad_agg, outgoing = whole(
         node_kernel,
         (
-            shape((latent, masters), BF16),
-            shape((latent, masters), F32),
-            shape((latent, masters), BF16),
-            shape((peers, latent + NODE_ROWS, TILE), BF16),
+            sent((latent, masters), BF16),
+            sent((latent, masters), F32),
+            sent((latent, masters), BF16),
+            sent((peers, latent + NODE_ROWS, TILE), BF16),
         ),
         10,
-        [pltpu.VMEM((latent, masters), F32), pltpu.VMEM((peers * NODE_ROWS, TILE), F32)],
+        [pltpu.VMEM((peers * NODE_ROWS, TILE), F32)],
         "node",
     )(
-        idx,
-        local_sum,
-        returned,
-        node_feat,
-        node_cot,
-        w_node1,
-        column(bias_node1),
-        w_node2,
-        column(gain_node),
-        column(shift_node),
+        near(idx),
+        hbm(local_sum),
+        near(returned),
+        hbm(node_feat),
+        hbm(node_cot),
+        hbm(w_node1),
+        row(bias_node1),
+        hbm(w_node2),
+        row(gain_node),
+        row(shift_node),
     )
     mirrors = swap(outgoing)
     node_shard = jnp.sum(mirrors[:, latent:, :].astype(F32), axis=0).astype(BF16)
@@ -526,9 +540,9 @@
         edge_bwd_kernel,
         grid=(steps,),
         out_shape=(
-            shape((latent, slots), BF16),
-            shape((latent, masters), F32),
-            shape((peers, latent + EDGE_ROWS, TILE), BF16),
+            sent((latent, slots), BF16),
+            sent((latent, masters), F32),
+            sent((peers, latent + EDGE_ROWS, TILE), BF16),
         ),
         in_specs=[
             SMEM,
@@ -545,7 +559,7 @@
             full((latent, masters)),
             full((latent, 3 * latent)),
             full((latent, latent)),
-            full((latent, 1)),
+            full((1, latent)),
         ],
         out_specs=(
             wide(latent),
@@ -561,43 +575,46 @@
             pltpu.VMEM((latent, TILE), F32),
             pltpu.VMEM((latent, TILE), F32),
             pltpu.VMEM((4 * latent, TILE), F32),
+            pltpu.VMEM((latent, latent), BF16),
+            pltpu.VMEM((latent, 2 * latent), BF16),
+            pltpu.VMEM((latent, latent), BF16),
         ],
         compiler_params=PARAMS,
         interpret=INTERPRET,
         name="edge_bwd",
     )(
-        block_tile,
-        block_count,
-        block_offset,
-        edge_feat,
-        pair,
-        hidden,
-        slope,
-        normed,
-        inv,
-        grad_agg,
-        mirrors,
-        base,
-        w_edge1,
-        w_edge2,
-        column(gain_edge),
+        hbm(block_tile.T),
+        hbm(block_count),
+        hbm(block_offset),
+        hbm(edge_feat),
+        hbm(pair),
+        hbm(hidden),
+        hbm(slope),
+        hbm(normed),
+        hbm(inv),
+        hbm(grad_agg),
+        near(mirrors),
+        hbm(base),
+        hbm(w_edge1),
+        hbm(w_edge2),
+        row(gain_edge),
     )
     returned = swap(returned)
     edge_shard = jnp.sum(returned[:, latent:, :].astype(F32), axis=0).astype(BF16)
     shard = jnp.concatenate([edge_shard, node_shard], axis=0)
     gathered = swap(jnp.broadcast_to(shard[None], (peers,) + shard.shape))
-    node_grad = whole(final_kernel, shape((latent, masters), F32), 3, [], "final")(
-        idx, local_grad, returned
+    node_grad = whole(final_kernel, sent((latent, masters), F32), 3, [], "final")(
+        near(idx), hbm(local_grad), near(returned)
     )
     param_rows = whole(
         functools.partial(
             params_kernel, 1.0 / math.sqrt(total_edges), 1.0 / math.sqrt(total_nodes)
         ),
-        shape((902, TILE), F32),
+        sent((902, TILE), F32),
         1,
         [pltpu.VMEM((peers * 16, TILE), F32), pltpu.VMEM((peers * NODE_ROWS, TILE), F32)],
         "params",
-    )(gathered)
+    )(near(gathered))
     return (node_out, node_grad, edge_grad, param_rows.reshape(-1))
 
 

time: 232 us -> 208 us (0.90)
  blocking collectives: 57.8 us -> 122 us
  waiting for transfers between devices: 89.1 us -> 41.7 us
  local copies, waits for them, and re-layouts: 20.1 us -> 0.77 us
  Pallas kernels: 45.2 us -> 32.9 us
  starting transfers between devices: 18 us -> 8.96 us
    all_to_all x2 -> x4, blocking collectives: 57.8 us -> 122 us  [swap(): lax.all_to_all(values, 'cut', split_axis=0, concat_axis=0, tiled=True)]
    all_to_all x4 -> x2, waiting for transfers between devices: 89.1 us -> 41.7 us  [swap(): lax.all_to_all(values, 'cut', split_axis=0, concat_axis=0, tiled=True)]
    unnamed x61 -> x0, local copies, waits for them, and re-layouts: 14.8 us -> none
    pallas_call x5, Pallas kernels: 44.3 us -> 32 us  [the longest x1 10.7 us: per_device(): pl.pallas_call(edge_bwd_kernel, grid=(steps,), out_shape=(sent((latent, s...]
    all_to_all x4 -> x2, starting transfers between devices: 18 us -> 8.96 us  [swap(): lax.all_to_all(values, 'cut', split_axis=0, concat_axis=0, tiled=True)]
    broadcast_in_dim x6 -> x0, local copies, waits for them, and re-layouts: 4.51 us -> none  [column(): return vector[:, None]]
  transfers between devices with their start and end apart: 4 -> 2, of which waited for: 4 -> 2; matrix products, arithmetic and copies ran while one was open for 2% -> 0% of each run, Pallas kernels for 3% -> 2%
where the time goes in v2:
time: 208 us; the launch traced here: 207 us
  blocking collectives  122 us (59%)
  waiting for transfers between devices  41.7 us (20%)
  Pallas kernels  32.9 us (16%)
  starting transfers between devices  8.96 us (4%)
    all_to_all x4, blocking collectives, swap(): lax.all_to_all(values, 'cut', split_axis=0, concat_axis=0, tiled=True)  122 us
    all_to_all x2, waiting for transfers between devices, swap(): lax.all_to_all(values, 'cut', split_axis=0, concat_axis=0, tiled=True)  41.7 us
    pallas_call x1, Pallas kernels, per_device(): pl.pallas_call(edge_bwd_kernel, grid=(steps,), out_shape=(sent((latent, s...  10.7 us
    all_to_all x2, starting transfers between devices, swap(): lax.all_to_all(values, 'cut', split_axis=0, concat_axis=0, tiled=True)  8.96 us
    pallas_call x1, Pallas kernels, per_device(): pl.pallas_call(edge_fwd_kernel, grid=(steps,), out_shape=(sent((2 * laten...  8.45 us
    pallas_call x1, Pallas kernels, per_device(): whole(node_kernel, (sent((latent, masters), BF16), sent((latent, masters)...  6.41 us
  transfers between devices with their start and end apart: 2, of which 2 were waited for; matrix products, arithmetic and copies ran while one was open for 0% of the time, Pallas kernels for 2%

profile of v2, /device:TPU:6, one launch (start us, length us, event | category | flops | bytes accessed | tf_op | source)
XLA Modules:
  0.0 207.0 jit_solution(1076790813540697015)
XLA Ops:
  0.6 21.2 %all_to_all.30.idx_ref = s32[32,1,128]{2,1,0:T(1,128)S(1)} all-to-all(s32[32,1,128]{2,1,0:T(1,128)} %bitcast.10), channel_id=1, replica_groups=mesh['dp'=8,'cut'=32] {'cut'}, dimensions={0} | all-to-all | bytes 32768 | tf_op jit(solution)/shard_map/all_to_all | solution.py:427
  21.8 3.2 %gather.1 = bf16[32,128,128]{2,1,0:T(8,128)(2,1)} custom-call(s32[32,1,128]{2,1,0:T(1,128)S(1)} %all_to_all.30.idx_ref, bf16[128,1024]{1,0:T(8,128)(2,1)} %node_ref.3), custom_call_target="tpu_custom_call" | custom-call | tf_op jit(solution)/shard_map/gather/pallas_call | solution.py:442
  25.1 31.5 %all_to_all.31.mirror_ref = bf16[32,128,128]{2,1,0:T(8,128)(2,1)S(1)} all-to-all(bf16[32,128,128]{2,1,0:T(8,128)(2,1)} %gather.1), channel_id=1, replica_groups=mesh['dp'=8,'cut'=32] {'cut'}, dimensions={0} | all-to-all | bytes 2097152 | tf_op jit(solution)/shard_map/all_to_all | solution.py:427
  56.6 8.5 %edge_fwd.1 = (bf16[256,4096]{1,0:T(8,128)(2,1)}, bf16[128,4096]{1,0:T(8,128)(2,1)}, f32[128,4096]{1,0:T(8,128)}, f32[128,4096]{1,0:T(8,128)}, f32[1,4096]{1,0:T...) custom-call(s32[2,32]{1,0:T(2,128)} %bitcast.11, s32[32]{0:T(128)} %count_ref.3, s32[32,2,128]{2,1,0:T(2,128)} %offset_ref.3, ...), custom_call_target="tpu_custom_call" | custom-call | tf_op jit(solution)/shard_map/edge_fwd/pallas_call | solution.py:457
  65.0 32.6 %all_to_all.32.mirror_ref = bf16[32,128,128]{2,1,0:T(8,128)(2,1)S(1)} all-to-all(bf16[32,128,128]{2,1,0:T(8,128)(2,1)} %get-tuple-element.19), channel_id=1, replica_groups=mesh['dp'=8,'cut'=32] {'cut'}, dimensions={0} | all-to-all | bytes 2097152 | tf_op jit(solution)/shard_map/all_to_all | solution.py:427
  97.7 6.4 %node.1 = (bf16[128,1024]{1,0:T(8,128)(2,1)}, f32[128,1024]{1,0:T(8,128)}, bf16[128,1024]{1,0:T(8,128)(2,1)}, bf16[32,144,128]{2,1,0:T(8,128)(2,1)}) custom-call(s32[32,1,128]{2,1,0:T(1,128)S(1)} %all_to_all.30.idx_ref, f32[128,1024]{1,0:T(8,128)} %get-tuple-element.18.local_ref, bf16[32,128,128]{2,1,0:T(8,128)(2,1)S(1)} %all_to_all.32.mirror_ref, ...), custom_call_target="tpu_custom_call" | custom-call | tf_op jit(solution)/shard_map/node/pallas_call | solution.py:513
  104.1 36.6 %all_to_all.33.mirror_ref = bf16[32,144,128]{2,1,0:T(8,128)(2,1)S(1)} all-to-all(bf16[32,144,128]{2,1,0:T(8,128)(2,1)} %get-tuple-element.27), channel_id=1, replica_groups=mesh['dp'=8,'cut'=32] {'cut'}, dimensions={0} | all-to-all | bytes 2359296 | tf_op jit(solution)/shard_map/all_to_all | solution.py:427
  140.7 10.7 %edge_bwd.1 = (bf16[128,4096]{1,0:T(8,128)(2,1)}, f32[128,1024]{1,0:T(8,128)}, bf16[32,152,128]{2,1,0:T(8,128)(2,1)}) custom-call(s32[2,32]{1,0:T(2,128)} %bitcast.12, s32[32]{0:T(128)} %count_ref.3, s32[32,2,128]{2,1,0:T(2,128)} %offset_ref.3, bf16[128,4096]{1,0:T(8,128)(2,1)} %edge_ref.3, bf16[256,4096]{1,0:T(8,128)(2,1)} %get-tuple-element.21.pair_ref, ...), custom_call_target="tpu_custom_call" | custom-call | tf_op jit(solution)/shard_map/edge_bwd/pallas_call | solution.py:539
  151.4 4.0 %all-to-all-start.4 = ((bf16[32,152,128]{2,1,0:T(8,128)(2,1)}), bf16[32,152,128]{2,1,0:T(8,128)(2,1)S(1)}, u32[]{:S(2)}, u32[]{:S(2)}) async-start(bf16[32,152,128]{2,1,0:T(8,128)(2,1)} %get-tuple-element.30), calls=%async_computation.4 | async-start | bytes 2490368 | tf_op jit(solution)/shard_map/all_to_all | solution.py:427
  155.4 32.1 %all-to-all-done.4.mirror_ref = bf16[32,152,128]{2,1,0:T(8,128)(2,1)S(1)} async-done(((bf16[32,152,128]{2,1,0:T(8,128)(2,1)}), bf16[32,152,128]{2,1,0:T(8,128)(2,1)S(1)}, u32[]{:S(2)}, u32[]{:S(2)}) %all-to-all-start.4) | async-done | bytes 1245216 | tf_op jit(solution)/shard_map/all_to_all | solution.py:427
  187.5 0.8 broadcast_in_dim.31
  188.3 5.0 %all-to-all-start.5 = ((bf16[32,40,128]{2,1,0:T(8,128)(2,1)}), bf16[32,40,128]{2,1,0:T(8,128)(2,1)S(1)}, u32[]{:S(2)}, u32[]{:S(2)}) async-start(bf16[32,40,128]{2,1,0:T(8,128)(2,1)} %broadcast_in_dim.31), calls=%async_computation.5 | async-start | bytes 655360 | tf_op jit(solution)/shard_map/all_to_all | solution.py:427
  193.3 3.3 %final.1 = f32[128,1024]{1,0:T(8,128)} custom-call(s32[32,1,128]{2,1,0:T(1,128)S(1)} %all_to_all.30.idx_ref, f32[128,1024]{1,0:T(8,128)} %get-tuple-element.29.local_ref, bf16[32,152,128]{2,1,0:T(8,128)(2,1)S(1)} %all-to-all-done.4.mirror_ref), custom_call_target="tpu_custom_call" | custom-call | tf_op jit(solution)/shard_map/final/pallas_call | solution.py:606
  196.6 9.6 %all-to-all-done.5.all_ref = bf16[32,40,128]{2,1,0:T(8,128)(2,1)S(1)} async-done(((bf16[32,40,128]{2,1,0:T(8,128)(2,1)}), bf16[32,40,128]{2,1,0:T(8,128)(2,1)S(1)}, u32[]{:S(2)}, u32[]{:S(2)}) %all-to-all-start.5) | async-done | bytes 327712 | tf_op jit(solution)/shard_map/all_to_all | solution.py:427
  206.2 0.8 params.1
  (3 shorter events, 0.1 us)
Async XLA Ops:
  151.4 36.1 %all-to-all-start.4 = ((bf16[32,152,128]{2,1,0:T(8,128)(2,1)}), bf16[32,152,128]{2,1,0:T(8,128)(2,1)S(1)}, u32[]{:S(2)}, u32[]{:S(2)}) async-start(bf16[32,152,128]{2,1,0:T(8,128)(2,1)} %get-tuple-element.30), calls=%async_computation.4 | async-start | bytes 2490368 | tf_op jit(solution)/shard_map/all_to_all | solution.py:427
  188.3 17.9 %all-to-all-start.5 = ((bf16[32,40,128]{2,1,0:T(8,128)(2,1)}), bf16[32,40,128]{2,1,0:T(8,128)(2,1)S(1)}, u32[]{:S(2)}, u32[]{:S(2)}) async-start(bf16[32,40,128]{2,1,0:T(8,128)(2,1)} %broadcast_in_dim.31), calls=%async_computation.5 | async-start | bytes 655360 | tf_op jit(solution)/shard_map/all_to_all | solution.py:427

commit v3 on v2

v3 whole, which is shorter than its diff:
```python
import functools
import math

import jax
import jax.numpy as jnp
from jax import lax
from jax.experimental import pallas as pl
from jax.experimental.pallas import tpu as pltpu
from jax.sharding import PartitionSpec as P

F32 = jnp.float32
BF16 = jnp.bfloat16
TILE = 128
GROUP = 16
WIDE = 4
QUARTER = 232
INTERPRET = False


def dot_nn(left, right):
    return lax.dot_general(left, right, (((1,), (0,)), ((), ())), preferred_element_type=F32)


def dot_nt(left, right):
    return lax.dot_general(left, right, (((1,), (1,)), ((), ())), preferred_element_type=F32)


def dot_tn(left, right):
    return lax.dot_general(left, right, (((0,), (0,)), ((), ())), preferred_element_type=F32)


def one_hot(index_row, depth):
    rows = lax.broadcasted_iota(jnp.int32, (depth, index_row.shape[1]), 0)
    return jnp.where(rows == index_row, 1.0, 0.0).astype(BF16)


def sigmoid(values):
    return 1.0 / (1.0 + jnp.exp(-values))


def one_hot_rows(index_columns, depth):
    lanes = lax.broadcasted_iota(jnp.int32, (index_columns.shape[0], depth), 1)
    return jnp.where(lanes == index_columns, 1.0, 0.0).astype(BF16)


def column(row_ref):
    return jnp.broadcast_to(row_ref[...], (8, row_ref.shape[1])).T[:, :1]


def layer_norm(values):
    centred = values - jnp.mean(values, axis=0, keepdims=True)
    inverse = lax.rsqrt(jnp.mean(centred * centred, axis=0, keepdims=True) + 1e-05)
    return centred * inverse, inverse


def norm_back(upstream, normed, inverse, gain):
    scaled = upstream * gain
    return inverse * (
        scaled
        - jnp.mean(scaled, axis=0, keepdims=True)
        - normed * jnp.mean(scaled * normed, axis=0, keepdims=True)
    )


def gather_peers(idx_ref, table, store):
    depth = table.shape[1]
    for q in range(0, idx_ref.shape[0], WIDE):
        index_row = jnp.concatenate([idx_ref[q + k] for k in range(WIDE)], axis=1)
        picked = dot_nn(table, one_hot(index_row, depth)).astype(BF16)
        for k in range(WIDE):
            store(q + k, picked[:, k * TILE : (k + 1) * TILE])


def gather_kernel(idx_ref, table_ref, out_ref):
    def store(p, values):
        out_ref[p] = values

    gather_peers(idx_ref, table_ref[...], store)


def fill_table(table, local_ref, mirror_ref):
    local_tiles = local_ref.shape[1] // TILE
    for t in range(local_tiles):
        table[t] = local_ref[:, t * TILE : (t + 1) * TILE]

    def body(p, carry):
        table[local_tiles + p] = mirror_ref[p, :TILE, :]
        return carry

    lax.fori_loop(0, mirror_ref.shape[0], body, 0)


def edge_network(step, tile_ref, offset_ref, edge_ref, table, w1_ref, b1_ref, w2_ref):
    latent = edge_ref.shape[0]
    pairs = []
    for j in range(GROUP):
        b = step * GROUP + j
        both = jnp.concatenate([offset_ref[j, 0:1, :], offset_ref[j, 1:2, :] + TILE], axis=1)
        tiles = jnp.concatenate([table[tile_ref[0, b]], table[tile_ref[1, b]]], axis=1)
        found = dot_nn(tiles, one_hot(both, 2 * TILE)).astype(BF16)
        pairs.append(jnp.concatenate([found[:, :TILE], found[:, TILE:]], axis=0))
    pair = jnp.concatenate(pairs, axis=1)
    pre = (
        dot_nn(w1_ref[:, :latent], edge_ref[...])
        + dot_nn(w1_ref[:, latent:], pair)
        + column(b1_ref)
    )
    gate = sigmoid(pre)
    hidden = (pre * gate).astype(BF16)
    normed, inverse = layer_norm(dot_nn(w2_ref[...], hidden))
    return pair, pre, gate, hidden, normed, inverse


def edge_fwd_kernel(
    tile_ref,
    count_ref,
    offset_ref,
    edge_ref,
    node_ref,
    mirror_ref,
    w1_ref,
    b1_ref,
    w2_ref,
    gain_ref,
    shift_ref,
    local_ref,
    out_ref,
    table,
    total,
):
    step = pl.program_id(0)
    latent = edge_ref.shape[0]
    local_tiles = node_ref.shape[1] // TILE

    @pl.when(step == 0)
    def _():
        fill_table(table, node_ref, mirror_ref)
        total[...] = jnp.zeros_like(total)

    normed = edge_network(step, tile_ref, offset_ref, edge_ref, table, w1_ref, b1_ref, w2_ref)[4]
    message = column(gain_ref) * normed + column(shift_ref)
    turned = offset_ref[:, 1, :].T
    lane = lax.broadcasted_iota(jnp.int32, (latent, TILE), 1)
    spread = []
    for j in range(GROUP):
        values = message[:, j * TILE : (j + 1) * TILE]
        kept = jnp.where(lane < count_ref[step * GROUP + j], values, 0.0).astype(BF16)
        spread.append(dot_nn(kept, one_hot_rows(turned[:, j : j + 1], TILE)))
    for j in range(GROUP):
        total[tile_ref[1, step * GROUP + j]] += spread[j]

    @pl.when(step == pl.num_programs(0) - 1)
    def _():
        for t in range(local_tiles):
            local_ref[:, t * TILE : (t + 1) * TILE] = total[t]

        def body(p, carry):
            out_ref[p] = total[local_tiles + p].astype(BF16)
            return carry

        lax.fori_loop(0, out_ref.shape[0], body, 0)


def edge_keep_kernel(
    tile_ref,
    offset_ref,
    edge_ref,
    node_ref,
    mirror_ref,
    w1_ref,
    b1_ref,
    w2_ref,
    pair_ref,
    hidden_ref,
    slope_ref,
    normed_ref,
    inv_ref,
    table,
):
    step = pl.program_id(0)

    @pl.when(step == 0)
    def _():
        fill_table(table, node_ref, mirror_ref)

    pair, pre, gate, hidden, normed, inverse = edge_network(
        step, tile_ref, offset_ref, edge_ref, table, w1_ref, b1_ref, w2_ref
    )
    pair_ref[...] = pair
    hidden_ref[...] = hidden
    slope_ref[...] = gate * (1.0 + pre * (1.0 - gate))
    normed_ref[...] = normed
    inv_ref[...] = inverse


def scatter_mirrors(total, idx_ref, mirror_ref):
    depth = total.shape[1]
    peers = idx_ref.shape[0]
    turned = jnp.concatenate([idx_ref[p] for p in range(peers)], axis=0).T
    for q in range(0, peers, WIDE):
        hot = jnp.concatenate(
            [one_hot_rows(turned[:, p : p + 1], depth) for p in range(q, q + WIDE)], axis=0
        )
        values = jnp.concatenate([mirror_ref[p, :TILE, :] for p in range(q, q + WIDE)], axis=1)
        total += dot_nn(values, hot)
    return total


def row_sum(values):
    folded = values[:, :TILE]
    for start in range(TILE, values.shape[1], TILE):
        folded = folded + values[:, start : start + TILE]
    return jnp.sum(folded.T, axis=0, keepdims=True)


def node_network(node_low, agg_low, cot_ref, w1_ref, b1_ref, w2_ref, gain):
    latent = node_low.shape[0]
    pre = dot_nn(w1_ref[:, :latent], node_low) + dot_nn(w1_ref[:, latent:], agg_low) + column(b1_ref)
    gate = sigmoid(pre)
    hidden = (pre * gate).astype(BF16)
    normed, inverse = layer_norm(dot_nn(w2_ref[...], hidden))
    upstream = cot_ref[...].astype(F32)
    grad_post = norm_back(upstream, normed, inverse, gain).astype(BF16)
    grad_full = dot_tn(w2_ref[...], grad_post) * (gate * (1.0 + pre * (1.0 - gate)))
    return hidden, normed, upstream, grad_post, grad_full


def node_kernel(
    idx_ref,
    local_ref,
    mirror_ref,
    node_ref,
    cot_ref,
    w1_ref,
    b1_ref,
    w2_ref,
    gain_ref,
    agg_low_ref,
    grad_agg_ref,
    out_ref,
):
    latent = node_ref.shape[0]
    agg_low = scatter_mirrors(local_ref[...], idx_ref, mirror_ref).astype(BF16)
    agg_low_ref[...] = agg_low
    grad_full = node_network(
        node_ref[...], agg_low, cot_ref, w1_ref, b1_ref, w2_ref, column(gain_ref)
    )[4]
    grad_agg = dot_tn(w1_ref[:, latent:], grad_full.astype(BF16)).astype(BF16)
    grad_agg_ref[...] = grad_agg

    def store(p, values):
        out_ref[p] = values

    gather_peers(idx_ref, grad_agg, store)


def node_rest_kernel(
    agg_low_ref,
    node_ref,
    cot_ref,
    w1_ref,
    b1_ref,
    w2_ref,
    gain_ref,
    shift_ref,
    node_out_ref,
    base_ref,
    rows,
):
    latent = node_ref.shape[0]
    node_low, agg_low, gain = node_ref[...], agg_low_ref[...], column(gain_ref)
    hidden, normed, upstream, grad_post, grad_full = node_network(
        node_low, agg_low, cot_ref, w1_ref, b1_ref, w2_ref, gain
    )
    grad_pre = grad_full.astype(BF16)
    node_out_ref[...] = (node_low.astype(F32) + gain * normed + column(shift_ref)).astype(BF16)
    base_ref[...] = upstream + dot_tn(w1_ref[:, :latent], grad_pre)
    rows[0:latent, :] = dot_nt(grad_pre, node_low)
    rows[latent : 2 * latent, :] = dot_nt(grad_pre, agg_low)
    rows[2 * latent : 3 * latent, :] = dot_nt(grad_post, hidden)
    sums = [row_sum(grad_full), row_sum(upstream * normed), row_sum(upstream)]
    rows[3 * latent :, :] = jnp.concatenate(sums + [jnp.zeros((5, TILE), F32)], axis=0)


def edge_bwd_kernel(
    tile_ref,
    count_ref,
    offset_ref,
    slope_ref,
    normed_ref,
    inv_ref,
    agg_ref,
    mirror_ref,
    base_ref,
    w1_ref,
    w2_ref,
    gain_ref,
    post_ref,
    pre_ref,
    local_ref,
    out_ref,
    sums_ref,
    table,
    total,
    sums,
    w1_pair,
    w2_turned,
):
    step = pl.program_id(0)
    latent = slope_ref.shape[0]
    local_tiles = agg_ref.shape[1] // TILE

    @pl.when(step == 0)
    def _():
        fill_table(table, agg_ref, mirror_ref)
        total[...] = jnp.zeros_like(total)
        sums[...] = jnp.zeros_like(sums)
        w2_turned[...] = w2_ref[...].T
        w1_pair[:, :latent] = w1_ref[:, latent : 2 * latent].T
        w1_pair[:, latent:] = w1_ref[:, 2 * latent :].T

    lane = lax.broadcasted_iota(jnp.int32, (latent, TILE), 1)
    gain = column(gain_ref)
    senders = offset_ref[:, 0, :].T
    receivers = offset_ref[:, 1, :].T
    bias_part, gain_part, shift_part = sums[0], sums[1], sums[2]
    picked = []
    for j in range(GROUP):
        b = step * GROUP + j
        found = dot_nn(table[tile_ref[1, b]], one_hot(offset_ref[j, 1:2, :], TILE))
        picked.append(jnp.where(lane < count_ref[b], found, 0.0))
    upstream = jnp.concatenate(picked, axis=1)
    normed = normed_ref[...]
    weighted = upstream * normed
    grad_post = norm_back(upstream, normed, inv_ref[...], gain).astype(BF16)
    post_ref[...] = grad_post
    grad_full = dot_nn(w2_turned[...], grad_post) * slope_ref[...]
    grad_pre = grad_full.astype(BF16)
    pre_ref[...] = grad_pre
    spread = []
    for j in range(GROUP):
        cols = slice(j * TILE, (j + 1) * TILE)
        bias_part += grad_full[:, cols]
        gain_part += weighted[:, cols]
        shift_part += upstream[:, cols]
        hot = jnp.concatenate(
            [
                one_hot_rows(senders[:, j : j + 1], TILE),
                one_hot_rows(receivers[:, j : j + 1], TILE),
            ],
            axis=1,
        )
        spread.append(dot_nn(grad_pre[:, cols], hot))
    for j in range(GROUP):
        b = step * GROUP + j
        total[tile_ref[0, b], :latent, :] += spread[j][:, :TILE]
        total[tile_ref[1, b], latent:, :] += spread[j][:, TILE:]
    sums[0], sums[1], sums[2] = bias_part, gain_part, shift_part

    @pl.when(step == pl.num_programs(0) - 1)
    def _():
        sums_ref[...] = sums[...]
        for t in range(0, table.shape[0], WIDE):
            group = range(t, t + WIDE)
            low = jnp.concatenate([total[k].astype(BF16) for k in group], axis=1)
            back = dot_nn(w1_pair[...], low)
            for k in group:
                part = back[:, (k - t) * TILE : (k - t + 1) * TILE]
                if k < local_tiles:
                    cols = slice(k * TILE, (k + 1) * TILE)
                    local_ref[:, cols] = base_ref[:, cols] + part
                else:
                    out_ref[k - local_tiles] = part.astype(BF16)


def edge_weights_kernel(
    edge_ref,
    pair_ref,
    hidden_ref,
    post_ref,
    pre_ref,
    w1_ref,
    sums_ref,
    node_rows_ref,
    edge_grad_ref,
    rows_ref,
    grad_w1,
    grad_w2,
    w1_turned,
):
    step = pl.program_id(0)
    latent = edge_ref.shape[0]

    @pl.when(step == 0)
    def _():
        grad_w1[...] = jnp.zeros_like(grad_w1)
        grad_w2[...] = jnp.zeros_like(grad_w2)
        w1_turned[...] = w1_ref[:, :latent].T

    grad_pre = pre_ref[...]
    edge_grad_ref[...] = dot_nn(w1_turned[...], grad_pre).astype(BF16)
    grad_w2[...] += dot_nt(post_ref[...], hidden_ref[...])
    grad_w1[:latent] += dot_nt(edge_ref[...], grad_pre)
    grad_w1[latent:] += dot_nt(pair_ref[...], grad_pre)

    @pl.when(step == pl.num_programs(0) - 1)
    def _():
        n = latent
        for c in range(3):
            rows_ref[c * n : (c + 1) * n, :] = grad_w1[c * n : (c + 1) * n, :].T.astype(BF16)
        rows_ref[3 * n : 4 * n, :] = grad_w2[...].astype(BF16)
        rows_ref[4 * n : 7 * n, :] = node_rows_ref[: 3 * n, :].astype(BF16)
        tail = [row_sum(sums_ref[k]) for k in range(3)]
        tail += [node_rows_ref[3 * n : 3 * n + 3, :], jnp.zeros((26, TILE), F32)]
        rows_ref[7 * n :, :] = jnp.concatenate(tail, axis=0).astype(BF16)


def final_kernel(idx_ref, local_ref, mirror_ref, out_ref):
    out_ref[...] = scatter_mirrors(local_ref[...], idx_ref, mirror_ref)


def params_kernel(edge_scale, node_scale, place_ref, quarters_ref, out_ref, flat):
    for q in range(4):
        rows = quarters_ref[(place_ref[0] - q) & 3]
        flat[q * QUARTER : (q + 1) * QUARTER, :] = rows.astype(F32)
    n = TILE
    tail = flat[7 * n : 7 * n + 8, :]
    for c in range(3):
        out_ref[pl.ds(c, n, stride=3), :] = flat[c * n : (c + 1) * n, :] * edge_scale
    out_ref[3 * n : 3 * n + 1, :] = tail[0:1] * edge_scale
    out_ref[3 * n + 1 : 4 * n + 1, :] = flat[3 * n : 4 * n, :] * edge_scale
    out_ref[4 * n + 1 : 4 * n + 3, :] = tail[1:3] * edge_scale
    at = 4 * n + 3
    for c in range(2):
        rows = flat[(4 + c) * n : (5 + c) * n, :]
        out_ref[pl.ds(at + c, n, stride=2), :] = rows * node_scale
    at += 2 * n
    out_ref[at : at + 1, :] = tail[3:4] * node_scale
    out_ref[at + 1 : at + 1 + n, :] = flat[6 * n : 7 * n, :] * node_scale
    out_ref[at + 1 + n : at + 3 + n, :] = tail[4:6] * node_scale


def sum_over_cut(rows, other_work):
    fast = lax.axis_size("cut") // 4
    place = lax.axis_index("cut") // fast
    every = range(4 * fast)

    def ahead(values, k):
        return lax.ppermute(values, "cut", [(i, (i + k * fast) % (4 * fast)) for i in every])

    def across(values, bits):
        return lax.ppermute(values, "cut", [(i, i ^ bits) for i in every])

    def quarter(k):
        return lax.dynamic_index_in_dim(rows, (place + k) % 4, 0, keepdims=False)

    def add(left, right):
        return left.astype(F32) + right.astype(F32)

    first, second, third = [ahead(quarter(k), k) for k in range(1, 4)]
    mine = (add(quarter(0), first) + add(second, third)).astype(BF16)
    terms = [mine] + [across(mine, bits) for bits in range(1, fast)]
    while len(terms) > 1:
        terms = [add(terms[k], terms[k + 1]) for k in range(0, len(terms), 2)]
    mine = terms[0].astype(BF16)
    quarters = [mine] + [ahead(mine, k) for k in range(1, 4)]
    quarters, other_work = lax.optimization_barrier((quarters, other_work))
    return jnp.stack(quarters), place, other_work


VMEM = pl.BlockSpec(memory_space=pltpu.VMEM)
SMEM = pl.BlockSpec(memory_space=pltpu.SMEM)
PARAMS = pltpu.CompilerParams(vmem_limit_bytes=40 * 1024 * 1024)


def whole(kernel, out_shape, n_in, scratch, name, cost=None):
    return pl.pallas_call(
        kernel,
        out_shape=out_shape,
        in_specs=[VMEM] * n_in,
        out_specs=jax.tree.map(lambda _: VMEM, out_shape),
        scratch_shapes=scratch,
        compiler_params=PARAMS,
        interpret=INTERPRET,
        cost_estimate=cost,
        name=name,
    )


def per_device(
    node_feat,
    edge_feat,
    route,
    block_tile,
    block_offset,
    block_count,
    w_edge1,
    bias_edge1,
    w_edge2,
    gain_edge,
    shift_edge,
    w_node1,
    bias_node1,
    w_node2,
    gain_node,
    shift_node,
    node_cot,
):
    latent, masters = node_feat.shape
    slots = edge_feat.shape[1]
    blocks = block_tile.shape[0]
    peers = route.shape[1]
    total_nodes = masters * peers
    total_edges = slots * peers
    tiles = masters // TILE + peers
    shape = jax.ShapeDtypeStruct

    def swap(values):
        return lax.all_to_all(values, "cut", split_axis=0, concat_axis=0, tiled=True)

    def near(values):
        return pltpu.with_memory_space_constraint(values, pltpu.VMEM)

    def hbm(values):
        return pltpu.with_memory_space_constraint(values, pltpu.HBM)

    def sent(dims, dtype):
        return pltpu.HBM(dims, dtype)

    def row(vector):
        return hbm(vector[None, :])

    idx = swap(route[0][:, None, :])
    outgoing = whole(gather_kernel, sent((peers, latent, TILE), BF16), 2, [], "gather")(
        near(idx), hbm(node_feat)
    )
    mirrors = swap(outgoing)

    steps = blocks // GROUP
    width = GROUP * TILE

    def full(dims):
        return pl.BlockSpec(dims, lambda i: (0,) * len(dims))

    def wide(height):
        return pl.BlockSpec((height, width), lambda i: (0, i))

    offsets = pl.BlockSpec((GROUP, 2, TILE), lambda i: (i, 0, 0))
    table = pltpu.VMEM((tiles, latent, TILE), BF16)
    local_sum, sent_back = pl.pallas_call(
        edge_fwd_kernel,
        grid=(steps,),
        out_shape=(sent((latent, masters), F32), sent((peers, latent, TILE), BF16)),
        in_specs=[
            SMEM,
            SMEM,
            offsets,
            wide(latent),
            full((latent, masters)),
            full((peers, latent, TILE)),
            full((latent, 3 * latent)),
            full((1, latent)),
            full((latent, latent)),
            full((1, latent)),
            full((1, latent)),
        ],
        out_specs=(full((latent, masters)), full((peers, latent, TILE))),
        scratch_shapes=[table, pltpu.VMEM((tiles, latent, TILE), F32)],
        compiler_params=PARAMS,
        interpret=INTERPRET,
        name="edge_fwd",
    )(
        hbm(block_tile.T),
        hbm(block_count),
        hbm(block_offset),
        hbm(edge_feat),
        hbm(node_feat),
        near(mirrors),
        hbm(w_edge1),
        row(bias_edge1),
        hbm(w_edge2),
        row(gain_edge),
        row(shift_edge),
    )
    returned = swap(sent_back)
    again, _ = lax.optimization_barrier((mirrors, local_sum))
    pair, hidden, slope, normed, inv = pl.pallas_call(
        edge_keep_kernel,
        grid=(steps,),
        out_shape=(
            sent((2 * latent, slots), BF16),
            sent((latent, slots), BF16),
            sent((latent, slots), F32),
            sent((latent, slots), F32),
            sent((1, slots), F32),
        ),
        in_specs=[
            SMEM,
            offsets,
            wide(latent),
            full((latent, masters)),
            full((peers, latent, TILE)),
            full((latent, 3 * latent)),
            full((1, latent)),
            full((latent, latent)),
        ],
        out_specs=(wide(2 * latent), wide(latent), wide(latent), wide(latent), wide(1)),
        scratch_shapes=[table],
        compiler_params=PARAMS,
        interpret=INTERPRET,
        cost_estimate=pl.CostEstimate(
            flops=12 * latent * latent * slots,
            bytes_accessed=16 * latent * slots,
            transcendentals=latent * slots,
        ),
        name="edge_keep",
    )(
        hbm(block_tile.T),
        hbm(block_offset),
        hbm(edge_feat),
        hbm(node_feat),
        near(again),
        hbm(w_edge1),
        row(bias_edge1),
        hbm(w_edge2),
    )

    agg_low, grad_agg, outgoing = whole(
        node_kernel,
        (
            sent((latent, masters), BF16),
            sent((latent, masters), BF16),
            sent((peers, latent, TILE), BF16),
        ),
        9,
        [],
        "node",
    )(
        near(idx),
        hbm(local_sum),
        near(returned),
        hbm(node_feat),
        hbm(node_cot),
        hbm(w_node1),
        row(bias_node1),
        hbm(w_node2),
        row(gain_node),
    )
    mirrors = swap(outgoing)
    node_out, base, node_rows = whole(
        node_rest_kernel,
        (
            sent((latent, masters), BF16),
            sent((latent, masters), F32),
            sent((3 * latent + 8, TILE), F32),
        ),
        8,
        [],
        "node_rest",
        pl.CostEstimate(
            flops=22 * latent * latent * masters,
            bytes_accessed=20 * latent * masters,
            transcendentals=latent * masters,
        ),
    )(
        hbm(agg_low),
        hbm(node_feat),
        hbm(node_cot),
        hbm(w_node1),
        row(bias_node1),
        hbm(w_node2),
        row(gain_node),
        row(shift_node),
    )

    mirrors = swap(outgoing)

    grad_post, grad_pre, local_grad, returned, sums = pl.pallas_call(
        edge_bwd_kernel,
        grid=(steps,),
        out_shape=(
            sent((latent, slots), BF16),
            sent((latent, slots), BF16),
            sent((latent, masters), F32),
            sent((peers, latent, TILE), BF16),
            sent((3, latent, TILE), F32),
        ),
        in_specs=[
            SMEM,
            SMEM,
            offsets,
            wide(latent),
            wide(latent),
            wide(1),
            full((latent, masters)),
            full((peers, latent, TILE)),
            full((latent, masters)),
            full((latent, 3 * latent)),
            full((latent, latent)),
            full((1, latent)),
        ],
        out_specs=(
            wide(latent),
            wide(latent),
            full((latent, masters)),
            full((peers, latent, TILE)),
            full((3, latent, TILE)),
        ),
        scratch_shapes=[
            pltpu.VMEM((tiles, latent, TILE), BF16),
            pltpu.VMEM((tiles, 2 * latent, TILE), F32),
            pltpu.VMEM((3, latent, TILE), F32),
            pltpu.VMEM((latent, 2 * latent), BF16),
            pltpu.VMEM((latent, latent), BF16),
        ],
        compiler_params=PARAMS,
        interpret=INTERPRET,
        name="edge_bwd",
    )(
        hbm(block_tile.T),
        hbm(block_count),
        hbm(block_offset),
        hbm(slope),
        hbm(normed),
        hbm(inv),
        hbm(grad_agg),
        near(mirrors),
        hbm(base),
        hbm(w_edge1),
        hbm(w_edge2),
        row(gain_edge),
    )
    returned = swap(returned)
    edge_grad, rows = pl.pallas_call(
        edge_weights_kernel,
        grid=(steps,),
        out_shape=(sent((latent, slots), BF16), sent((4 * QUARTER, TILE), BF16)),
        in_specs=[
            wide(latent),
            wide(2 * latent),
            wide(latent),
            wide(latent),
            wide(latent),
            full((latent, 3 * latent)),
            full((3, latent, TILE)),
            full((3 * latent + 8, TILE)),
        ],
        out_specs=(wide(latent), full((4 * QUARTER, TILE))),
        scratch_shapes=[
            pltpu.VMEM((3 * latent, latent), F32),
            pltpu.VMEM((latent, latent), F32),
            pltpu.VMEM((latent, latent), BF16),
        ],
        compiler_params=PARAMS,
        interpret=INTERPRET,
        cost_estimate=pl.CostEstimate(
            flops=10 * latent * latent * slots, bytes_accessed=14 * latent * slots, transcendentals=0
        ),
        name="edge_weights",
    )(
        hbm(edge_feat),
        hbm(pair),
        hbm(hidden),
        hbm(grad_post),
        hbm(grad_pre),
        hbm(w_edge1),
        hbm(sums),
        hbm(node_rows),
    )
    node_grad = whole(final_kernel, sent((latent, masters), F32), 3, [], "final")(
        near(idx), hbm(local_grad), near(returned)
    )
    quarters, place, node_grad = sum_over_cut(rows.reshape(4, QUARTER, TILE), node_grad)
    param_rows = pl.pallas_call(
        functools.partial(
            params_kernel, 1.0 / math.sqrt(total_edges), 1.0 / math.sqrt(total_nodes)
        ),
        out_shape=sent((902, TILE), F32),
        in_specs=[SMEM, VMEM],
        out_specs=VMEM,
        scratch_shapes=[pltpu.VMEM((4 * QUARTER, TILE), F32)],
        compiler_params=PARAMS,
        interpret=INTERPRET,
        name="params",
    )(place.reshape(1), quarters)
    return (node_out, node_grad, edge_grad, param_rows.reshape(-1))


def solution(mesh):
    nodes = P(None, ("dp", "cut"))
    rows = P(("dp", "cut"))
    in_specs = (nodes, nodes, rows, rows, rows, rows) + (P(),) * 10 + (nodes,)
    out_specs = (nodes, nodes, nodes, P("dp"))
    return jax.shard_map(
        per_device, mesh=mesh, in_specs=in_specs, out_specs=out_specs, check_vma=False
    )
```

time: 208 us -> 197 us (0.947)
  blocking collectives: 122 us -> 85.3 us
  starting transfers between devices: 8.96 us -> 38.4 us
  waiting for transfers between devices: 41.7 us -> 28.5 us
  Pallas kernels: 32.9 us -> 41.3 us
    all_to_all x4 -> x3, blocking collectives: 122 us -> 85.3 us  [swap(): lax.all_to_all(values, 'cut', split_axis=0, concat_axis=0, tiled=True)]
    ppermute x0 -> x13, starting transfers between devices: none -> 28.3 us  [the longest x7 16.7 us: across(): return lax.ppermute(values, 'cut', [(i, i ^ bits) for i in every])]
    all_to_all x2, waiting for transfers between devices: 41.7 us -> 18.7 us  [swap(): lax.all_to_all(values, 'cut', split_axis=0, concat_axis=0, tiled=True)]
    pallas_call x2 -> x5, Pallas kernels: 9.27 us -> 20.8 us  [the longest x1 5.95 us: per_device(): pl.pallas_call(edge_fwd_kernel, grid=(steps,), out_shape=(sent((latent, m...]
    ppermute x0 -> x13, waiting for transfers between devices: none -> 9.76 us  [the longest x6 6.35 us: ahead(): lax.ppermute(values, 'cut', [(i, (i + k * fast) % (4 * fast)) for i in ev...]
    pallas_call x1, Pallas kernels: 10.7 us -> 7.97 us  [per_device(): pl.pallas_call(edge_bwd_kernel, grid=(steps,), out_shape=(sent((latent, s...]
  transfers between devices with their start and end apart: 2 -> 15, of which waited for: 2 -> 8; matrix products, arithmetic and copies ran while one was open for 0% -> 1% of each run, Pallas kernels for 2% -> 9%
where the time goes in v3:
time: 197 us; the launch traced here: 196 us
  blocking collectives  85.3 us (43%)
  Pallas kernels  41.3 us (21%)
  starting transfers between devices  38.4 us (19%)
  waiting for transfers between devices  28.5 us (14%)
    all_to_all x3, blocking collectives, swap(): lax.all_to_all(values, 'cut', split_axis=0, concat_axis=0, tiled=True)  85.3 us
    all_to_all x2, waiting for transfers between devices, swap(): lax.all_to_all(values, 'cut', split_axis=0, concat_axis=0, tiled=True)  18.7 us
    ppermute x7, starting transfers between devices, across(): return lax.ppermute(values, 'cut', [(i, i ^ bits) for i in every])  16.7 us
    ppermute x6, starting transfers between devices, ahead(): lax.ppermute(values, 'cut', [(i, (i + k * fast) % (4 * fast)) for i in ev...  11.6 us
    all_to_all x2, starting transfers between devices, swap(): lax.all_to_all(values, 'cut', split_axis=0, concat_axis=0, tiled=True)  10.1 us
    pallas_call x1, Pallas kernels, per_device(): pl.pallas_call(edge_bwd_kernel, grid=(steps,), out_shape=(sent((latent, s...  7.97 us
    ppermute x6, waiting for transfers between devices, ahead(): lax.ppermute(values, 'cut', [(i, (i + k * fast) % (4 * fast)) for i in ev...  6.35 us
    pallas_call x1, Pallas kernels, per_device(): whole(node_kernel, (sent((latent, masters), BF16), sent((latent, masters)...  6.05 us
  transfers between devices with their start and end apart: 15, of which 8 were waited for; matrix products, arithmetic and copies ran while one was open for 1% of the time, Pallas kernels for 9%

profile of v3, /device:TPU:6, one launch (start us, length us, event | category | flops | bytes accessed | tf_op | source)
XLA Modules:
  0.0 196.2 jit_solution(11274445933053353336)
XLA Ops:
  0.6 21.2 %all_to_all.25.idx_ref = s32[32,1,128]{2,1,0:T(1,128)S(1)} all-to-all(s32[32,1,128]{2,1,0:T(1,128)} %bitcast.31), channel_id=1, replica_groups=mesh['dp'=8,'cut'=32] {'cut'}, dimensions={0} | all-to-all | bytes 32768 | tf_op jit(solution)/shard_map/all_to_all | solution.py:519
  21.8 3.2 %gather.1 = bf16[32,128,128]{2,1,0:T(8,128)(2,1)} custom-call(s32[32,1,128]{2,1,0:T(1,128)S(1)} %all_to_all.25.idx_ref, bf16[128,1024]{1,0:T(8,128)(2,1)} %node_ref.7), custom_call_target="tpu_custom_call" | custom-call | tf_op jit(solution)/shard_map/gather/pallas_call | solution.py:534
  25.1 31.5 %all_to_all.26.mirror_ref = bf16[32,128,128]{2,1,0:T(8,128)(2,1)S(1)} all-to-all(bf16[32,128,128]{2,1,0:T(8,128)(2,1)} %gather.1), channel_id=1, replica_groups=mesh['dp'=8,'cut'=32] {'cut'}, dimensions={0} | all-to-all | bytes 2097152 | tf_op jit(solution)/shard_map/all_to_all | solution.py:519
  56.6 5.9 %edge_fwd.1 = (f32[128,1024]{1,0:T(8,128)}, bf16[32,128,128]{2,1,0:T(8,128)(2,1)}) custom-call(s32[2,32]{1,0:T(2,128)} %bitcast.32, s32[32]{0:T(128)} %count_ref.3, s32[32,2,128]{2,1,0:T(2,128)} %offset_ref.5, bf16[128,4096]{1,0:T(8,128)(2,1)} %edge_ref.5, bf16[128,1024]{1,0:T(8,128)(2,1)} %node_ref.7, bf16[32,128,128]{2,1,0:T(8,128)(2,1)S(1)} %all_to_all.26.mirror_ref, ...), custom_call_target="tpu_custom_call" | custom-call | tf_op jit(solution)/shard_map/edge_fwd/pallas_call | solution.py:550
  62.5 32.6 %all_to_all.27.mirror_ref = bf16[32,128,128]{2,1,0:T(8,128)(2,1)S(1)} all-to-all(bf16[32,128,128]{2,1,0:T(8,128)(2,1)} %get-tuple-element.31), channel_id=1, replica_groups=mesh['dp'=8,'cut'=32] {'cut'}, dimensions={0} | all-to-all | bytes 2097152 | tf_op jit(solution)/shard_map/all_to_all | solution.py:519
  95.1 6.0 %node.1 = (bf16[128,1024]{1,0:T(8,128)(2,1)}, bf16[128,1024]{1,0:T(8,128)(2,1)}, bf16[32,128,128]{2,1,0:T(8,128)(2,1)}) custom-call(s32[32,1,128]{2,1,0:T(1,128)S(1)} %all_to_all.25.idx_ref, f32[128,1024]{1,0:T(8,128)} %get-tuple-element.30.local_ref, bf16[32,128,128]{2,1,0:T(8,128)(2,1)S(1)} %all_to_all.27.mirror_ref, bf16[128,1024]{1,0:T(8,128)(2,1)} %node_ref.7, ...), custom_call_target="tpu_custom_call" | custom-call | tf_op jit(solution)/shard_map/node/pallas_call | solution.py:628
  101.2 5.2 %all-to-all-start.3 = ((bf16[32,128,128]{2,1,0:T(8,128)(2,1)}), bf16[32,128,128]{2,1,0:T(8,128)(2,1)S(1)}, u32[]{:S(2)}, u32[]{:S(2)}) async-start(bf16[32,128,128]{2,1,0:T(8,128)(2,1)} %get-tuple-element.41), calls=%async_computation.3 | async-start | bytes 2097152 | tf_op jit(solution)/shard_map/all_to_all | solution.py:519
  106.4 5.5 %edge_keep.1 = (bf16[256,4096]{1,0:T(8,128)(2,1)}, bf16[128,4096]{1,0:T(8,128)(2,1)}, f32[128,4096]{1,0:T(8,128)}, f32[128,4096]{1,0:T(8,128)}, f32[1,4096]{1,0:T(1,128)}) custom-call(s32[2,32]{1,0:T(2,128)} %bitcast.33, s32[32,2,128]{2,1,0:T(2,128)} %offset_ref.5, bf16[128,4096]{1,0:T(8,128)(2,1)} %edge_ref.5, bf16[128,1024]{1,0:T(8,128)(2,1)} %node_ref.7, ...), custom_call_target="tpu_custom_call" | custom-call | flops 805306368 | bytes 8388608 | tf_op jit(solution)/shard_map/edge_keep/pallas_call | solution.py:587
  111.9 3.2 %node_rest.1 = (bf16[128,1024]{1,0:T(8,128)(2,1)}, f32[128,1024]{1,0:T(8,128)}, f32[392,128]{1,0:T(8,128)}) custom-call(bf16[128,1024]{1,0:T(8,128)(2,1)} %get-tuple-element.32.agg_low_ref, bf16[128,1024]{1,0:T(8,128)(2,1)} %node_ref.7, bf16[128,1024]{1,0:T(8,128)(2,1)} %cot_ref.3, bf16[128,256]{1,0:T(8,128)(2,1)} %w1_ref.8, f32[1,128]{1,0:T(1,128)} %bitcast.41, ...), custom_call_target="tpu_custom_call" | custom-call | flops 369098752 | bytes 2621440 | tf_op jit(solution)/shard_map/node_rest/pallas_call | solution.py:650
  115.1 18.7 %all-to-all-done.3.mirror_ref = bf16[32,128,128]{2,1,0:T(8,128)(2,1)S(1)} async-done(((bf16[32,128,128]{2,1,0:T(8,128)(2,1)}), bf16[32,128,128]{2,1,0:T(8,128)(2,1)S(1)}, u32[]{:S(2)}, u32[]{:S(2)}) %all-to-all-start.3) | async-done | bytes 1048608 | tf_op jit(solution)/shard_map/all_to_all | solution.py:519
  133.8 8.0 %edge_bwd.1 = (bf16[128,4096]{1,0:T(8,128)(2,1)}, bf16[128,4096]{1,0:T(8,128)(2,1)}, f32[128,1024]{1,0:T(8,128)}, bf16[32,128,128]{2,1,0:T(8,128)(2,1)}, f32[3,128,128]{2,1,0:T(8,128)}) custom-call(s32[2,32]{1,0:T(2,128)} %bitcast.34, s32[32]{0:T(128)} %count_ref.3, s32[32,2,128]{2,1,0:T(2,128)} %offset_ref.5, f32[128,4096]{1,0:T(8,128)} %get-tuple-element.37.slope_ref, ...), custom_call_target="tpu_custom_call" | custom-call | tf_op jit(solution)/shard_map/edge_bwd/pallas_call | solution.py:678
  141.8 5.0 %all-to-all-start.4 = ((bf16[32,128,128]{2,1,0:T(8,128)(2,1)}), bf16[32,128,128]{2,1,0:T(8,128)(2,1)S(1)}, u32[]{:S(2)}, u32[]{:S(2)}) async-start(bf16[32,128,128]{2,1,0:T(8,128)(2,1)} %get-tuple-element.49), calls=%async_computation.4 | async-start | bytes 2097152 | tf_op jit(solution)/shard_map/all_to_all | solution.py:519
  146.9 5.3 %edge_weights.1 = (bf16[128,4096]{1,0:T(8,128)(2,1)}, bf16[928,128]{1,0:T(8,128)(2,1)}) custom-call(bf16[128,4096]{1,0:T(8,128)(2,1)} %edge_ref.5, bf16[256,4096]{1,0:T(8,128)(2,1)} %get-tuple-element.35.pair_ref, bf16[128,4096]{1,0:T(8,128)(2,1)} %get-tuple-element.36.hidden_ref, bf16[128,4096]{1,0:T(8,128)(2,1)} %get-tuple-element.43.post_ref, ...), custom_call_target="tpu_custom_call" | custom-call | flops 671088640 | bytes 7340032 | tf_op jit(solution)/shard_map/edge_weights/pallas_call | solution.py:734
  152.1 0.9 dynamic-slice_bitcast_fusion.2
  153.0 3.1 %collective-permute-start.2 = (bf16[232,128]{1,0:T(8,128)(2,1)S(1)}, bf16[232,128]{1,0:T(8,128)(2,1)S(1)}, u32[]{:S(2)}, u32[]{:S(2)}) collective-permute-start(bf16[232,128]{1,0:T(8,128)(2,1)S(1)} %get-tuple-element.57), channel_id=1, source_target_pairs={{0,24},{1,25},{2,26},{3,27},{4,28},{5,29},{6,30},{7,31},{8,0},{9,1... | collective-permute-start | bytes 178184 | tf_op jit(solution)/shard_map/ppermute | solution.py:449
  156.2 0.8 collective-permute-start.1
  157.0 0.9 collective-permute-start
  157.8 0.2 collective-permute-done.2
  158.0 4.6 %collective-permute-done.1 = bf16[232,128]{1,0:T(8,128)(2,1)S(1)} collective-permute-done((bf16[232,128]{1,0:T(8,128)(2,1)S(1)}, bf16[232,128]{1,0:T(8,128)(2,1)S(1)}, u32[]{:S(2)}, u32[]{:S(2)}) %collective-permute-start.1) | collective-permute-done | bytes 59424 | tf_op jit(solution)/shard_map/ppermute | solution.py:449
  162.6 1.5 collective-permute-done
  164.2 0.9 fusion.1
  165.1 2.6 %collective-permute-start.9 = (bf16[232,128]{1,0:T(8,128)(2,1)S(1)}, bf16[232,128]{1,0:T(8,128)(2,1)S(1)}, u32[]{:S(2)}, u32[]{:S(2)}) collective-permute-start(bf16[232,128]{1,0:T(8,128)(2,1)S(1)} %fusion.1), channel_id=1, source_target_pairs={{0,7},{1,6},{2,5},{3,4},{4,3},{5,2},{6,1},{7,0},{8,15},{9,14},{10,... | collective-permute-start | bytes 178184 | tf_op jit(solution)/shard_map/ppermute | solution.py:452
  167.6 2.1 %collective-permute-start.8 = (bf16[232,128]{1,0:T(8,128)(2,1)S(1)}, bf16[232,128]{1,0:T(8,128)(2,1)S(1)}, u32[]{:S(2)}, u32[]{:S(2)}) collective-permute-start(bf16[232,128]{1,0:T(8,128)(2,1)S(1)} %fusion.1), channel_id=1, source_target_pairs={{0,6},{1,7},{2,4},{3,5},{4,2},{5,3},{6,0},{7,1},{8,14},{9,15},{10,... | collective-permute-start | bytes 178184 | tf_op jit(solution)/shard_map/ppermute | solution.py:452
  169.8 3.5 %collective-permute-start.7 = (bf16[232,128]{1,0:T(8,128)(2,1)S(1)}, bf16[232,128]{1,0:T(8,128)(2,1)S(1)}, u32[]{:S(2)}, u32[]{:S(2)}) collective-permute-start(bf16[232,128]{1,0:T(8,128)(2,1)S(1)} %fusion.1), channel_id=1, source_target_pairs={{0,5},{1,4},{2,7},{3,6},{4,1},{5,0},{6,3},{7,2},{8,13},{9,12},{10,... | collective-permute-start | bytes 178184 | tf_op jit(solution)/shard_map/ppermute | solution.py:452
  173.3 2.2 %collective-permute-start.6 = (bf16[232,128]{1,0:T(8,128)(2,1)S(1)}, bf16[232,128]{1,0:T(8,128)(2,1)S(1)}, u32[]{:S(2)}, u32[]{:S(2)}) collective-permute-start(bf16[232,128]{1,0:T(8,128)(2,1)S(1)} %fusion.1), channel_id=1, source_target_pairs={{0,4},{1,5},{2,6},{3,7},{4,0},{5,1},{6,2},{7,3},{8,12},{9,13},{10,... | collective-permute-start | bytes 178184 | tf_op jit(solution)/shard_map/ppermute | solution.py:452
  175.4 2.4 %collective-permute-start.5 = (bf16[232,128]{1,0:T(8,128)(2,1)S(1)}, bf16[232,128]{1,0:T(8,128)(2,1)S(1)}, u32[]{:S(2)}, u32[]{:S(2)}) collective-permute-start(bf16[232,128]{1,0:T(8,128)(2,1)S(1)} %fusion.1), channel_id=1, source_target_pairs={{0,3},{1,2},{2,1},{3,0},{4,7},{5,6},{6,5},{7,4},{8,11},{9,10},{10,... | collective-permute-start | bytes 178184 | tf_op jit(solution)/shard_map/ppermute | solution.py:452
  177.8 1.0 collective-permute-done.9
  178.8 0.0 collective-permute-start.4
  178.8 0.0 collective-permute-done.8
  178.8 3.9 %collective-permute-start.3 = (bf16[232,128]{1,0:T(8,128)(2,1)S(1)}, bf16[232,128]{1,0:T(8,128)(2,1)S(1)}, u32[]{:S(2)}, u32[]{:S(2)}) collective-permute-start(bf16[232,128]{1,0:T(8,128)(2,1)S(1)} %fusion.1), channel_id=1, source_target_pairs={{0,1},{1,0},{2,3},{3,2},{4,5},{5,4},{6,7},{7,6},{8,9},{9,8},{10,11... | collective-permute-start | bytes 178184 | tf_op jit(solution)/shard_map/ppermute | solution.py:452
  182.7 0.0 collective-permute-done.7
  182.7 1.2 collective-permute-done.6
  183.9 0.0 collective-permute-done.5
  183.9 0.9 collective-permute-done.4
  184.9 0.3 collective-permute-done.3
  185.2 0.1 add_convert_fusion
  185.2 2.8 %collective-permute-start.10 = (bf16[232,128]{1,0:T(8,128)(2,1)S(1)}, bf16[232,128]{1,0:T(8,128)(2,1)S(1)}, u32[]{:S(2)}, u32[]{:S(2)}) collective-permute-start(bf16[232,128]{1,0:T(8,128)(2,1)S(1)} %add_convert_fusion), channel_id=1, source_target_pairs={{0,8},{1,9},{2,10},{3,11},{4,12},{5,13},{6,14},{7,15},{8,16},{9,17... | collective-permute-start | bytes 178184 | tf_op jit(solution)/shard_map/ppermute | solution.py:449
  188.0 2.7 %collective-permute-start.11 = (bf16[232,128]{1,0:T(8,128)(2,1)S(1)}, bf16[232,128]{1,0:T(8,128)(2,1)S(1)}, u32[]{:S(2)}, u32[]{:S(2)}) collective-permute-start(bf16[232,128]{1,0:T(8,128)(2,1)S(1)} %add_convert_fusion), channel_id=1, source_target_pairs={{0,16},{1,17},{2,18},{3,19},{4,20},{5,21},{6,22},{7,23},{8,24},{9,... | collective-permute-start | bytes 178184 | tf_op jit(solution)/shard_map/ppermute | solution.py:449
  190.7 1.3 collective-permute-start.12
  192.1 0.0 all-to-all-done.4.mirror_ref
  192.1 3.3 %final.1 = f32[128,1024]{1,0:T(8,128)} custom-call(s32[32,1,128]{2,1,0:T(1,128)S(1)} %all_to_all.25.idx_ref, f32[128,1024]{1,0:T(8,128)} %get-tuple-element.48.local_ref, bf16[32,128,128]{2,1,0:T(8,128)(2,1)S(1)} %all-to-all-done.4.mirror_ref), custom_call_target="tpu_custom_call" | custom-call | tf_op jit(solution)/shard_map/final/pallas_call | solution.py:770
  195.3 0.0 collective-permute-done.10
  195.3 0.0 collective-permute-done.11
  195.4 0.0 collective-permute-done.12
  195.4 0.8 params.1
  (1 shorter events, 0.0 us)
Async XLA Ops:
  101.2 32.6 %all-to-all-start.3 = ((bf16[32,128,128]{2,1,0:T(8,128)(2,1)}), bf16[32,128,128]{2,1,0:T(8,128)(2,1)S(1)}, u32[]{:S(2)}, u32[]{:S(2)}) async-start(bf16[32,128,128]{2,1,0:T(8,128)(2,1)} %get-tuple-element.41), calls=%async_computation.3 | async-start | bytes 2097152 | tf_op jit(solution)/shard_map/all_to_all | solution.py:519
  141.8 50.3 %all-to-all-start.4 = ((bf16[32,128,128]{2,1,0:T(8,128)(2,1)}), bf16[32,128,128]{2,1,0:T(8,128)(2,1)S(1)}, u32[]{:S(2)}, u32[]{:S(2)}) async-start(bf16[32,128,128]{2,1,0:T(8,128)(2,1)} %get-tuple-element.49), calls=%async_computation.4 | async-start | bytes 2097152 | tf_op jit(solution)/shard_map/all_to_all | solution.py:519
  153.0 5.0 %collective-permute-start.2 = (bf16[232,128]{1,0:T(8,128)(2,1)S(1)}, bf16[232,128]{1,0:T(8,128)(2,1)S(1)}, u32[]{:S(2)}, u32[]{:S(2)}) collective-permute-start(bf16[232,128]{1,0:T(8,128)(2,1)S(1)} %get-tuple-element.57), channel_id=1, source_target_pairs={{0,24},{1,25},{2,26},{3,27},{4,28},{5,29},{6,30},{7,31},{8,0},{9,1... | collective-permute-start | bytes 178184 | tf_op jit(solution)/shard_map/ppermute | solution.py:449
  156.2 6.5 %collective-permute-start.1 = (bf16[232,128]{1,0:T(8,128)(2,1)S(1)}, bf16[232,128]{1,0:T(8,128)(2,1)S(1)}, u32[]{:S(2)}, u32[]{:S(2)}) collective-permute-start(bf16[232,128]{1,0:T(8,128)(2,1)S(1)} %get-tuple-element.58), channel_id=1, source_target_pairs={{0,16},{1,17},{2,18},{3,19},{4,20},{5,21},{6,22},{7,23},{8,24},{9,... | collective-permute-start | bytes 178184 | tf_op jit(solution)/shard_map/ppermute | solution.py:449
  157.0 7.2 %collective-permute-start = (bf16[232,128]{1,0:T(8,128)(2,1)S(1)}, bf16[232,128]{1,0:T(8,128)(2,1)S(1)}, u32[]{:S(2)}, u32[]{:S(2)}) collective-permute-start(bf16[232,128]{1,0:T(8,128)(2,1)S(1)} %get-tuple-element.56), channel_id=1, source_target_pairs={{0,8},{1,9},{2,10},{3,11},{4,12},{5,13},{6,14},{7,15},{8,16},{9,17... | collective-permute-start | bytes 178184 | tf_op jit(solution)/shard_map/ppermute | solution.py:449
  165.1 13.7 %collective-permute-start.9 = (bf16[232,128]{1,0:T(8,128)(2,1)S(1)}, bf16[232,128]{1,0:T(8,128)(2,1)S(1)}, u32[]{:S(2)}, u32[]{:S(2)}) collective-permute-start(bf16[232,128]{1,0:T(8,128)(2,1)S(1)} %fusion.1), channel_id=1, source_target_pairs={{0,7},{1,6},{2,5},{3,4},{4,3},{5,2},{6,1},{7,0},{8,15},{9,14},{10,... | collective-permute-start | bytes 178184 | tf_op jit(solution)/shard_map/ppermute | solution.py:452
  167.6 11.2 %collective-permute-start.8 = (bf16[232,128]{1,0:T(8,128)(2,1)S(1)}, bf16[232,128]{1,0:T(8,128)(2,1)S(1)}, u32[]{:S(2)}, u32[]{:S(2)}) collective-permute-start(bf16[232,128]{1,0:T(8,128)(2,1)S(1)} %fusion.1), channel_id=1, source_target_pairs={{0,6},{1,7},{2,4},{3,5},{4,2},{5,3},{6,0},{7,1},{8,14},{9,15},{10,... | collective-permute-start | bytes 178184 | tf_op jit(solution)/shard_map/ppermute | solution.py:452
  169.8 13.0 %collective-permute-start.7 = (bf16[232,128]{1,0:T(8,128)(2,1)S(1)}, bf16[232,128]{1,0:T(8,128)(2,1)S(1)}, u32[]{:S(2)}, u32[]{:S(2)}) collective-permute-start(bf16[232,128]{1,0:T(8,128)(2,1)S(1)} %fusion.1), channel_id=1, source_target_pairs={{0,5},{1,4},{2,7},{3,6},{4,1},{5,0},{6,3},{7,2},{8,13},{9,12},{10,... | collective-permute-start | bytes 178184 | tf_op jit(solution)/shard_map/ppermute | solution.py:452
  173.3 10.6 %collective-permute-start.6 = (bf16[232,128]{1,0:T(8,128)(2,1)S(1)}, bf16[232,128]{1,0:T(8,128)(2,1)S(1)}, u32[]{:S(2)}, u32[]{:S(2)}) collective-permute-start(bf16[232,128]{1,0:T(8,128)(2,1)S(1)} %fusion.1), channel_id=1, source_target_pairs={{0,4},{1,5},{2,6},{3,7},{4,0},{5,1},{6,2},{7,3},{8,12},{9,13},{10,... | collective-permute-start | bytes 178184 | tf_op jit(solution)/shard_map/ppermute | solution.py:452
  175.4 8.5 %collective-permute-start.5 = (bf16[232,128]{1,0:T(8,128)(2,1)S(1)}, bf16[232,128]{1,0:T(8,128)(2,1)S(1)}, u32[]{:S(2)}, u32[]{:S(2)}) collective-permute-start(bf16[232,128]{1,0:T(8,128)(2,1)S(1)} %fusion.1), channel_id=1, source_target_pairs={{0,3},{1,2},{2,1},{3,0},{4,7},{5,6},{6,5},{7,4},{8,11},{9,10},{10,... | collective-permute-start | bytes 178184 | tf_op jit(solution)/shard_map/ppermute | solution.py:452
  178.8 6.1 %collective-permute-start.4 = (bf16[232,128]{1,0:T(8,128)(2,1)S(1)}, bf16[232,128]{1,0:T(8,128)(2,1)S(1)}, u32[]{:S(2)}, u32[]{:S(2)}) collective-permute-start(bf16[232,128]{1,0:T(8,128)(2,1)S(1)} %fusion.1), channel_id=1, source_target_pairs={{0,2},{1,3},{2,0},{3,1},{4,6},{5,7},{6,4},{7,5},{8,10},{9,11},{10,... | collective-permute-start | bytes 178184 | tf_op jit(solution)/shard_map/ppermute | solution.py:452
  178.8 6.4 %collective-permute-start.3 = (bf16[232,128]{1,0:T(8,128)(2,1)S(1)}, bf16[232,128]{1,0:T(8,128)(2,1)S(1)}, u32[]{:S(2)}, u32[]{:S(2)}) collective-permute-start(bf16[232,128]{1,0:T(8,128)(2,1)S(1)} %fusion.1), channel_id=1, source_target_pairs={{0,1},{1,0},{2,3},{3,2},{4,5},{5,4},{6,7},{7,6},{8,9},{9,8},{10,11... | collective-permute-start | bytes 178184 | tf_op jit(solution)/shard_map/ppermute | solution.py:452
  185.2 10.1 %collective-permute-start.10 = (bf16[232,128]{1,0:T(8,128)(2,1)S(1)}, bf16[232,128]{1,0:T(8,128)(2,1)S(1)}, u32[]{:S(2)}, u32[]{:S(2)}) collective-permute-start(bf16[232,128]{1,0:T(8,128)(2,1)S(1)} %add_convert_fusion), channel_id=1, source_target_pairs={{0,8},{1,9},{2,10},{3,11},{4,12},{5,13},{6,14},{7,15},{8,16},{9,17... | collective-permute-start | bytes 178184 | tf_op jit(solution)/shard_map/ppermute | solution.py:449
  188.0 7.3 %collective-permute-start.11 = (bf16[232,128]{1,0:T(8,128)(2,1)S(1)}, bf16[232,128]{1,0:T(8,128)(2,1)S(1)}, u32[]{:S(2)}, u32[]{:S(2)}) collective-permute-start(bf16[232,128]{1,0:T(8,128)(2,1)S(1)} %add_convert_fusion), channel_id=1, source_target_pairs={{0,16},{1,17},{2,18},{3,19},{4,20},{5,21},{6,22},{7,23},{8,24},{9,... | collective-permute-start | bytes 178184 | tf_op jit(solution)/shard_map/ppermute | solution.py:449
  190.7 4.6 %collective-permute-start.12 = (bf16[232,128]{1,0:T(8,128)(2,1)S(1)}, bf16[232,128]{1,0:T(8,128)(2,1)S(1)}, u32[]{:S(2)}, u32[]{:S(2)}) collective-permute-start(bf16[232,128]{1,0:T(8,128)(2,1)S(1)} %add_convert_fusion), channel_id=1, source_target_pairs={{0,24},{1,25},{2,26},{3,27},{4,28},{5,29},{6,30},{7,31},{8,0},{9,1... | collective-permute-start | bytes 178184 | tf_op jit(solution)/shard_map/ppermute | solution.py:449

commit v4 on v3

--- a/solution.py
+++ b/solution.py
@@ -459,10 +459,12 @@
 
     first, second, third = [ahead(quarter(k), k) for k in range(1, 4)]
     mine = (add(quarter(0), first) + add(second, third)).astype(BF16)
-    terms = [mine] + [across(mine, bits) for bits in range(1, fast)]
-    while len(terms) > 1:
-        terms = [add(terms[k], terms[k + 1]) for k in range(0, len(terms), 2)]
-    mine = terms[0].astype(BF16)
+    one, two = fast // 2, fast // 4
+    first, second, third = [across(mine, bits) for bits in (one, two, one | two)]
+    mine = (add(mine, first) + add(second, third)).astype(BF16)
+    while two > 1:
+        two //= 2
+        mine = add(mine, across(mine, two)).astype(BF16)
     quarters = [mine] + [ahead(mine, k) for k in range(1, 4)]
     quarters, other_work = lax.optimization_barrier((quarters, other_work))
     return jnp.stack(quarters), place, other_work

time: 197 us -> 193 us (0.980)
  starting transfers between devices: 38.4 us -> 27.2 us
  waiting for transfers between devices: 28.5 us -> 35.8 us
    ppermute x7 -> x4, starting transfers between devices: 16.7 us -> 8.08 us  [across(): return lax.ppermute(values, 'cut', [(i, i ^ bits) for i in every])]
    ppermute x7 -> x4, waiting for transfers between devices: 3.41 us -> 10.9 us  [across(): return lax.ppermute(values, 'cut', [(i, i ^ bits) for i in every])]
    ppermute x6, starting transfers between devices: 11.6 us -> 9.04 us  [ahead(): lax.ppermute(values, 'cut', [(i, (i + k * fast) % (4 * fast)) for i in ev...]
  transfers between devices with their start and end apart: 15 -> 12, of which waited for: 8 -> 7; matrix products, arithmetic and copies ran while one was open for 1% -> 1% of each run, Pallas kernels for 9% -> 9%
where the time goes in v4:
time: 193 us
  blocking collectives  85.3 us (44%)
  Pallas kernels  41.5 us (22%)
  waiting for transfers between devices  35.8 us (19%)
  starting transfers between devices  27.2 us (14%)
    all_to_all x3, blocking collectives, swap(): lax.all_to_all(values, 'cut', split_axis=0, concat_axis=0, tiled=True)  85.3 us
    all_to_all x2, waiting for transfers between devices, swap(): lax.all_to_all(values, 'cut', split_axis=0, concat_axis=0, tiled=True)  18.6 us
    ppermute x4, waiting for transfers between devices, across(): return lax.ppermute(values, 'cut', [(i, i ^ bits) for i in every])  10.9 us
    all_to_all x2, starting transfers between devices, swap(): lax.all_to_all(values, 'cut', split_axis=0, concat_axis=0, tiled=True)  10.1 us
    ppermute x6, starting transfers between devices, ahead(): lax.ppermute(values, 'cut', [(i, (i + k * fast) % (4 * fast)) for i in ev...  9.04 us
    ppermute x4, starting transfers between devices, across(): return lax.ppermute(values, 'cut', [(i, i ^ bits) for i in every])  8.08 us
    pallas_call x1, Pallas kernels, per_device(): pl.pallas_call(edge_bwd_kernel, grid=(steps,), out_shape=(sent((latent, s...  7.99 us
    ppermute x6, waiting for transfers between devices, ahead(): lax.ppermute(values, 'cut', [(i, (i + k * fast) % (4 * fast)) for i in ev...  6.37 us
  transfers between devices with their start and end apart: 12, of which 7 were waited for; matrix products, arithmetic and copies ran while one was open for 1% of the time, Pallas kernels for 9%

profile of v4, /device:TPU:6, one launch (start us, length us, event | category | flops | bytes accessed | tf_op | source)
XLA Modules:
  0.0 192.5 jit_solution(15972294697939148387)
XLA Ops:
  0.6 21.2 %all_to_all.25.idx_ref = s32[32,1,128]{2,1,0:T(1,128)S(1)} all-to-all(s32[32,1,128]{2,1,0:T(1,128)} %bitcast.31), channel_id=1, replica_groups=mesh['dp'=8,'cut'=32] {'cut'}, dimensions={0} | all-to-all | bytes 32768 | tf_op jit(solution)/shard_map/all_to_all | solution.py:521
  21.8 3.2 %gather.1 = bf16[32,128,128]{2,1,0:T(8,128)(2,1)} custom-call(s32[32,1,128]{2,1,0:T(1,128)S(1)} %all_to_all.25.idx_ref, bf16[128,1024]{1,0:T(8,128)(2,1)} %node_ref.7), custom_call_target="tpu_custom_call" | custom-call | tf_op jit(solution)/shard_map/gather/pallas_call | solution.py:536
  25.1 31.5 %all_to_all.26.mirror_ref = bf16[32,128,128]{2,1,0:T(8,128)(2,1)S(1)} all-to-all(bf16[32,128,128]{2,1,0:T(8,128)(2,1)} %gather.1), channel_id=1, replica_groups=mesh['dp'=8,'cut'=32] {'cut'}, dimensions={0} | all-to-all | bytes 2097152 | tf_op jit(solution)/shard_map/all_to_all | solution.py:521
  56.6 5.9 %edge_fwd.1 = (f32[128,1024]{1,0:T(8,128)}, bf16[32,128,128]{2,1,0:T(8,128)(2,1)}) custom-call(s32[2,32]{1,0:T(2,128)} %bitcast.32, s32[32]{0:T(128)} %count_ref.3, s32[32,2,128]{2,1,0:T(2,128)} %offset_ref.5, bf16[128,4096]{1,0:T(8,128)(2,1)} %edge_ref.5, bf16[128,1024]{1,0:T(8,128)(2,1)} %node_ref.7, bf16[32,128,128]{2,1,0:T(8,128)(2,1)S(1)} %all_to_all.26.mirror_ref, ...), custom_call_target="tpu_custom_call" | custom-call | tf_op jit(solution)/shard_map/edge_fwd/pallas_call | solution.py:552
  62.5 32.6 %all_to_all.27.mirror_ref = bf16[32,128,128]{2,1,0:T(8,128)(2,1)S(1)} all-to-all(bf16[32,128,128]{2,1,0:T(8,128)(2,1)} %get-tuple-element.31), channel_id=1, replica_groups=mesh['dp'=8,'cut'=32] {'cut'}, dimensions={0} | all-to-all | bytes 2097152 | tf_op jit(solution)/shard_map/all_to_all | solution.py:521
  95.1 6.0 %node.1 = (bf16[128,1024]{1,0:T(8,128)(2,1)}, bf16[128,1024]{1,0:T(8,128)(2,1)}, bf16[32,128,128]{2,1,0:T(8,128)(2,1)}) custom-call(s32[32,1,128]{2,1,0:T(1,128)S(1)} %all_to_all.25.idx_ref, f32[128,1024]{1,0:T(8,128)} %get-tuple-element.30.local_ref, bf16[32,128,128]{2,1,0:T(8,128)(2,1)S(1)} %all_to_all.27.mirror_ref, bf16[128,1024]{1,0:T(8,128)(2,1)} %node_ref.7, ...), custom_call_target="tpu_custom_call" | custom-call | tf_op jit(solution)/shard_map/node/pallas_call | solution.py:630
  101.2 5.2 %all-to-all-start.3 = ((bf16[32,128,128]{2,1,0:T(8,128)(2,1)}), bf16[32,128,128]{2,1,0:T(8,128)(2,1)S(1)}, u32[]{:S(2)}, u32[]{:S(2)}) async-start(bf16[32,128,128]{2,1,0:T(8,128)(2,1)} %get-tuple-element.41), calls=%async_computation.3 | async-start | bytes 2097152 | tf_op jit(solution)/shard_map/all_to_all | solution.py:521
  106.4 5.7 %edge_keep.1 = (bf16[256,4096]{1,0:T(8,128)(2,1)}, bf16[128,4096]{1,0:T(8,128)(2,1)}, f32[128,4096]{1,0:T(8,128)}, f32[128,4096]{1,0:T(8,128)}, f32[1,4096]{1,0:T(1,128)}) custom-call(s32[2,32]{1,0:T(2,128)} %bitcast.33, s32[32,2,128]{2,1,0:T(2,128)} %offset_ref.5, bf16[128,4096]{1,0:T(8,128)(2,1)} %edge_ref.5, bf16[128,1024]{1,0:T(8,128)(2,1)} %node_ref.7, ...), custom_call_target="tpu_custom_call" | custom-call | flops 805306368 | bytes 8388608 | tf_op jit(solution)/shard_map/edge_keep/pallas_call | solution.py:589
  112.0 3.2 %node_rest.1 = (bf16[128,1024]{1,0:T(8,128)(2,1)}, f32[128,1024]{1,0:T(8,128)}, f32[392,128]{1,0:T(8,128)}) custom-call(bf16[128,1024]{1,0:T(8,128)(2,1)} %get-tuple-element.32.agg_low_ref, bf16[128,1024]{1,0:T(8,128)(2,1)} %node_ref.7, bf16[128,1024]{1,0:T(8,128)(2,1)} %cot_ref.3, bf16[128,256]{1,0:T(8,128)(2,1)} %w1_ref.8, f32[1,128]{1,0:T(1,128)} %bitcast.41, ...), custom_call_target="tpu_custom_call" | custom-call | flops 369098752 | bytes 2621440 | tf_op jit(solution)/shard_map/node_rest/pallas_call | solution.py:652
  115.2 18.6 %all-to-all-done.3.mirror_ref = bf16[32,128,128]{2,1,0:T(8,128)(2,1)S(1)} async-done(((bf16[32,128,128]{2,1,0:T(8,128)(2,1)}), bf16[32,128,128]{2,1,0:T(8,128)(2,1)S(1)}, u32[]{:S(2)}, u32[]{:S(2)}) %all-to-all-start.3) | async-done | bytes 1048608 | tf_op jit(solution)/shard_map/all_to_all | solution.py:521
  133.8 8.0 %edge_bwd.1 = (bf16[128,4096]{1,0:T(8,128)(2,1)}, bf16[128,4096]{1,0:T(8,128)(2,1)}, f32[128,1024]{1,0:T(8,128)}, bf16[32,128,128]{2,1,0:T(8,128)(2,1)}, f32[3,128,128]{2,1,0:T(8,128)}) custom-call(s32[2,32]{1,0:T(2,128)} %bitcast.34, s32[32]{0:T(128)} %count_ref.3, s32[32,2,128]{2,1,0:T(2,128)} %offset_ref.5, f32[128,4096]{1,0:T(8,128)} %get-tuple-element.37.slope_ref, ...), custom_call_target="tpu_custom_call" | custom-call | tf_op jit(solution)/shard_map/edge_bwd/pallas_call | solution.py:680
  141.8 5.0 %all-to-all-start.4 = ((bf16[32,128,128]{2,1,0:T(8,128)(2,1)}), bf16[32,128,128]{2,1,0:T(8,128)(2,1)S(1)}, u32[]{:S(2)}, u32[]{:S(2)}) async-start(bf16[32,128,128]{2,1,0:T(8,128)(2,1)} %get-tuple-element.49), calls=%async_computation.4 | async-start | bytes 2097152 | tf_op jit(solution)/shard_map/all_to_all | solution.py:521
  146.9 5.3 %edge_weights.1 = (bf16[128,4096]{1,0:T(8,128)(2,1)}, bf16[928,128]{1,0:T(8,128)(2,1)}) custom-call(bf16[128,4096]{1,0:T(8,128)(2,1)} %edge_ref.5, bf16[256,4096]{1,0:T(8,128)(2,1)} %get-tuple-element.35.pair_ref, bf16[128,4096]{1,0:T(8,128)(2,1)} %get-tuple-element.36.hidden_ref, bf16[128,4096]{1,0:T(8,128)(2,1)} %get-tuple-element.43.post_ref, ...), custom_call_target="tpu_custom_call" | custom-call | flops 671088640 | bytes 7340032 | tf_op jit(solution)/shard_map/edge_weights/pallas_call | solution.py:736
  152.2 0.9 dynamic-slice_bitcast_fusion.2
  153.1 3.1 %collective-permute-start.2 = (bf16[232,128]{1,0:T(8,128)(2,1)S(1)}, bf16[232,128]{1,0:T(8,128)(2,1)S(1)}, u32[]{:S(2)}, u32[]{:S(2)}) collective-permute-start(bf16[232,128]{1,0:T(8,128)(2,1)S(1)} %get-tuple-element.57), channel_id=1, source_target_pairs={{0,24},{1,25},{2,26},{3,27},{4,28},{5,29},{6,30},{7,31},{8,0},{9,1... | collective-permute-start | bytes 178184 | tf_op jit(solution)/shard_map/ppermute | solution.py:449
  156.2 0.8 collective-permute-start.1
  157.0 0.9 collective-permute-start
  157.9 0.2 collective-permute-done.2
  158.1 4.6 %collective-permute-done.1 = bf16[232,128]{1,0:T(8,128)(2,1)S(1)} collective-permute-done((bf16[232,128]{1,0:T(8,128)(2,1)S(1)}, bf16[232,128]{1,0:T(8,128)(2,1)S(1)}, u32[]{:S(2)}, u32[]{:S(2)}) %collective-permute-start.1) | collective-permute-done | bytes 59424 | tf_op jit(solution)/shard_map/ppermute | solution.py:449
  162.7 1.5 collective-permute-done
  164.2 0.9 fusion.1
  165.1 3.5 %collective-permute-start.5 = (bf16[232,128]{1,0:T(8,128)(2,1)S(1)}, bf16[232,128]{1,0:T(8,128)(2,1)S(1)}, u32[]{:S(2)}, u32[]{:S(2)}) collective-permute-start(bf16[232,128]{1,0:T(8,128)(2,1)S(1)} %fusion.1), channel_id=1, source_target_pairs={{0,6},{1,7},{2,4},{3,5},{4,2},{5,3},{6,0},{7,1},{8,14},{9,15},{10,... | collective-permute-start | bytes 178184 | tf_op jit(solution)/shard_map/ppermute | solution.py:452
  168.6 2.1 %collective-permute-start.4 = (bf16[232,128]{1,0:T(8,128)(2,1)S(1)}, bf16[232,128]{1,0:T(8,128)(2,1)S(1)}, u32[]{:S(2)}, u32[]{:S(2)}) collective-permute-start(bf16[232,128]{1,0:T(8,128)(2,1)S(1)} %fusion.1), channel_id=1, source_target_pairs={{0,2},{1,3},{2,0},{3,1},{4,6},{5,7},{6,4},{7,5},{8,10},{9,11},{10,... | collective-permute-start | bytes 178184 | tf_op jit(solution)/shard_map/ppermute | solution.py:452
  170.6 1.0 collective-permute-start.3
  171.7 4.4 %collective-permute-done.5 = bf16[232,128]{1,0:T(8,128)(2,1)S(1)} collective-permute-done((bf16[232,128]{1,0:T(8,128)(2,1)S(1)}, bf16[232,128]{1,0:T(8,128)(2,1)S(1)}, u32[]{:S(2)}, u32[]{:S(2)}) %collective-permute-start.5) | collective-permute-done | bytes 59424 | tf_op jit(solution)/shard_map/ppermute | solution.py:452
  176.1 0.0 collective-permute-done.4
  176.1 3.6 %collective-permute-done.3 = bf16[232,128]{1,0:T(8,128)(2,1)S(1)} collective-permute-done((bf16[232,128]{1,0:T(8,128)(2,1)S(1)}, bf16[232,128]{1,0:T(8,128)(2,1)S(1)}, u32[]{:S(2)}, u32[]{:S(2)}) %collective-permute-start.3) | collective-permute-done | bytes 59424 | tf_op jit(solution)/shard_map/ppermute | solution.py:452
  179.8 1.5 collective-permute-start.6
  181.3 2.8 %collective-permute-done.6 = bf16[232,128]{1,0:T(8,128)(2,1)S(1)} collective-permute-done((bf16[232,128]{1,0:T(8,128)(2,1)S(1)}, bf16[232,128]{1,0:T(8,128)(2,1)S(1)}, u32[]{:S(2)}, u32[]{:S(2)}) %collective-permute-start.6) | collective-permute-done | bytes 59424 | tf_op jit(solution)/shard_map/ppermute | solution.py:452
  184.1 0.1 collective-permute-start.7
  184.2 2.7 %collective-permute-start.8 = (bf16[232,128]{1,0:T(8,128)(2,1)S(1)}, bf16[232,128]{1,0:T(8,128)(2,1)S(1)}, u32[]{:S(2)}, u32[]{:S(2)}) collective-permute-start(bf16[232,128]{1,0:T(8,128)(2,1)S(1)} %add_convert_fusion), channel_id=1, source_target_pairs={{0,16},{1,17},{2,18},{3,19},{4,20},{5,21},{6,22},{7,23},{8,24},{9,... | collective-permute-start | bytes 178184 | tf_op jit(solution)/shard_map/ppermute | solution.py:449
  186.9 1.5 collective-permute-start.9
  188.4 0.0 all-to-all-done.4.mirror_ref
  188.4 3.3 %final.1 = f32[128,1024]{1,0:T(8,128)} custom-call(s32[32,1,128]{2,1,0:T(1,128)S(1)} %all_to_all.25.idx_ref, f32[128,1024]{1,0:T(8,128)} %get-tuple-element.48.local_ref, bf16[32,128,128]{2,1,0:T(8,128)(2,1)S(1)} %all-to-all-done.4.mirror_ref), custom_call_target="tpu_custom_call" | custom-call | tf_op jit(solution)/shard_map/final/pallas_call | solution.py:772
  191.7 0.0 collective-permute-done.7
  191.7 0.0 collective-permute-done.8
  191.7 0.0 collective-permute-done.9
  191.7 0.8 params.1
  (3 shorter events, 0.1 us)
Async XLA Ops:
  101.2 32.6 %all-to-all-start.3 = ((bf16[32,128,128]{2,1,0:T(8,128)(2,1)}), bf16[32,128,128]{2,1,0:T(8,128)(2,1)S(1)}, u32[]{:S(2)}, u32[]{:S(2)}) async-start(bf16[32,128,128]{2,1,0:T(8,128)(2,1)} %get-tuple-element.41), calls=%async_computation.3 | async-start | bytes 2097152 | tf_op jit(solution)/shard_map/all_to_all | solution.py:521
  141.8 46.6 %all-to-all-start.4 = ((bf16[32,128,128]{2,1,0:T(8,128)(2,1)}), bf16[32,128,128]{2,1,0:T(8,128)(2,1)S(1)}, u32[]{:S(2)}, u32[]{:S(2)}) async-start(bf16[32,128,128]{2,1,0:T(8,128)(2,1)} %get-tuple-element.49), calls=%async_computation.4 | async-start | bytes 2097152 | tf_op jit(solution)/shard_map/all_to_all | solution.py:521
  153.1 5.0 %collective-permute-start.2 = (bf16[232,128]{1,0:T(8,128)(2,1)S(1)}, bf16[232,128]{1,0:T(8,128)(2,1)S(1)}, u32[]{:S(2)}, u32[]{:S(2)}) collective-permute-start(bf16[232,128]{1,0:T(8,128)(2,1)S(1)} %get-tuple-element.57), channel_id=1, source_target_pairs={{0,24},{1,25},{2,26},{3,27},{4,28},{5,29},{6,30},{7,31},{8,0},{9,1... | collective-permute-start | bytes 178184 | tf_op jit(solution)/shard_map/ppermute | solution.py:449
  156.2 6.5 %collective-permute-start.1 = (bf16[232,128]{1,0:T(8,128)(2,1)S(1)}, bf16[232,128]{1,0:T(8,128)(2,1)S(1)}, u32[]{:S(2)}, u32[]{:S(2)}) collective-permute-start(bf16[232,128]{1,0:T(8,128)(2,1)S(1)} %get-tuple-element.58), channel_id=1, source_target_pairs={{0,16},{1,17},{2,18},{3,19},{4,20},{5,21},{6,22},{7,23},{8,24},{9,... | collective-permute-start | bytes 178184 | tf_op jit(solution)/shard_map/ppermute | solution.py:449
  157.0 7.2 %collective-permute-start = (bf16[232,128]{1,0:T(8,128)(2,1)S(1)}, bf16[232,128]{1,0:T(8,128)(2,1)S(1)}, u32[]{:S(2)}, u32[]{:S(2)}) collective-permute-start(bf16[232,128]{1,0:T(8,128)(2,1)S(1)} %get-tuple-element.56), channel_id=1, source_target_pairs={{0,8},{1,9},{2,10},{3,11},{4,12},{5,13},{6,14},{7,15},{8,16},{9,17... | collective-permute-start | bytes 178184 | tf_op jit(solution)/shard_map/ppermute | solution.py:449
  165.1 11.0 %collective-permute-start.5 = (bf16[232,128]{1,0:T(8,128)(2,1)S(1)}, bf16[232,128]{1,0:T(8,128)(2,1)S(1)}, u32[]{:S(2)}, u32[]{:S(2)}) collective-permute-start(bf16[232,128]{1,0:T(8,128)(2,1)S(1)} %fusion.1), channel_id=1, source_target_pairs={{0,6},{1,7},{2,4},{3,5},{4,2},{5,3},{6,0},{7,1},{8,14},{9,15},{10,... | collective-permute-start | bytes 178184 | tf_op jit(solution)/shard_map/ppermute | solution.py:452
  168.6 7.5 %collective-permute-start.4 = (bf16[232,128]{1,0:T(8,128)(2,1)S(1)}, bf16[232,128]{1,0:T(8,128)(2,1)S(1)}, u32[]{:S(2)}, u32[]{:S(2)}) collective-permute-start(bf16[232,128]{1,0:T(8,128)(2,1)S(1)} %fusion.1), channel_id=1, source_target_pairs={{0,2},{1,3},{2,0},{3,1},{4,6},{5,7},{6,4},{7,5},{8,10},{9,11},{10,... | collective-permute-start | bytes 178184 | tf_op jit(solution)/shard_map/ppermute | solution.py:452
  170.6 9.1 %collective-permute-start.3 = (bf16[232,128]{1,0:T(8,128)(2,1)S(1)}, bf16[232,128]{1,0:T(8,128)(2,1)S(1)}, u32[]{:S(2)}, u32[]{:S(2)}) collective-permute-start(bf16[232,128]{1,0:T(8,128)(2,1)S(1)} %fusion.1), channel_id=1, source_target_pairs={{0,4},{1,5},{2,6},{3,7},{4,0},{5,1},{6,2},{7,3},{8,12},{9,13},{10,... | collective-permute-start | bytes 178184 | tf_op jit(solution)/shard_map/ppermute | solution.py:452
  179.8 4.3 %collective-permute-start.6 = (bf16[232,128]{1,0:T(8,128)(2,1)S(1)}, bf16[232,128]{1,0:T(8,128)(2,1)S(1)}, u32[]{:S(2)}, u32[]{:S(2)}) collective-permute-start(bf16[232,128]{1,0:T(8,128)(2,1)S(1)} %add_convert_fusion.1), channel_id=1, source_target_pairs={{0,1},{1,0},{2,3},{3,2},{4,5},{5,4},{6,7},{7,6},{8,9},{9,8},{10,11... | collective-permute-start | bytes 178184 | tf_op jit(solution)/shard_map/ppermute | solution.py:452
  184.1 7.6 %collective-permute-start.7 = (bf16[232,128]{1,0:T(8,128)(2,1)S(1)}, bf16[232,128]{1,0:T(8,128)(2,1)S(1)}, u32[]{:S(2)}, u32[]{:S(2)}) collective-permute-start(bf16[232,128]{1,0:T(8,128)(2,1)S(1)} %add_convert_fusion), channel_id=1, source_target_pairs={{0,8},{1,9},{2,10},{3,11},{4,12},{5,13},{6,14},{7,15},{8,16},{9,17... | collective-permute-start | bytes 178184 | tf_op jit(solution)/shard_map/ppermute | solution.py:449
  184.2 7.5 %collective-permute-start.8 = (bf16[232,128]{1,0:T(8,128)(2,1)S(1)}, bf16[232,128]{1,0:T(8,128)(2,1)S(1)}, u32[]{:S(2)}, u32[]{:S(2)}) collective-permute-start(bf16[232,128]{1,0:T(8,128)(2,1)S(1)} %add_convert_fusion), channel_id=1, source_target_pairs={{0,16},{1,17},{2,18},{3,19},{4,20},{5,21},{6,22},{7,23},{8,24},{9,... | collective-permute-start | bytes 178184 | tf_op jit(solution)/shard_map/ppermute | solution.py:449
  186.9 4.8 %collective-permute-start.9 = (bf16[232,128]{1,0:T(8,128)(2,1)S(1)}, bf16[232,128]{1,0:T(8,128)(2,1)S(1)}, u32[]{:S(2)}, u32[]{:S(2)}) collective-permute-start(bf16[232,128]{1,0:T(8,128)(2,1)S(1)} %add_convert_fusion), channel_id=1, source_target_pairs={{0,24},{1,25},{2,26},{3,27},{4,28},{5,29},{6,30},{7,31},{8,0},{9,1... | collective-permute-start | bytes 178184 | tf_op jit(solution)/shard_map/ppermute | solution.py:449

commit v5 on v4

--- a/solution.py
+++ b/solution.py
@@ -83,11 +83,8 @@
     for t in range(local_tiles):
         table[t] = local_ref[:, t * TILE : (t + 1) * TILE]
 
-    def body(p, carry):
-        table[local_tiles + p] = mirror_ref[p, :TILE, :]
-        return carry
-
-    lax.fori_loop(0, mirror_ref.shape[0], body, 0)
+    for p in range(mirror_ref.shape[0]):
+        table[local_tiles + p] = mirror_ref[p]
 
 
 def edge_network(step, tile_ref, offset_ref, edge_ref, table, w1_ref, b1_ref, w2_ref):
@@ -154,11 +151,8 @@
         for t in range(local_tiles):
             local_ref[:, t * TILE : (t + 1) * TILE] = total[t]
 
-        def body(p, carry):
+        for p in range(out_ref.shape[0]):
             out_ref[p] = total[local_tiles + p].astype(BF16)
-            return carry
-
-        lax.fori_loop(0, out_ref.shape[0], body, 0)
 
 
 def edge_keep_kernel(
@@ -188,8 +182,8 @@
     )
     pair_ref[...] = pair
     hidden_ref[...] = hidden
-    slope_ref[...] = gate * (1.0 + pre * (1.0 - gate))
-    normed_ref[...] = normed
+    slope_ref[...] = (gate * (1.0 + pre * (1.0 - gate))).astype(BF16)
+    normed_ref[...] = normed.astype(BF16)
     inv_ref[...] = inverse
 
 
@@ -330,7 +324,7 @@
         found = dot_nn(table[tile_ref[1, b]], one_hot(offset_ref[j, 1:2, :], TILE))
         picked.append(jnp.where(lane < count_ref[b], found, 0.0))
     upstream = jnp.concatenate(picked, axis=1)
-    normed = normed_ref[...]
+    normed = normed_ref[...].astype(F32)
     weighted = upstream * normed
     grad_post = norm_back(upstream, normed, inv_ref[...], gain).astype(BF16)
     post_ref[...] = grad_post
@@ -592,8 +586,8 @@
         out_shape=(
             sent((2 * latent, slots), BF16),
             sent((latent, slots), BF16),
-            sent((latent, slots), F32),
-            sent((latent, slots), F32),
+            sent((latent, slots), BF16),
+            sent((latent, slots), BF16),
             sent((1, slots), F32),
         ),
         in_specs=[

time: 193 us -> 193 us (level)
  no operation moved by 1% of the time
where the time goes in v5:
time: 193 us; the launch traced here: 192 us
  blocking collectives  85.3 us (44%)
  Pallas kernels  40.8 us (21%)
  waiting for transfers between devices  35.8 us (19%)
  starting transfers between devices  27.4 us (14%)
    all_to_all x3, blocking collectives, swap(): lax.all_to_all(values, 'cut', split_axis=0, concat_axis=0, tiled=True)  85.3 us
    all_to_all x2, waiting for transfers between devices, swap(): lax.all_to_all(values, 'cut', split_axis=0, concat_axis=0, tiled=True)  18.7 us
    ppermute x4, waiting for transfers between devices, across(): return lax.ppermute(values, 'cut', [(i, i ^ bits) for i in every])  10.8 us
    all_to_all x2, starting transfers between devices, swap(): lax.all_to_all(values, 'cut', split_axis=0, concat_axis=0, tiled=True)  10.1 us
    ppermute x6, starting transfers between devices, ahead(): lax.ppermute(values, 'cut', [(i, (i + k * fast) % (4 * fast)) for i in ev...  9.14 us
    ppermute x4, starting transfers between devices, across(): return lax.ppermute(values, 'cut', [(i, i ^ bits) for i in every])  8.11 us
    pallas_call x1, Pallas kernels, per_device(): pl.pallas_call(edge_bwd_kernel, grid=(steps,), out_shape=(sent((latent, s...  7.63 us
    ppermute x6, waiting for transfers between devices, ahead(): lax.ppermute(values, 'cut', [(i, (i + k * fast) % (4 * fast)) for i in ev...  6.35 us
  transfers between devices with their start and end apart: 12, of which 7 were waited for; matrix products, arithmetic and copies ran while one was open for 1% of the time, Pallas kernels for 9%

profile of v5, /device:TPU:6, one launch (start us, length us, event | category | flops | bytes accessed | tf_op | source)
XLA Modules:
  0.0 192.0 jit_solution(17779646733146866747)
XLA Ops:
  0.6 21.2 %all_to_all.25.idx_ref = s32[32,1,128]{2,1,0:T(1,128)S(1)} all-to-all(s32[32,1,128]{2,1,0:T(1,128)} %bitcast.31), channel_id=1, replica_groups=mesh['dp'=8,'cut'=32] {'cut'}, dimensions={0} | all-to-all | bytes 32768 | tf_op jit(solution)/shard_map/all_to_all | solution.py:515
  21.8 3.2 %gather.1 = bf16[32,128,128]{2,1,0:T(8,128)(2,1)} custom-call(s32[32,1,128]{2,1,0:T(1,128)S(1)} %all_to_all.25.idx_ref, bf16[128,1024]{1,0:T(8,128)(2,1)} %node_ref.7), custom_call_target="tpu_custom_call" | custom-call | tf_op jit(solution)/shard_map/gather/pallas_call | solution.py:530
  25.1 31.5 %all_to_all.26.mirror_ref = bf16[32,128,128]{2,1,0:T(8,128)(2,1)S(1)} all-to-all(bf16[32,128,128]{2,1,0:T(8,128)(2,1)} %gather.1), channel_id=1, replica_groups=mesh['dp'=8,'cut'=32] {'cut'}, dimensions={0} | all-to-all | bytes 2097152 | tf_op jit(solution)/shard_map/all_to_all | solution.py:515
  56.6 5.7 %edge_fwd.1 = (f32[128,1024]{1,0:T(8,128)}, bf16[32,128,128]{2,1,0:T(8,128)(2,1)}) custom-call(s32[2,32]{1,0:T(2,128)} %bitcast.32, s32[32]{0:T(128)} %count_ref.3, s32[32,2,128]{2,1,0:T(2,128)} %offset_ref.5, bf16[128,4096]{1,0:T(8,128)(2,1)} %edge_ref.5, bf16[128,1024]{1,0:T(8,128)(2,1)} %node_ref.7, bf16[32,128,128]{2,1,0:T(8,128)(2,1)S(1)} %all_to_all.26.mirror_ref, ...), custom_call_target="tpu_custom_call" | custom-call | tf_op jit(solution)/shard_map/edge_fwd/pallas_call | solution.py:546
  62.3 32.6 %all_to_all.27.mirror_ref = bf16[32,128,128]{2,1,0:T(8,128)(2,1)S(1)} all-to-all(bf16[32,128,128]{2,1,0:T(8,128)(2,1)} %get-tuple-element.31), channel_id=1, replica_groups=mesh['dp'=8,'cut'=32] {'cut'}, dimensions={0} | all-to-all | bytes 2097152 | tf_op jit(solution)/shard_map/all_to_all | solution.py:515
  94.9 6.1 %node.1 = (bf16[128,1024]{1,0:T(8,128)(2,1)}, bf16[128,1024]{1,0:T(8,128)(2,1)}, bf16[32,128,128]{2,1,0:T(8,128)(2,1)}) custom-call(s32[32,1,128]{2,1,0:T(1,128)S(1)} %all_to_all.25.idx_ref, f32[128,1024]{1,0:T(8,128)} %get-tuple-element.30.local_ref, bf16[32,128,128]{2,1,0:T(8,128)(2,1)S(1)} %all_to_all.27.mirror_ref, bf16[128,1024]{1,0:T(8,128)(2,1)} %node_ref.7, ...), custom_call_target="tpu_custom_call" | custom-call | tf_op jit(solution)/shard_map/node/pallas_call | solution.py:624
  101.0 5.1 %all-to-all-start.3 = ((bf16[32,128,128]{2,1,0:T(8,128)(2,1)}), bf16[32,128,128]{2,1,0:T(8,128)(2,1)S(1)}, u32[]{:S(2)}, u32[]{:S(2)}) async-start(bf16[32,128,128]{2,1,0:T(8,128)(2,1)} %get-tuple-element.41), calls=%async_computation.3 | async-start | bytes 2097152 | tf_op jit(solution)/shard_map/all_to_all | solution.py:515
  106.1 5.6 %edge_keep.1 = (bf16[256,4096]{1,0:T(8,128)(2,1)}, bf16[128,4096]{1,0:T(8,128)(2,1)}, bf16[128,4096]{1,0:T(8,128)(2,1)}, bf16[128,4096]{1,0:T(8,128)(2,1)}, f32[1,4096]{1,0:T(1,128)}) custom-call(s32[2,32]{1,0:T(2,128)} %bitcast.33, s32[32,2,128]{2,1,0:T(2,128)} %offset_ref.5, bf16[128,4096]{1,0:T(8,128)(2,1)} %edge_ref.5, bf16[128,1024]{1,0:T(8,128)(2,1)} %node_ref.7, ...), custom_call_target="tpu_custom_call" | custom-call | flops 805306368 | bytes 8388608 | tf_op jit(solution)/shard_map/edge_keep/pallas_call | solution.py:583
  111.7 3.2 %node_rest.1 = (bf16[128,1024]{1,0:T(8,128)(2,1)}, f32[128,1024]{1,0:T(8,128)}, f32[392,128]{1,0:T(8,128)}) custom-call(bf16[128,1024]{1,0:T(8,128)(2,1)} %get-tuple-element.32.agg_low_ref, bf16[128,1024]{1,0:T(8,128)(2,1)} %node_ref.7, bf16[128,1024]{1,0:T(8,128)(2,1)} %cot_ref.3, bf16[128,256]{1,0:T(8,128)(2,1)} %w1_ref.8, f32[1,128]{1,0:T(1,128)} %bitcast.41, ...), custom_call_target="tpu_custom_call" | custom-call | flops 369098752 | bytes 2621440 | tf_op jit(solution)/shard_map/node_rest/pallas_call | solution.py:646
  114.9 18.7 %all-to-all-done.3.mirror_ref = bf16[32,128,128]{2,1,0:T(8,128)(2,1)S(1)} async-done(((bf16[32,128,128]{2,1,0:T(8,128)(2,1)}), bf16[32,128,128]{2,1,0:T(8,128)(2,1)S(1)}, u32[]{:S(2)}, u32[]{:S(2)}) %all-to-all-start.3) | async-done | bytes 1048608 | tf_op jit(solution)/shard_map/all_to_all | solution.py:515
  133.6 7.6 %edge_bwd.1 = (bf16[128,4096]{1,0:T(8,128)(2,1)}, bf16[128,4096]{1,0:T(8,128)(2,1)}, f32[128,1024]{1,0:T(8,128)}, bf16[32,128,128]{2,1,0:T(8,128)(2,1)}, f32[3,128,128]{2,1,0:T(8,128)}) custom-call(s32[2,32]{1,0:T(2,128)} %bitcast.34, s32[32]{0:T(128)} %count_ref.3, s32[32,2,128]{2,1,0:T(2,128)} %offset_ref.5, ...), custom_call_target="tpu_custom_call" | custom-call | tf_op jit(solution)/shard_map/edge_bwd/pallas_call | solution.py:674
  141.2 5.0 %all-to-all-start.4 = ((bf16[32,128,128]{2,1,0:T(8,128)(2,1)}), bf16[32,128,128]{2,1,0:T(8,128)(2,1)S(1)}, u32[]{:S(2)}, u32[]{:S(2)}) async-start(bf16[32,128,128]{2,1,0:T(8,128)(2,1)} %get-tuple-element.49), calls=%async_computation.4 | async-start | bytes 2097152 | tf_op jit(solution)/shard_map/all_to_all | solution.py:515
  146.3 5.3 %edge_weights.1 = (bf16[128,4096]{1,0:T(8,128)(2,1)}, bf16[928,128]{1,0:T(8,128)(2,1)}) custom-call(bf16[128,4096]{1,0:T(8,128)(2,1)} %edge_ref.5, bf16[256,4096]{1,0:T(8,128)(2,1)} %get-tuple-element.35.pair_ref, bf16[128,4096]{1,0:T(8,128)(2,1)} %get-tuple-element.36.hidden_ref, bf16[128,4096]{1,0:T(8,128)(2,1)} %get-tuple-element.43.post_ref, ...), custom_call_target="tpu_custom_call" | custom-call | flops 671088640 | bytes 7340032 | tf_op jit(solution)/shard_map/edge_weights/pallas_call | solution.py:730
  151.6 0.9 dynamic-slice_bitcast_fusion.2
  152.5 3.1 %collective-permute-start.2 = (bf16[232,128]{1,0:T(8,128)(2,1)S(1)}, bf16[232,128]{1,0:T(8,128)(2,1)S(1)}, u32[]{:S(2)}, u32[]{:S(2)}) collective-permute-start(bf16[232,128]{1,0:T(8,128)(2,1)S(1)} %get-tuple-element.57), channel_id=1, source_target_pairs={{0,24},{1,25},{2,26},{3,27},{4,28},{5,29},{6,30},{7,31},{8,0},{9,1... | collective-permute-start | bytes 178184 | tf_op jit(solution)/shard_map/ppermute | solution.py:443
  155.6 0.8 collective-permute-start.1
  156.4 0.9 collective-permute-start
  157.3 0.2 collective-permute-done.2
  157.5 4.6 %collective-permute-done.1 = bf16[232,128]{1,0:T(8,128)(2,1)S(1)} collective-permute-done((bf16[232,128]{1,0:T(8,128)(2,1)S(1)}, bf16[232,128]{1,0:T(8,128)(2,1)S(1)}, u32[]{:S(2)}, u32[]{:S(2)}) %collective-permute-start.1) | collective-permute-done | bytes 59424 | tf_op jit(solution)/shard_map/ppermute | solution.py:443
  162.1 1.6 collective-permute-done
  163.6 0.9 fusion.1
  164.5 3.5 %collective-permute-start.5 = (bf16[232,128]{1,0:T(8,128)(2,1)S(1)}, bf16[232,128]{1,0:T(8,128)(2,1)S(1)}, u32[]{:S(2)}, u32[]{:S(2)}) collective-permute-start(bf16[232,128]{1,0:T(8,128)(2,1)S(1)} %fusion.1), channel_id=1, source_target_pairs={{0,6},{1,7},{2,4},{3,5},{4,2},{5,3},{6,0},{7,1},{8,14},{9,15},{10,... | collective-permute-start | bytes 178184 | tf_op jit(solution)/shard_map/ppermute | solution.py:446
  168.0 2.1 %collective-permute-start.4 = (bf16[232,128]{1,0:T(8,128)(2,1)S(1)}, bf16[232,128]{1,0:T(8,128)(2,1)S(1)}, u32[]{:S(2)}, u32[]{:S(2)}) collective-permute-start(bf16[232,128]{1,0:T(8,128)(2,1)S(1)} %fusion.1), channel_id=1, source_target_pairs={{0,2},{1,3},{2,0},{3,1},{4,6},{5,7},{6,4},{7,5},{8,10},{9,11},{10,... | collective-permute-start | bytes 178184 | tf_op jit(solution)/shard_map/ppermute | solution.py:446
  170.0 1.0 collective-permute-start.3
  171.1 4.4 %collective-permute-done.5 = bf16[232,128]{1,0:T(8,128)(2,1)S(1)} collective-permute-done((bf16[232,128]{1,0:T(8,128)(2,1)S(1)}, bf16[232,128]{1,0:T(8,128)(2,1)S(1)}, u32[]{:S(2)}, u32[]{:S(2)}) %collective-permute-start.5) | collective-permute-done | bytes 59424 | tf_op jit(solution)/shard_map/ppermute | solution.py:446
  175.5 0.0 collective-permute-done.4
  175.5 3.6 %collective-permute-done.3 = bf16[232,128]{1,0:T(8,128)(2,1)S(1)} collective-permute-done((bf16[232,128]{1,0:T(8,128)(2,1)S(1)}, bf16[232,128]{1,0:T(8,128)(2,1)S(1)}, u32[]{:S(2)}, u32[]{:S(2)}) %collective-permute-start.3) | collective-permute-done | bytes 59424 | tf_op jit(solution)/shard_map/ppermute | solution.py:446
  179.2 1.5 collective-permute-start.6
  180.7 2.8 %collective-permute-done.6 = bf16[232,128]{1,0:T(8,128)(2,1)S(1)} collective-permute-done((bf16[232,128]{1,0:T(8,128)(2,1)S(1)}, bf16[232,128]{1,0:T(8,128)(2,1)S(1)}, u32[]{:S(2)}, u32[]{:S(2)}) %collective-permute-start.6) | collective-permute-done | bytes 59424 | tf_op jit(solution)/shard_map/ppermute | solution.py:446
  183.5 0.1 collective-permute-start.7
  183.6 2.7 %collective-permute-start.8 = (bf16[232,128]{1,0:T(8,128)(2,1)S(1)}, bf16[232,128]{1,0:T(8,128)(2,1)S(1)}, u32[]{:S(2)}, u32[]{:S(2)}) collective-permute-start(bf16[232,128]{1,0:T(8,128)(2,1)S(1)} %add_convert_fusion), channel_id=1, source_target_pairs={{0,16},{1,17},{2,18},{3,19},{4,20},{5,21},{6,22},{7,23},{8,24},{9,... | collective-permute-start | bytes 178184 | tf_op jit(solution)/shard_map/ppermute | solution.py:443
  186.3 1.5 collective-permute-start.9
  187.8 0.0 all-to-all-done.4.mirror_ref
  187.8 3.3 %final.1 = f32[128,1024]{1,0:T(8,128)} custom-call(s32[32,1,128]{2,1,0:T(1,128)S(1)} %all_to_all.25.idx_ref, f32[128,1024]{1,0:T(8,128)} %get-tuple-element.48.local_ref, bf16[32,128,128]{2,1,0:T(8,128)(2,1)S(1)} %all-to-all-done.4.mirror_ref), custom_call_target="tpu_custom_call" | custom-call | tf_op jit(solution)/shard_map/final/pallas_call | solution.py:766
  191.1 0.0 collective-permute-done.7
  191.1 0.0 collective-permute-done.8
  191.1 0.0 collective-permute-done.9
  191.2 0.8 params.1
  (3 shorter events, 0.1 us)
Async XLA Ops:
  101.0 32.6 %all-to-all-start.3 = ((bf16[32,128,128]{2,1,0:T(8,128)(2,1)}), bf16[32,128,128]{2,1,0:T(8,128)(2,1)S(1)}, u32[]{:S(2)}, u32[]{:S(2)}) async-start(bf16[32,128,128]{2,1,0:T(8,128)(2,1)} %get-tuple-element.41), calls=%async_computation.3 | async-start | bytes 2097152 | tf_op jit(solution)/shard_map/all_to_all | solution.py:515
  141.2 46.6 %all-to-all-start.4 = ((bf16[32,128,128]{2,1,0:T(8,128)(2,1)}), bf16[32,128,128]{2,1,0:T(8,128)(2,1)S(1)}, u32[]{:S(2)}, u32[]{:S(2)}) async-start(bf16[32,128,128]{2,1,0:T(8,128)(2,1)} %get-tuple-element.49), calls=%async_computation.4 | async-start | bytes 2097152 | tf_op jit(solution)/shard_map/all_to_all | solution.py:515
  152.5 5.0 %collective-permute-start.2 = (bf16[232,128]{1,0:T(8,128)(2,1)S(1)}, bf16[232,128]{1,0:T(8,128)(2,1)S(1)}, u32[]{:S(2)}, u32[]{:S(2)}) collective-permute-start(bf16[232,128]{1,0:T(8,128)(2,1)S(1)} %get-tuple-element.57), channel_id=1, source_target_pairs={{0,24},{1,25},{2,26},{3,27},{4,28},{5,29},{6,30},{7,31},{8,0},{9,1... | collective-permute-start | bytes 178184 | tf_op jit(solution)/shard_map/ppermute | solution.py:443
  155.6 6.5 %collective-permute-start.1 = (bf16[232,128]{1,0:T(8,128)(2,1)S(1)}, bf16[232,128]{1,0:T(8,128)(2,1)S(1)}, u32[]{:S(2)}, u32[]{:S(2)}) collective-permute-start(bf16[232,128]{1,0:T(8,128)(2,1)S(1)} %get-tuple-element.58), channel_id=1, source_target_pairs={{0,16},{1,17},{2,18},{3,19},{4,20},{5,21},{6,22},{7,23},{8,24},{9,... | collective-permute-start | bytes 178184 | tf_op jit(solution)/shard_map/ppermute | solution.py:443
  156.4 7.2 %collective-permute-start = (bf16[232,128]{1,0:T(8,128)(2,1)S(1)}, bf16[232,128]{1,0:T(8,128)(2,1)S(1)}, u32[]{:S(2)}, u32[]{:S(2)}) collective-permute-start(bf16[232,128]{1,0:T(8,128)(2,1)S(1)} %get-tuple-element.56), channel_id=1, source_target_pairs={{0,8},{1,9},{2,10},{3,11},{4,12},{5,13},{6,14},{7,15},{8,16},{9,17... | collective-permute-start | bytes 178184 | tf_op jit(solution)/shard_map/ppermute | solution.py:443
  164.5 11.0 %collective-permute-start.5 = (bf16[232,128]{1,0:T(8,128)(2,1)S(1)}, bf16[232,128]{1,0:T(8,128)(2,1)S(1)}, u32[]{:S(2)}, u32[]{:S(2)}) collective-permute-start(bf16[232,128]{1,0:T(8,128)(2,1)S(1)} %fusion.1), channel_id=1, source_target_pairs={{0,6},{1,7},{2,4},{3,5},{4,2},{5,3},{6,0},{7,1},{8,14},{9,15},{10,... | collective-permute-start | bytes 178184 | tf_op jit(solution)/shard_map/ppermute | solution.py:446
  168.0 7.5 %collective-permute-start.4 = (bf16[232,128]{1,0:T(8,128)(2,1)S(1)}, bf16[232,128]{1,0:T(8,128)(2,1)S(1)}, u32[]{:S(2)}, u32[]{:S(2)}) collective-permute-start(bf16[232,128]{1,0:T(8,128)(2,1)S(1)} %fusion.1), channel_id=1, source_target_pairs={{0,2},{1,3},{2,0},{3,1},{4,6},{5,7},{6,4},{7,5},{8,10},{9,11},{10,... | collective-permute-start | bytes 178184 | tf_op jit(solution)/shard_map/ppermute | solution.py:446
  170.0 9.1 %collective-permute-start.3 = (bf16[232,128]{1,0:T(8,128)(2,1)S(1)}, bf16[232,128]{1,0:T(8,128)(2,1)S(1)}, u32[]{:S(2)}, u32[]{:S(2)}) collective-permute-start(bf16[232,128]{1,0:T(8,128)(2,1)S(1)} %fusion.1), channel_id=1, source_target_pairs={{0,4},{1,5},{2,6},{3,7},{4,0},{5,1},{6,2},{7,3},{8,12},{9,13},{10,... | collective-permute-start | bytes 178184 | tf_op jit(solution)/shard_map/ppermute | solution.py:446
  179.2 4.3 %collective-permute-start.6 = (bf16[232,128]{1,0:T(8,128)(2,1)S(1)}, bf16[232,128]{1,0:T(8,128)(2,1)S(1)}, u32[]{:S(2)}, u32[]{:S(2)}) collective-permute-start(bf16[232,128]{1,0:T(8,128)(2,1)S(1)} %add_convert_fusion.1), channel_id=1, source_target_pairs={{0,1},{1,0},{2,3},{3,2},{4,5},{5,4},{6,7},{7,6},{8,9},{9,8},{10,11... | collective-permute-start | bytes 178184 | tf_op jit(solution)/shard_map/ppermute | solution.py:446
  183.5 7.6 %collective-permute-start.7 = (bf16[232,128]{1,0:T(8,128)(2,1)S(1)}, bf16[232,128]{1,0:T(8,128)(2,1)S(1)}, u32[]{:S(2)}, u32[]{:S(2)}) collective-permute-start(bf16[232,128]{1,0:T(8,128)(2,1)S(1)} %add_convert_fusion), channel_id=1, source_target_pairs={{0,8},{1,9},{2,10},{3,11},{4,12},{5,13},{6,14},{7,15},{8,16},{9,17... | collective-permute-start | bytes 178184 | tf_op jit(solution)/shard_map/ppermute | solution.py:443
  183.6 7.6 %collective-permute-start.8 = (bf16[232,128]{1,0:T(8,128)(2,1)S(1)}, bf16[232,128]{1,0:T(8,128)(2,1)S(1)}, u32[]{:S(2)}, u32[]{:S(2)}) collective-permute-start(bf16[232,128]{1,0:T(8,128)(2,1)S(1)} %add_convert_fusion), channel_id=1, source_target_pairs={{0,16},{1,17},{2,18},{3,19},{4,20},{5,21},{6,22},{7,23},{8,24},{9,... | collective-permute-start | bytes 178184 | tf_op jit(solution)/shard_map/ppermute | solution.py:443
  186.3 4.8 %collective-permute-start.9 = (bf16[232,128]{1,0:T(8,128)(2,1)S(1)}, bf16[232,128]{1,0:T(8,128)(2,1)S(1)}, u32[]{:S(2)}, u32[]{:S(2)}) collective-permute-start(bf16[232,128]{1,0:T(8,128)(2,1)S(1)} %add_convert_fusion), channel_id=1, source_target_pairs={{0,24},{1,25},{2,26},{3,27},{4,28},{5,29},{6,30},{7,31},{8,0},{9,1... | collective-permute-start | bytes 178184 | tf_op jit(solution)/shard_map/ppermute | solution.py:443

commit v6 on v5

--- a/solution.py
+++ b/solution.py
@@ -12,7 +12,7 @@
 BF16 = jnp.bfloat16
 TILE = 128
 GROUP = 16
-WIDE = 4
+WIDE = 8
 QUARTER = 232
 INTERPRET = False
 

time: 193 us -> 193 us (level)
  no operation moved by 1% of the time
where the time goes in v6:
time: 193 us; the launch traced here: 192 us
  blocking collectives  85.3 us (44%)
  Pallas kernels  40.9 us (21%)
  waiting for transfers between devices  35.9 us (19%)
  starting transfers between devices  27.3 us (14%)
    all_to_all x3, blocking collectives, swap(): lax.all_to_all(values, 'cut', split_axis=0, concat_axis=0, tiled=True)  85.3 us
    all_to_all x2, waiting for transfers between devices, swap(): lax.all_to_all(values, 'cut', split_axis=0, concat_axis=0, tiled=True)  18.7 us
    ppermute x4, waiting for transfers between devices, across(): return lax.ppermute(values, 'cut', [(i, i ^ bits) for i in every])  10.9 us
    all_to_all x2, starting transfers between devices, swap(): lax.all_to_all(values, 'cut', split_axis=0, concat_axis=0, tiled=True)  10.1 us
    ppermute x6, starting transfers between devices, ahead(): lax.ppermute(values, 'cut', [(i, (i + k * fast) % (4 * fast)) for i in ev...  9.05 us
    ppermute x4, starting transfers between devices, across(): return lax.ppermute(values, 'cut', [(i, i ^ bits) for i in every])  8.09 us
    pallas_call x1, Pallas kernels, per_device(): pl.pallas_call(edge_bwd_kernel, grid=(steps,), out_shape=(sent((latent, s...  7.63 us
    ppermute x6, waiting for transfers between devices, ahead(): lax.ppermute(values, 'cut', [(i, (i + k * fast) % (4 * fast)) for i in ev...  6.35 us
  transfers between devices with their start and end apart: 12, of which 7 were waited for; matrix products, arithmetic and copies ran while one was open for 1% of the time, Pallas kernels for 9%

profile of v6, /device:TPU:6, one launch (start us, length us, event | category | flops | bytes accessed | tf_op | source)
XLA Modules:
  0.0 192.0 jit_solution(15452080032404637597)
XLA Ops:
  0.6 21.2 %all_to_all.25.idx_ref = s32[32,1,128]{2,1,0:T(1,128)S(1)} all-to-all(s32[32,1,128]{2,1,0:T(1,128)} %bitcast.31), channel_id=1, replica_groups=mesh['dp'=8,'cut'=32] {'cut'}, dimensions={0} | all-to-all | bytes 32768 | tf_op jit(solution)/shard_map/all_to_all | solution.py:515
  21.8 3.2 %gather.1 = bf16[32,128,128]{2,1,0:T(8,128)(2,1)} custom-call(s32[32,1,128]{2,1,0:T(1,128)S(1)} %all_to_all.25.idx_ref, bf16[128,1024]{1,0:T(8,128)(2,1)} %node_ref.7), custom_call_target="tpu_custom_call" | custom-call | tf_op jit(solution)/shard_map/gather/pallas_call | solution.py:530
  25.1 31.5 %all_to_all.26.mirror_ref = bf16[32,128,128]{2,1,0:T(8,128)(2,1)S(1)} all-to-all(bf16[32,128,128]{2,1,0:T(8,128)(2,1)} %gather.1), channel_id=1, replica_groups=mesh['dp'=8,'cut'=32] {'cut'}, dimensions={0} | all-to-all | bytes 2097152 | tf_op jit(solution)/shard_map/all_to_all | solution.py:515
  56.6 5.7 %edge_fwd.1 = (f32[128,1024]{1,0:T(8,128)}, bf16[32,128,128]{2,1,0:T(8,128)(2,1)}) custom-call(s32[2,32]{1,0:T(2,128)} %bitcast.32, s32[32]{0:T(128)} %count_ref.3, s32[32,2,128]{2,1,0:T(2,128)} %offset_ref.5, bf16[128,4096]{1,0:T(8,128)(2,1)} %edge_ref.5, bf16[128,1024]{1,0:T(8,128)(2,1)} %node_ref.7, bf16[32,128,128]{2,1,0:T(8,128)(2,1)S(1)} %all_to_all.26.mirror_ref, ...), custom_call_target="tpu_custom_call" | custom-call | tf_op jit(solution)/shard_map/edge_fwd/pallas_call | solution.py:546
  62.3 32.6 %all_to_all.27.mirror_ref = bf16[32,128,128]{2,1,0:T(8,128)(2,1)S(1)} all-to-all(bf16[32,128,128]{2,1,0:T(8,128)(2,1)} %get-tuple-element.31), channel_id=1, replica_groups=mesh['dp'=8,'cut'=32] {'cut'}, dimensions={0} | all-to-all | bytes 2097152 | tf_op jit(solution)/shard_map/all_to_all | solution.py:515
  94.9 6.1 %node.1 = (bf16[128,1024]{1,0:T(8,128)(2,1)}, bf16[128,1024]{1,0:T(8,128)(2,1)}, bf16[32,128,128]{2,1,0:T(8,128)(2,1)}) custom-call(s32[32,1,128]{2,1,0:T(1,128)S(1)} %all_to_all.25.idx_ref, f32[128,1024]{1,0:T(8,128)} %get-tuple-element.30.local_ref, bf16[32,128,128]{2,1,0:T(8,128)(2,1)S(1)} %all_to_all.27.mirror_ref, bf16[128,1024]{1,0:T(8,128)(2,1)} %node_ref.7, ...), custom_call_target="tpu_custom_call" | custom-call | tf_op jit(solution)/shard_map/node/pallas_call | solution.py:624
  101.0 5.2 %all-to-all-start.3 = ((bf16[32,128,128]{2,1,0:T(8,128)(2,1)}), bf16[32,128,128]{2,1,0:T(8,128)(2,1)S(1)}, u32[]{:S(2)}, u32[]{:S(2)}) async-start(bf16[32,128,128]{2,1,0:T(8,128)(2,1)} %get-tuple-element.41), calls=%async_computation.3 | async-start | bytes 2097152 | tf_op jit(solution)/shard_map/all_to_all | solution.py:515
  106.1 5.6 %edge_keep.1 = (bf16[256,4096]{1,0:T(8,128)(2,1)}, bf16[128,4096]{1,0:T(8,128)(2,1)}, bf16[128,4096]{1,0:T(8,128)(2,1)}, bf16[128,4096]{1,0:T(8,128)(2,1)}, f32[1,4096]{1,0:T(1,128)}) custom-call(s32[2,32]{1,0:T(2,128)} %bitcast.33, s32[32,2,128]{2,1,0:T(2,128)} %offset_ref.5, bf16[128,4096]{1,0:T(8,128)(2,1)} %edge_ref.5, bf16[128,1024]{1,0:T(8,128)(2,1)} %node_ref.7, ...), custom_call_target="tpu_custom_call" | custom-call | flops 805306368 | bytes 8388608 | tf_op jit(solution)/shard_map/edge_keep/pallas_call | solution.py:583
  111.7 3.2 %node_rest.1 = (bf16[128,1024]{1,0:T(8,128)(2,1)}, f32[128,1024]{1,0:T(8,128)}, f32[392,128]{1,0:T(8,128)}) custom-call(bf16[128,1024]{1,0:T(8,128)(2,1)} %get-tuple-element.32.agg_low_ref, bf16[128,1024]{1,0:T(8,128)(2,1)} %node_ref.7, bf16[128,1024]{1,0:T(8,128)(2,1)} %cot_ref.3, bf16[128,256]{1,0:T(8,128)(2,1)} %w1_ref.8, f32[1,128]{1,0:T(1,128)} %bitcast.41, ...), custom_call_target="tpu_custom_call" | custom-call | flops 369098752 | bytes 2621440 | tf_op jit(solution)/shard_map/node_rest/pallas_call | solution.py:646
  114.9 18.7 %all-to-all-done.3.mirror_ref = bf16[32,128,128]{2,1,0:T(8,128)(2,1)S(1)} async-done(((bf16[32,128,128]{2,1,0:T(8,128)(2,1)}), bf16[32,128,128]{2,1,0:T(8,128)(2,1)S(1)}, u32[]{:S(2)}, u32[]{:S(2)}) %all-to-all-start.3) | async-done | bytes 1048608 | tf_op jit(solution)/shard_map/all_to_all | solution.py:515
  133.6 7.6 %edge_bwd.1 = (bf16[128,4096]{1,0:T(8,128)(2,1)}, bf16[128,4096]{1,0:T(8,128)(2,1)}, f32[128,1024]{1,0:T(8,128)}, bf16[32,128,128]{2,1,0:T(8,128)(2,1)}, f32[3,128,128]{2,1,0:T(8,128)}) custom-call(s32[2,32]{1,0:T(2,128)} %bitcast.34, s32[32]{0:T(128)} %count_ref.3, s32[32,2,128]{2,1,0:T(2,128)} %offset_ref.5, ...), custom_call_target="tpu_custom_call" | custom-call | tf_op jit(solution)/shard_map/edge_bwd/pallas_call | solution.py:674
  141.2 5.0 %all-to-all-start.4 = ((bf16[32,128,128]{2,1,0:T(8,128)(2,1)}), bf16[32,128,128]{2,1,0:T(8,128)(2,1)S(1)}, u32[]{:S(2)}, u32[]{:S(2)}) async-start(bf16[32,128,128]{2,1,0:T(8,128)(2,1)} %get-tuple-element.49), calls=%async_computation.4 | async-start | bytes 2097152 | tf_op jit(solution)/shard_map/all_to_all | solution.py:515
  146.3 5.3 %edge_weights.1 = (bf16[128,4096]{1,0:T(8,128)(2,1)}, bf16[928,128]{1,0:T(8,128)(2,1)}) custom-call(bf16[128,4096]{1,0:T(8,128)(2,1)} %edge_ref.5, bf16[256,4096]{1,0:T(8,128)(2,1)} %get-tuple-element.35.pair_ref, bf16[128,4096]{1,0:T(8,128)(2,1)} %get-tuple-element.36.hidden_ref, bf16[128,4096]{1,0:T(8,128)(2,1)} %get-tuple-element.43.post_ref, ...), custom_call_target="tpu_custom_call" | custom-call | flops 671088640 | bytes 7340032 | tf_op jit(solution)/shard_map/edge_weights/pallas_call | solution.py:730
  151.6 0.9 dynamic-slice_bitcast_fusion.2
  152.5 3.1 %collective-permute-start.2 = (bf16[232,128]{1,0:T(8,128)(2,1)S(1)}, bf16[232,128]{1,0:T(8,128)(2,1)S(1)}, u32[]{:S(2)}, u32[]{:S(2)}) collective-permute-start(bf16[232,128]{1,0:T(8,128)(2,1)S(1)} %get-tuple-element.57), channel_id=1, source_target_pairs={{0,24},{1,25},{2,26},{3,27},{4,28},{5,29},{6,30},{7,31},{8,0},{9,1... | collective-permute-start | bytes 178184 | tf_op jit(solution)/shard_map/ppermute | solution.py:443
  155.6 0.8 collective-permute-start.1
  156.4 0.9 collective-permute-start
  157.3 0.2 collective-permute-done.2
  157.5 4.6 %collective-permute-done.1 = bf16[232,128]{1,0:T(8,128)(2,1)S(1)} collective-permute-done((bf16[232,128]{1,0:T(8,128)(2,1)S(1)}, bf16[232,128]{1,0:T(8,128)(2,1)S(1)}, u32[]{:S(2)}, u32[]{:S(2)}) %collective-permute-start.1) | collective-permute-done | bytes 59424 | tf_op jit(solution)/shard_map/ppermute | solution.py:443
  162.1 1.6 collective-permute-done
  163.6 0.9 fusion.1
  164.5 3.5 %collective-permute-start.5 = (bf16[232,128]{1,0:T(8,128)(2,1)S(1)}, bf16[232,128]{1,0:T(8,128)(2,1)S(1)}, u32[]{:S(2)}, u32[]{:S(2)}) collective-permute-start(bf16[232,128]{1,0:T(8,128)(2,1)S(1)} %fusion.1), channel_id=1, source_target_pairs={{0,6},{1,7},{2,4},{3,5},{4,2},{5,3},{6,0},{7,1},{8,14},{9,15},{10,... | collective-permute-start | bytes 178184 | tf_op jit(solution)/shard_map/ppermute | solution.py:446
  168.0 2.0 %collective-permute-start.4 = (bf16[232,128]{1,0:T(8,128)(2,1)S(1)}, bf16[232,128]{1,0:T(8,128)(2,1)S(1)}, u32[]{:S(2)}, u32[]{:S(2)}) collective-permute-start(bf16[232,128]{1,0:T(8,128)(2,1)S(1)} %fusion.1), channel_id=1, source_target_pairs={{0,2},{1,3},{2,0},{3,1},{4,6},{5,7},{6,4},{7,5},{8,10},{9,11},{10,... | collective-permute-start | bytes 178184 | tf_op jit(solution)/shard_map/ppermute | solution.py:446
  170.1 1.0 collective-permute-start.3
  171.1 4.4 %collective-permute-done.5 = bf16[232,128]{1,0:T(8,128)(2,1)S(1)} collective-permute-done((bf16[232,128]{1,0:T(8,128)(2,1)S(1)}, bf16[232,128]{1,0:T(8,128)(2,1)S(1)}, u32[]{:S(2)}, u32[]{:S(2)}) %collective-permute-start.5) | collective-permute-done | bytes 59424 | tf_op jit(solution)/shard_map/ppermute | solution.py:446
  175.5 0.0 collective-permute-done.4
  175.5 3.6 %collective-permute-done.3 = bf16[232,128]{1,0:T(8,128)(2,1)S(1)} collective-permute-done((bf16[232,128]{1,0:T(8,128)(2,1)S(1)}, bf16[232,128]{1,0:T(8,128)(2,1)S(1)}, u32[]{:S(2)}, u32[]{:S(2)}) %collective-permute-start.3) | collective-permute-done | bytes 59424 | tf_op jit(solution)/shard_map/ppermute | solution.py:446
  179.2 1.5 collective-permute-start.6
  180.7 2.8 %collective-permute-done.6 = bf16[232,128]{1,0:T(8,128)(2,1)S(1)} collective-permute-done((bf16[232,128]{1,0:T(8,128)(2,1)S(1)}, bf16[232,128]{1,0:T(8,128)(2,1)S(1)}, u32[]{:S(2)}, u32[]{:S(2)}) %collective-permute-start.6) | collective-permute-done | bytes 59424 | tf_op jit(solution)/shard_map/ppermute | solution.py:446
  183.5 0.1 collective-permute-start.7
  183.6 2.7 %collective-permute-start.8 = (bf16[232,128]{1,0:T(8,128)(2,1)S(1)}, bf16[232,128]{1,0:T(8,128)(2,1)S(1)}, u32[]{:S(2)}, u32[]{:S(2)}) collective-permute-start(bf16[232,128]{1,0:T(8,128)(2,1)S(1)} %add_convert_fusion), channel_id=1, source_target_pairs={{0,16},{1,17},{2,18},{3,19},{4,20},{5,21},{6,22},{7,23},{8,24},{9,... | collective-permute-start | bytes 178184 | tf_op jit(solution)/shard_map/ppermute | solution.py:443
  186.3 1.5 collective-permute-start.9
  187.8 0.0 all-to-all-done.4.mirror_ref
  187.8 3.3 %final.1 = f32[128,1024]{1,0:T(8,128)} custom-call(s32[32,1,128]{2,1,0:T(1,128)S(1)} %all_to_all.25.idx_ref, f32[128,1024]{1,0:T(8,128)} %get-tuple-element.48.local_ref, bf16[32,128,128]{2,1,0:T(8,128)(2,1)S(1)} %all-to-all-done.4.mirror_ref), custom_call_target="tpu_custom_call" | custom-call | tf_op jit(solution)/shard_map/final/pallas_call | solution.py:766
  191.1 0.0 collective-permute-done.7
  191.1 0.0 collective-permute-done.8
  191.1 0.0 collective-permute-done.9
  191.1 0.8 params.1
  (3 shorter events, 0.1 us)
Async XLA Ops:
  101.0 32.6 %all-to-all-start.3 = ((bf16[32,128,128]{2,1,0:T(8,128)(2,1)}), bf16[32,128,128]{2,1,0:T(8,128)(2,1)S(1)}, u32[]{:S(2)}, u32[]{:S(2)}) async-start(bf16[32,128,128]{2,1,0:T(8,128)(2,1)} %get-tuple-element.41), calls=%async_computation.3 | async-start | bytes 2097152 | tf_op jit(solution)/shard_map/all_to_all | solution.py:515
  141.2 46.5 %all-to-all-start.4 = ((bf16[32,128,128]{2,1,0:T(8,128)(2,1)}), bf16[32,128,128]{2,1,0:T(8,128)(2,1)S(1)}, u32[]{:S(2)}, u32[]{:S(2)}) async-start(bf16[32,128,128]{2,1,0:T(8,128)(2,1)} %get-tuple-element.49), calls=%async_computation.4 | async-start | bytes 2097152 | tf_op jit(solution)/shard_map/all_to_all | solution.py:515
  152.5 5.0 %collective-permute-start.2 = (bf16[232,128]{1,0:T(8,128)(2,1)S(1)}, bf16[232,128]{1,0:T(8,128)(2,1)S(1)}, u32[]{:S(2)}, u32[]{:S(2)}) collective-permute-start(bf16[232,128]{1,0:T(8,128)(2,1)S(1)} %get-tuple-element.57), channel_id=1, source_target_pairs={{0,24},{1,25},{2,26},{3,27},{4,28},{5,29},{6,30},{7,31},{8,0},{9,1... | collective-permute-start | bytes 178184 | tf_op jit(solution)/shard_map/ppermute | solution.py:443
  155.6 6.5 %collective-permute-start.1 = (bf16[232,128]{1,0:T(8,128)(2,1)S(1)}, bf16[232,128]{1,0:T(8,128)(2,1)S(1)}, u32[]{:S(2)}, u32[]{:S(2)}) collective-permute-start(bf16[232,128]{1,0:T(8,128)(2,1)S(1)} %get-tuple-element.58), channel_id=1, source_target_pairs={{0,16},{1,17},{2,18},{3,19},{4,20},{5,21},{6,22},{7,23},{8,24},{9,... | collective-permute-start | bytes 178184 | tf_op jit(solution)/shard_map/ppermute | solution.py:443
  156.4 7.2 %collective-permute-start = (bf16[232,128]{1,0:T(8,128)(2,1)S(1)}, bf16[232,128]{1,0:T(8,128)(2,1)S(1)}, u32[]{:S(2)}, u32[]{:S(2)}) collective-permute-start(bf16[232,128]{1,0:T(8,128)(2,1)S(1)} %get-tuple-element.56), channel_id=1, source_target_pairs={{0,8},{1,9},{2,10},{3,11},{4,12},{5,13},{6,14},{7,15},{8,16},{9,17... | collective-permute-start | bytes 178184 | tf_op jit(solution)/shard_map/ppermute | solution.py:443
  164.5 11.0 %collective-permute-start.5 = (bf16[232,128]{1,0:T(8,128)(2,1)S(1)}, bf16[232,128]{1,0:T(8,128)(2,1)S(1)}, u32[]{:S(2)}, u32[]{:S(2)}) collective-permute-start(bf16[232,128]{1,0:T(8,128)(2,1)S(1)} %fusion.1), channel_id=1, source_target_pairs={{0,6},{1,7},{2,4},{3,5},{4,2},{5,3},{6,0},{7,1},{8,14},{9,15},{10,... | collective-permute-start | bytes 178184 | tf_op jit(solution)/shard_map/ppermute | solution.py:446
  168.0 7.5 %collective-permute-start.4 = (bf16[232,128]{1,0:T(8,128)(2,1)S(1)}, bf16[232,128]{1,0:T(8,128)(2,1)S(1)}, u32[]{:S(2)}, u32[]{:S(2)}) collective-permute-start(bf16[232,128]{1,0:T(8,128)(2,1)S(1)} %fusion.1), channel_id=1, source_target_pairs={{0,2},{1,3},{2,0},{3,1},{4,6},{5,7},{6,4},{7,5},{8,10},{9,11},{10,... | collective-permute-start | bytes 178184 | tf_op jit(solution)/shard_map/ppermute | solution.py:446
  170.1 9.1 %collective-permute-start.3 = (bf16[232,128]{1,0:T(8,128)(2,1)S(1)}, bf16[232,128]{1,0:T(8,128)(2,1)S(1)}, u32[]{:S(2)}, u32[]{:S(2)}) collective-permute-start(bf16[232,128]{1,0:T(8,128)(2,1)S(1)} %fusion.1), channel_id=1, source_target_pairs={{0,4},{1,5},{2,6},{3,7},{4,0},{5,1},{6,2},{7,3},{8,12},{9,13},{10,... | collective-permute-start | bytes 178184 | tf_op jit(solution)/shard_map/ppermute | solution.py:446
  179.2 4.3 %collective-permute-start.6 = (bf16[232,128]{1,0:T(8,128)(2,1)S(1)}, bf16[232,128]{1,0:T(8,128)(2,1)S(1)}, u32[]{:S(2)}, u32[]{:S(2)}) collective-permute-start(bf16[232,128]{1,0:T(8,128)(2,1)S(1)} %add_convert_fusion.1), channel_id=1, source_target_pairs={{0,1},{1,0},{2,3},{3,2},{4,5},{5,4},{6,7},{7,6},{8,9},{9,8},{10,11... | collective-permute-start | bytes 178184 | tf_op jit(solution)/shard_map/ppermute | solution.py:446
  183.5 7.6 %collective-permute-start.7 = (bf16[232,128]{1,0:T(8,128)(2,1)S(1)}, bf16[232,128]{1,0:T(8,128)(2,1)S(1)}, u32[]{:S(2)}, u32[]{:S(2)}) collective-permute-start(bf16[232,128]{1,0:T(8,128)(2,1)S(1)} %add_convert_fusion), channel_id=1, source_target_pairs={{0,8},{1,9},{2,10},{3,11},{4,12},{5,13},{6,14},{7,15},{8,16},{9,17... | collective-permute-start | bytes 178184 | tf_op jit(solution)/shard_map/ppermute | solution.py:443
  183.6 7.5 %collective-permute-start.8 = (bf16[232,128]{1,0:T(8,128)(2,1)S(1)}, bf16[232,128]{1,0:T(8,128)(2,1)S(1)}, u32[]{:S(2)}, u32[]{:S(2)}) collective-permute-start(bf16[232,128]{1,0:T(8,128)(2,1)S(1)} %add_convert_fusion), channel_id=1, source_target_pairs={{0,16},{1,17},{2,18},{3,19},{4,20},{5,21},{6,22},{7,23},{8,24},{9,... | collective-permute-start | bytes 178184 | tf_op jit(solution)/shard_map/ppermute | solution.py:443
  186.3 4.8 %collective-permute-start.9 = (bf16[232,128]{1,0:T(8,128)(2,1)S(1)}, bf16[232,128]{1,0:T(8,128)(2,1)S(1)}, u32[]{:S(2)}, u32[]{:S(2)}) collective-permute-start(bf16[232,128]{1,0:T(8,128)(2,1)S(1)} %add_convert_fusion), channel_id=1, source_target_pairs={{0,24},{1,25},{2,26},{3,27},{4,28},{5,29},{6,30},{7,31},{8,0},{9,1... | collective-permute-start | bytes 178184 | tf_op jit(solution)/shard_map/ppermute | solution.py:443
